TPU v7x, 32 devices: a whole 2x2x4 slice. The times are simulated.
32 devices in a mesh: row: 4 (over y, x), col: 4 (over z), depth: 2 (over core).
Axes of the slice: x: 2, y: 2, z: 4, core: 2. Of those that a mesh axis runs over, the one named last changes fastest.
Arguments:
- values: bfloat16 [800, 20, 128, 128], P(('row', 'depth'), 'col'), may hold values from -2 to 2
- pattern: int32 [800, 20], P(('row', 'depth'), 'col'), may hold values from 0 to 199, as said below
- branch_flag: int32 [40], replicated, may hold values from 0 to 1, as said below
Outputs:
- purified: bfloat16 [40, 20, 128, 128], P(('row', 'depth'), 'col')
Inputs may be any that keep to these rules, and one draw needn't show every extreme that they name: `pattern`: block columns fall into classes with 5 members in every column panel; block (i, j) is nonzero exactly when i and j are in the same class, and the 5 slots of a block row in panel c list, in no particular order, the distinct panel-local indices of the members of its class in that panel. `branch_flag`: exactly half of the entries, rounded down, are 1; the rest are 0.
All inputs are finite; a program needn't handle non-finite values.
Results may differ from a plain program's by a relative error of at most 0.001.
Values may be sent and summed in bfloat16 or wider, within the bound.
No kernel may reach another device: no remote copies, remote signals or barrier semaphores. Data moves between devices by JAX's collectives and lax.ppermute only.
A program may use at most 128 MiB of HBM per device.

v0:
```python
import jax
import jax.numpy as jnp
import numpy as np
from jax import lax
from jax.sharding import PartitionSpec as P

SLAB_DEV = 5


def body(values, pattern, branch_flag):
    groups = lax.axis_size(("row", "depth"))
    shard_index = lax.axis_index(("row", "depth"))
    panels = lax.axis_size("col")
    rows_here = values.shape[0]
    slot_count = values.shape[1]
    block_size = values.shape[2]
    total_rows = rows_here * groups
    panel_cols = total_rows // panels
    stride = rows_here // SLAB_DEV
    panel_count = max(1, rows_here // panel_cols)
    mine_vals = values[::stride]
    mine_cols = pattern[::stride]
    every_vals, every_cols = (
        lax.all_gather(mine_vals, "col", axis=1, tiled=True),
        lax.all_gather(mine_cols, "col", axis=1, tiled=True),
    )
    slot_table = np.zeros((groups, panel_count * slot_count), dtype=np.int32)
    for target in range(groups):
        start_panel = target * rows_here // panel_cols
        for offset in range(panel_count):
            for member in range(slot_count):
                slot_table[target, offset * slot_count + member] = (
                    start_panel + offset
                ) * slot_count + member
    panel_table = slot_table // slot_count
    send_vals = every_vals[:, slot_table]
    send_cols = (
        every_cols[:, slot_table] + jnp.asarray(panel_table * panel_cols)[None, :, :]
    ).astype(jnp.int32)
    send_own = jnp.broadcast_to(
        mine_cols[:, None, :], (mine_cols.shape[0], groups, mine_cols.shape[1])
    )
    recv_vals, recv_cols, recv_own = (
        lax.all_to_all(send_vals, ("row", "depth"), split_axis=1, concat_axis=0, tiled=True),
        lax.all_to_all(send_cols, ("row", "depth"), split_axis=1, concat_axis=0, tiled=True),
        lax.all_to_all(send_own, ("row", "depth"), split_axis=1, concat_axis=0, tiled=True),
    )
    left_vals = recv_vals.reshape(
        (recv_vals.shape[0], panel_count * slot_count, block_size, block_size)
    )
    left_cols = recv_cols.reshape((recv_cols.shape[0], panel_count * slot_count))
    out_cols = recv_own.reshape((recv_own.shape[0], recv_own.shape[2]))
    slab_total = left_vals.shape[0]
    left_slots = left_vals.shape[1]
    local_rows = left_cols - shard_index * rows_here
    inside = (local_rows >= 0) & (local_rows < rows_here)
    local_rows = jnp.clip(local_rows, 0, rows_here - 1).astype(jnp.int32)
    left_vals = jnp.where(inside[:, :, None, None], left_vals, jnp.zeros((), left_vals.dtype))
    right_cols = pattern[local_rows]
    match = right_cols[:, :, None, :] == out_cols[:, None, :, None]
    present = jnp.any(match, axis=3)
    slot_iota = lax.broadcasted_iota(jnp.int32, match.shape, 3)
    chosen = jnp.sum(jnp.where(match, slot_iota, 0), axis=3)
    group_rows = slab_total // groups

    def group_product(items):
        block_vals, row_index, slot_index, live = items
        picked = values[row_index[:, :, None], slot_index]
        picked = jnp.where(live[:, :, :, None, None], picked, jnp.zeros((), picked.dtype))
        return jnp.einsum(
            "ilab,ilmbc->imac", block_vals, picked, preferred_element_type=jnp.float32
        )

    partial_terms = lax.map(
        group_product,
        (
            left_vals.reshape(groups, group_rows, left_slots, block_size, block_size),
            local_rows.reshape(groups, group_rows, left_slots),
            chosen.reshape(groups, group_rows, left_slots, slot_count),
            present.reshape(groups, group_rows, left_slots, slot_count),
        ),
    )
    partial_terms = partial_terms.reshape(slab_total, slot_count, block_size, block_size)
    summed = lax.psum_scatter(partial_terms, ("row", "depth"), scatter_dimension=0, tiled=True)
    own_count = mine_vals.shape[0]
    own_flags = lax.dynamic_slice_in_dim(branch_flag, shard_index * own_count, own_count)
    own = mine_vals.astype(jnp.float32)
    result = jnp.where(own_flags[:, None, None, None] == 1, summed, 2.0 * own - summed)
    return result.astype(jnp.bfloat16)


def solution(mesh):
    in_specs = (P(("row", "depth"), "col", None, None), P(("row", "depth"), "col"), P())
    out_specs = P(("row", "depth"), "col", None, None)
    return jax.shard_map(body, mesh=mesh, in_specs=in_specs, out_specs=out_specs, check_vma=False)
```

profile of v0, /device:TPU:0, one launch (start us, length us, event | category | flops | bytes accessed | tf_op | source)
XLA Modules:
  0.0 472.9 jit_solution(6570311070689663833)
XLA Ops:
  6.5 2.1 slice.7
  8.7 0.8 slice.6
  9.4 15.0 %all-gather = s32[4,5,5]{2,1,0:T(8,128)S(1)} all-gather(s32[1,5,5]{2,1,0:T(8,128)S(1)} %bitcast.87), channel_id=1, replica_groups=mesh['row'=4,'col'=4,'depth'=2] {'col'}, dimensions={0}, use_global_device_ids=true | all-gather | bytes 500 | tf_op jit(solution)/shard_map/all_gather | solution.py:25
  24.5 0.7 pad_clamp_fusion.1
  25.2 0.6 gather_fusion.1
  25.9 0.7 add_bitcast_fusion
  26.6 8.3 %all_to_all.39 = s32[5,8,5]{2,0,1:T(8,128)S(1)} all-to-all(s32[5,8,5]{2,0,1:T(8,128)S(1)} %copy.54), channel_id=1, replica_groups=mesh['row'=4,'col'=4,'depth'=2] {'row','depth'}, dimensions={1} | all-to-all | bytes 1600 | tf_op jit(solution)/shard_map/all_to_all | solution.py:45
  34.9 0.6 broadcast_in_dim.75
  35.5 3.3 all-to-all-start.1
  38.9 38.4 %all-gather.3.cloned.1.call-done = bf16[5,20,128,128]{3,2,1,0:T(8,128)(2,1)} async-done(((bf16[5,5,128,128]{3,2,1,0:T(8,128)(2,1)}), bf16[5,20,128,128]{3,2,1,0:T(8,128)(2,1)}) %all-gather.3.cloned.1.call-update) | async-done | bytes 3276816 | tf_op jit(solution)/shard_map/all_gather | solution.py:24
  77.3 7.2 %gather_fusion.3 = bf16[40,5,128,128]{3,2,1,0:T(8,128)(2,1)} fusion(bf16[5,20,128,128]{3,2,1,0:T(8,128)(2,1)} %all-gather.3.cloned.1.call-done, s32[1024]{0:T(1024)S(1)} %pad_clamp_fusion.1), kind=kCustom, calls=%fused_computation.3 | custom fusion | bytes 13107360 | tf_op jit(solution)/shard_map/gather | solution.py:36
  84.5 8.3 %copy.74 = bf16[8,5,5,128,128]{4,3,1,2,0:T(8,128)(2,1)} copy(bf16[8,5,5,128,128]{4,3,2,1,0:T(8,128)(2,1)} %bitcast.82) | data formatting | bytes 13107200 | tf_op jit(solution)/shard_map/gather | solution.py:36
  92.8 4.9 %all-to-all-start.2 = ((bf16[5,8,5,128,128]{4,3,2,0,1:T(8,128)(2,1)}), bf16[5,8,5,128,128]{4,3,2,0,1:T(8,128)(2,1)}, u32[]{:S(2)}, u32[]{:S(2)}) async-start(bf16[5,8,5,128,128]{4,3,2,0,1:T(8,128)(2,1)} %bitcast.81), calls=%async_computation.2 | async-start | bytes 13107200 | tf_op jit(solution)/shard_map/all_to_all | solution.py:44
  98.2 0.7 gather_fusion.2
  99.6 0.2 copy.69
  99.8 72.3 %all-to-all-done.2 = bf16[5,8,5,128,128]{4,3,2,0,1:T(8,128)(2,1)} async-done(((bf16[5,8,5,128,128]{4,3,2,0,1:T(8,128)(2,1)}), bf16[5,8,5,128,128]{4,3,2,0,1:T(8,128)(2,1)}, u32[]{:S(2)}, u32[]{:S(2)}) %all-to-all-start.2) | async-done | bytes 6553632 | tf_op jit(solution)/shard_map/all_to_all | solution.py:44
  172.1 6.1 %bitcast_select_fusion = bf16[8,5,5,128,128]{4,3,2,1,0:T(8,128)(2,1)} fusion(bf16[5,8,5,128,128]{4,3,2,0,1:T(8,128)(2,1)} %all-to-all-done.2, pred[8,5,5]{2,1,0:T(8,128)(4,1)S(1)} %and_bitcast_fusion), kind=kLoop, calls=%fused_computation.24 | loop fusion | flops 3276800 | bytes 13107400 | tf_op jit(solution)/shard_map/jit(_where)/select_n | solution.py:58
  178.2 193.2 %while.10 = (s32[]{:T(128)}, f32[8,5,5,128,128]{4,3,2,1,0:T(8,128)}, pred[8,5,5,5]{3,2,1,0:T(8,128)(4,1)S(1)}, s32[8,5,5]{2,1,0:T(8,128)S(1)}, s32[8,5,5,5]{1,0,...) while((s32[]{:T(128)}, ...), condition=%wide.region_3.4_spmd, body=%wide.region_2.3_spmd.sunk | while | flops 526336864 | bytes 29498244 | solution.py:74
  178.5 9.1 %gather_fusion = bf16[125,128,128]{2,1,0:T(8,128)(2,1)} fusion(bf16[100,5,128,128]{3,2,1,0:T(8,128)(2,1)} %get-tuple-element.144, s32[125]{0:T(128)S(1)} %reshape.192), kind=kCustom, calls=%fused_computation.clone.1 | custom fusion | bytes 8193000 | tf_op jit(solution)/shard_map/while/body/eval_jaxpr/gather | solution.py:68
  187.6 7.8 %copy.80 = bf16[5,5,5,128,128]{3,4,1,2,0:T(8,128)(2,1)} copy(bf16[5,5,5,128,128]{4,3,2,1,0:T(8,128)(2,1)} %bitcast.80) | data formatting | bytes 8192000 | tf_op jit(solution)/shard_map/while/body/eval_jaxpr/gather | solution.py:68
  195.6 3.6 fusion.28
  199.2 1.8 copy.82
  201.0 1.3 constant_dynamic-update-slice_fusion.2
  202.6 9.1 %gather_fusion = bf16[125,128,128]{2,1,0:T(8,128)(2,1)} fusion(bf16[100,5,128,128]{3,2,1,0:T(8,128)(2,1)} %get-tuple-element.144, s32[125]{0:T(128)S(1)} %reshape.192), kind=kCustom, calls=%fused_computation.clone.1 | custom fusion | bytes 8193000 | tf_op jit(solution)/shard_map/while/body/eval_jaxpr/gather | solution.py:68
  211.7 7.8 %copy.80 = bf16[5,5,5,128,128]{3,4,1,2,0:T(8,128)(2,1)} copy(bf16[5,5,5,128,128]{4,3,2,1,0:T(8,128)(2,1)} %bitcast.80) | data formatting | bytes 8192000 | tf_op jit(solution)/shard_map/while/body/eval_jaxpr/gather | solution.py:68
  219.7 3.6 fusion.28
  223.3 1.8 copy.82
  225.1 1.3 constant_dynamic-update-slice_fusion.2
  226.8 9.1 %gather_fusion = bf16[125,128,128]{2,1,0:T(8,128)(2,1)} fusion(bf16[100,5,128,128]{3,2,1,0:T(8,128)(2,1)} %get-tuple-element.144, s32[125]{0:T(128)S(1)} %reshape.192), kind=kCustom, calls=%fused_computation.clone.1 | custom fusion | bytes 8193000 | tf_op jit(solution)/shard_map/while/body/eval_jaxpr/gather | solution.py:68
  235.9 7.8 %copy.80 = bf16[5,5,5,128,128]{3,4,1,2,0:T(8,128)(2,1)} copy(bf16[5,5,5,128,128]{4,3,2,1,0:T(8,128)(2,1)} %bitcast.80) | data formatting | bytes 8192000 | tf_op jit(solution)/shard_map/while/body/eval_jaxpr/gather | solution.py:68
  243.7 0.1 copy.81
  243.8 3.6 fusion.28
  247.5 1.8 copy.82
  249.3 1.3 constant_dynamic-update-slice_fusion.2
  250.9 9.1 %gather_fusion = bf16[125,128,128]{2,1,0:T(8,128)(2,1)} fusion(bf16[100,5,128,128]{3,2,1,0:T(8,128)(2,1)} %get-tuple-element.144, s32[125]{0:T(128)S(1)} %reshape.192), kind=kCustom, calls=%fused_computation.clone.1 | custom fusion | bytes 8193000 | tf_op jit(solution)/shard_map/while/body/eval_jaxpr/gather | solution.py:68
  260.0 7.8 %copy.80 = bf16[5,5,5,128,128]{3,4,1,2,0:T(8,128)(2,1)} copy(bf16[5,5,5,128,128]{4,3,2,1,0:T(8,128)(2,1)} %bitcast.80) | data formatting | bytes 8192000 | tf_op jit(solution)/shard_map/while/body/eval_jaxpr/gather | solution.py:68
  267.9 3.6 fusion.28
  271.6 1.8 copy.82
  273.4 1.3 constant_dynamic-update-slice_fusion.2
  275.1 9.1 %gather_fusion = bf16[125,128,128]{2,1,0:T(8,128)(2,1)} fusion(bf16[100,5,128,128]{3,2,1,0:T(8,128)(2,1)} %get-tuple-element.144, s32[125]{0:T(128)S(1)} %reshape.192), kind=kCustom, calls=%fused_computation.clone.1 | custom fusion | bytes 8193000 | tf_op jit(solution)/shard_map/while/body/eval_jaxpr/gather | solution.py:68
  284.2 7.8 %copy.80 = bf16[5,5,5,128,128]{3,4,1,2,0:T(8,128)(2,1)} copy(bf16[5,5,5,128,128]{4,3,2,1,0:T(8,128)(2,1)} %bitcast.80) | data formatting | bytes 8192000 | tf_op jit(solution)/shard_map/while/body/eval_jaxpr/gather | solution.py:68
  292.0 0.1 copy.81
  292.1 3.7 fusion.28
  295.8 1.8 copy.82
  297.6 1.3 constant_dynamic-update-slice_fusion.2
  299.2 9.1 %gather_fusion = bf16[125,128,128]{2,1,0:T(8,128)(2,1)} fusion(bf16[100,5,128,128]{3,2,1,0:T(8,128)(2,1)} %get-tuple-element.144, s32[125]{0:T(128)S(1)} %reshape.192), kind=kCustom, calls=%fused_computation.clone.1 | custom fusion | bytes 8193000 | tf_op jit(solution)/shard_map/while/body/eval_jaxpr/gather | solution.py:68
  308.3 7.8 %copy.80 = bf16[5,5,5,128,128]{3,4,1,2,0:T(8,128)(2,1)} copy(bf16[5,5,5,128,128]{4,3,2,1,0:T(8,128)(2,1)} %bitcast.80) | data formatting | bytes 8192000 | tf_op jit(solution)/shard_map/while/body/eval_jaxpr/gather | solution.py:68
  316.1 0.1 copy.81
  316.3 3.6 fusion.28
  319.9 1.8 copy.82
  321.7 1.4 constant_dynamic-update-slice_fusion.2
  323.4 9.1 %gather_fusion = bf16[125,128,128]{2,1,0:T(8,128)(2,1)} fusion(bf16[100,5,128,128]{3,2,1,0:T(8,128)(2,1)} %get-tuple-element.144, s32[125]{0:T(128)S(1)} %reshape.192), kind=kCustom, calls=%fused_computation.clone.1 | custom fusion | bytes 8193000 | tf_op jit(solution)/shard_map/while/body/eval_jaxpr/gather | solution.py:68
  332.5 7.8 %copy.80 = bf16[5,5,5,128,128]{3,4,1,2,0:T(8,128)(2,1)} copy(bf16[5,5,5,128,128]{4,3,2,1,0:T(8,128)(2,1)} %bitcast.80) | data formatting | bytes 8192000 | tf_op jit(solution)/shard_map/while/body/eval_jaxpr/gather | solution.py:68
  340.5 3.6 fusion.28
  344.2 1.8 copy.82
  345.9 1.3 constant_dynamic-update-slice_fusion.2
  347.6 9.1 %gather_fusion = bf16[125,128,128]{2,1,0:T(8,128)(2,1)} fusion(bf16[100,5,128,128]{3,2,1,0:T(8,128)(2,1)} %get-tuple-element.144, s32[125]{0:T(128)S(1)} %reshape.192), kind=kCustom, calls=%fused_computation.clone.1 | custom fusion | bytes 8193000 | tf_op jit(solution)/shard_map/while/body/eval_jaxpr/gather | solution.py:68
  356.7 7.8 %copy.80 = bf16[5,5,5,128,128]{3,4,1,2,0:T(8,128)(2,1)} copy(bf16[5,5,5,128,128]{4,3,2,1,0:T(8,128)(2,1)} %bitcast.80) | data formatting | bytes 8192000 | tf_op jit(solution)/shard_map/while/body/eval_jaxpr/gather | solution.py:68
  364.6 3.6 fusion.28
  368.3 1.8 copy.82
  370.1 1.3 constant_dynamic-update-slice_fusion.2
  371.4 0.6 copy-done.1
  372.1 91.0 %reduce-scatter.2.cloned.1.call-done = f32[5,5,128,128]{3,2,1,0:T(8,128)} async-done(((f32[40,5,128,128]{3,2,1,0:T(8,128)}), f32[5,5,128,128]{3,2,1,0:T(8,128)}) %reduce-scatter.2.cloned.1.call-update) | async-done | bytes 1638416 | tf_op jit(solution)/shard_map/reduce_scatter | solution.py:84
  463.1 2.9 fusion.17
  (84 shorter events, 4.8 us)
Async XLA Ops:
  6.5 70.8 %all-gather.3.cloned.1.call-start = ((), (), s32[]{:S(2)}) async-start(), calls=%async_computation.4 | async-start | bytes 4096000 | tf_op jit(solution)/shard_map/all_gather | solution.py:24
  35.5 57.3 %all-to-all-start.1 = ((s32[5,8,5]{0,2,1:T(8,128)}), s32[5,8,5]{0,2,1:T(8,128)S(1)}, u32[]{:S(2)}, u32[]{:S(2)}) async-start(s32[5,8,5]{0,2,1:T(8,128)} %broadcast_in_dim.75), calls=%async_computation.1 | async-start | bytes 65536 | tf_op jit(solution)/shard_map/all_to_all | solution.py:46
  92.8 5.0 %copy-start = (s32[100,5]{0,1:T(8,128)S(1)}, s32[100,5]{0,1:T(8,128)}, u32[]{:S(2)}) copy-start(s32[100,5]{0,1:T(8,128)} %param.10) | copy-start | bytes 6004
  92.8 79.3 %all-to-all-start.2 = ((bf16[5,8,5,128,128]{4,3,2,0,1:T(8,128)(2,1)}), bf16[5,8,5,128,128]{4,3,2,0,1:T(8,128)(2,1)}, u32[]{:S(2)}, u32[]{:S(2)}) async-start(bf16[5,8,5,128,128]{4,3,2,0,1:T(8,128)(2,1)} %bitcast.81), calls=%async_computation.2 | async-start | bytes 13107200 | tf_op jit(solution)/shard_map/all_to_all | solution.py:44
  97.7 365.4 %reduce-scatter.2.cloned.1.call-start = ((), (), s32[]{:S(2)}) async-start(), calls=%async_computation.5 | async-start | bytes 14745600 | tf_op jit(solution)/shard_map/reduce_scatter | solution.py:84
  371.4 0.7 copy-start.1
Sparse Core Ops, SparseCore 0:
  8.9 68.3 all-gather.2
  371.5 91.5 reduce-scatter.1
where the time goes:
time: 475 us; the launch traced here: 473 us
  waiting for transfers between devices  202 us (43%)
  local copies, waits for them, and re-layouts  185 us (39%)
  matrix products  29.2 us (6%)
  blocking collectives  23.4 us (5%)
  between operations  13.5 us (3%)
  other arithmetic  11.5 us (2%)
  starting transfers between devices  8.27 us (2%)
    gather x16, local copies, waits for them, and re-layouts, group_product(): picked = values[row_index[:, :, None], slot_index]  135 us
    reduce_scatter x1, waiting for transfers between devices, body(): lax.psum_scatter(partial_terms, ('row', 'depth'), scatter_dimension=0, ti...  91 us
    all_to_all x1, waiting for transfers between devices, body(): lax.all_to_all(send_vals, ('row', 'depth'), split_axis=1, concat_axis=0,...  72.3 us
    all_gather x1, waiting for transfers between devices, body(): lax.all_gather(mine_vals, 'col', axis=1, tiled=True)  38.4 us
    dot_general x8, matrix products, group_product(): jnp.einsum('ilab,ilmbc->imac', block_vals, picked, preferred_element_type...  29.2 us
    dynamic_update_slice x16, local copies, waits for them, and re-layouts, body(): lax.map(group_product, (left_vals.reshape(groups, group_rows, left_slots,...  24.7 us
    gather x2, local copies, waits for them, and re-layouts, body(): send_vals = every_vals[:, slot_table]  15.5 us
    all_gather x1, blocking collectives, body(): lax.all_gather(mine_cols, 'col', axis=1, tiled=True)  15 us
  transfers between devices with their start and end apart: 4, of which 3 were waited for; matrix products, arithmetic and copies ran while one was open for 4% of the time, Pallas kernels for 0%

commit v1 on v0

v1 whole, which is shorter than its diff:
```python
import jax
import jax.numpy as jnp
from jax import lax
from jax.experimental import pallas as pl
from jax.experimental.pallas import tpu as pltpu
from jax.sharding import PartitionSpec as P


PARTS = (3, 2)
TOP = 32767.0
MANT = 8192.0
HERE = pl.BlockSpec(memory_space=pl.ANY)
SCALARS = pl.BlockSpec(memory_space=pltpu.SMEM)
RIGHT_BYTES = 20 << 20


def chunks_of(count):
    total = sum(PARTS)
    edges = [round(count * sum(PARTS[:i]) / total) for i in range(len(PARTS) + 1)]
    return [(a, b - a) for a, b in zip(edges[:-1], edges[1:]) if b > a]


def code_rows(count, size):
    return count * size + -(-2 * count // 16) * 16


def encode(out_ref, blocks):
    size, count = blocks[0].shape[0], len(blocks)
    top = jnp.concatenate([jnp.max(jnp.abs(x), axis=0, keepdims=True) for x in blocks], axis=0)
    top = jnp.maximum(top, 1e-30)
    e = jnp.floor(jnp.log2(top))
    mant = jnp.ceil(top * jnp.exp2(-e) * MANT) + 1.0
    inv = (TOP * MANT) / (mant * jnp.exp2(e))
    for m, x in enumerate(blocks):
        q = jnp.round(x * inv[m : m + 1])
        out_ref[pl.ds(m * size, size), :] = q.astype(jnp.int32).astype(jnp.int16)
    pad = out_ref.shape[0] - count * size - 2 * count
    codes = jnp.concatenate([e, mant, jnp.zeros((pad, size), jnp.float32)], axis=0)
    out_ref[pl.ds(count * size, 2 * count + pad), :] = codes.astype(jnp.int32).astype(jnp.int16)


def scales(ref, count, size):
    codes = ref[count * size :, :].astype(jnp.int32).astype(jnp.float32)
    exps, mants = codes[:count], codes[count : 2 * count]
    return mants * jnp.exp2(exps) * (1.0 / (TOP * MANT))


def decode(ref, scale, m, size):
    q = ref[pl.ds(m * size, size), :].astype(jnp.int32).astype(jnp.float32)
    return q * scale[m : m + 1, :]


def make_tables(where, every, pattern, sizes, chunks):
    parts, panels, depths, count, slots, rows_here, panel_cols = sizes
    per_part = panels // parts
    terms = per_part * slots
    total = parts * depths * count

    def kernel(where_ref, every_ref, pattern_ref, krow_ref, term_ref, slot_ref, live_ref):
        row, depth, z = where_ref[0], where_ref[1], where_ref[2]
        base = 0
        for s in range(depths):
            d = lax.rem(depth + s, depths)
            for first, n in chunks:
                def one(g, carry, base=base, d=d, first=first, n=n):
                    t, i = lax.div(g, n), lax.rem(g, n)
                    p0 = row ^ t

                    def columns_at(q):
                        return (((p0 * panels + q) * depths + d) * count + first + i) * slots

                    at = base + g
                    target = [every_ref[columns_at(z) + m] for m in range(slots)]
                    for l in range(terms):
                        term_ref[at * terms + l] = 0
                        krow_ref[at * terms + l] = 0
                    live = jnp.int32(0)
                    for l in range(terms):
                        j, m = divmod(l, slots)
                        column = every_ref[columns_at(row * per_part + j) + m]
                        k = column + j * panel_cols - depth * rows_here
                        inside = jnp.logical_and(k >= 0, k < rows_here)

                        @pl.when(inside)
                        def _(k=k, l=l, live=live):
                            term_ref[at * terms + live] = l
                            krow_ref[at * terms + live] = k
                            mine = [pattern_ref[k * slots + x] for x in range(slots)]
                            for m, want in enumerate(target):
                                found = jnp.int32(0)
                                for x in range(1, slots):
                                    found = jnp.where(mine[x] == want, x, found)
                                slot_ref[(at * terms + live) * slots + m] = found

                        live = live + inside.astype(jnp.int32)
                    live_ref[at] = live
                    return carry

                lax.fori_loop(0, parts * n, one, 0)
                base += parts * n

    shapes = [total * terms, total * terms, total * terms * slots, total]
    return pl.pallas_call(
        kernel,
        out_shape=[jax.ShapeDtypeStruct((x,), jnp.int32) for x in shapes],
        in_specs=[SCALARS] * 3,
        out_specs=[SCALARS] * 4,
        name="tables",
    )(where, every, pattern)


def gather_panels(own, ups, downs, where, parts, per_part):
    n, slots, size, _ = own.shape
    sources = [own, *ups, *downs]
    offsets = [0] + [-(s + 1) for s in range(len(ups))] + [s + 1 for s in range(len(downs))]

    def kernel(where_ref, *refs):
        outs = refs[len(sources) : len(sources) + parts]
        held, into, outof = refs[len(sources) + parts :]
        row, z = where_ref[0], where_ref[2]
        order = list(range(parts - 1, -1, -1))
        for t in order:
            for j in range(per_part):
                q = (row ^ t) * per_part + j
                for k, offset in enumerate(offsets):
                    @pl.when(q == z + offset)
                    def _(t=t, j=j, k=k):
                        to = t * per_part + j
                        pltpu.make_async_copy(refs[k], held.at[to], into.at[to]).start()
        copies = []
        for t in order:
            for j in range(per_part):
                to = t * per_part + j
                pltpu.make_async_copy(refs[0], held.at[to], into.at[to]).wait()
                copies.append(
                    pltpu.make_async_copy(
                        held.at[to], outs[t].at[:, pl.ds(j * slots, slots)], outof.at[to]
                    )
                )
                copies[-1].start()
        for copy in copies:
            copy.wait()

    panels = parts * per_part
    out = jax.ShapeDtypeStruct((n, per_part * slots, size, size), own.dtype)
    return pl.pallas_call(
        kernel,
        out_shape=[out] * parts,
        in_specs=[SCALARS] + [HERE] * len(sources),
        out_specs=[HERE] * parts,
        scratch_shapes=[
            pltpu.VMEM((panels, n, slots, size, size), own.dtype),
            pltpu.SemaphoreType.DMA((panels,)),
            pltpu.SemaphoreType.DMA((panels,)),
        ],
        cost_estimate=pl.CostEstimate(
            flops=0, bytes_accessed=4 * panels * n * slots * size * size, transcendentals=0
        ),
        name="gather_panels",
    )(where, *sources)


def product(lefts, values, tables, base, extra=None, joined=False):
    parts = len(lefts)
    n, terms, size, _ = lefts[0].shape
    slots = values.shape[1]
    height = code_rows(slots, size)
    rows = parts * n
    ahead = max(2, min(rows, RIGHT_BYTES // (terms * slots * size * size * 2)))

    def kernel(krow_ref, term_ref, slot_ref, live_ref, values_ref, *refs):
        left_refs, rest = refs[:parts], refs[parts:]
        if extra is not None:
            extra_ref, rest = rest[0], rest[1:]
        outs = rest[: 1 if joined else parts]
        left, right, acc, coded, got, left_sem, right_sem, got_sem, out_sem = rest[len(outs) :]

        def rights(g, act):
            at = lax.rem(g, ahead)
            for l in range(terms):
                @pl.when(l < live_ref[base + g])
                def _(l=l):
                    k = krow_ref[(base + g) * terms + l]
                    act(pltpu.make_async_copy(values_ref.at[k], right.at[at, l], right_sem.at[at, l]))

        def left_copy(t):
            return pltpu.make_async_copy(left_refs[t], left.at[pl.ds(t * n, n)], left_sem.at[t])

        def got_copy(t):
            part = pl.ds(t * n, n)
            return pltpu.make_async_copy(extra_ref.at[part], got.at[part], got_sem.at[t])

        def out_copy(t):
            part = pl.ds(t * n, n)
            to = outs[0].at[part] if joined else outs[t]
            return pltpu.make_async_copy(coded.at[part], to, out_sem.at[t])

        for t in range(parts):
            left_copy(t).start()
            if extra is not None:
                got_copy(t).start()

        def prime(g, carry):
            rights(g, lambda copy: copy.start())
            return carry

        lax.fori_loop(0, ahead - 1 if ahead < rows else rows, prime, 0)

        def one(g, carry):
            if ahead < rows:
                @pl.when(g + ahead - 1 < rows)
                def _():
                    rights(g + ahead - 1, lambda copy: copy.start())
            for t in range(parts):
                @pl.when(g == t * n)
                def _(t=t):
                    left_copy(t).wait()
                    if extra is not None:
                        got_copy(t).wait()
            rights(g, lambda copy: copy.wait())
            live = live_ref[base + g]
            at = lax.rem(g, ahead)

            def dot_of(low, number):
                sides = []
                for l in range(low, low + number):
                    entry = (base + g) * terms + l
                    sides.append(
                        (
                            left[g, term_ref[entry]],
                            jnp.concatenate(
                                [right[at, l, slot_ref[entry * slots + m]] for m in range(slots)], axis=1
                            ),
                        )
                    )
                return jnp.dot(
                    jnp.concatenate([a for a, _ in sides], axis=1),
                    jnp.concatenate([b for _, b in sides], axis=0),
                    preferred_element_type=jnp.float32,
                )

            @pl.when(live == 0)
            def _():
                acc[...] = jnp.zeros_like(acc)

            for low in range(0, terms, 2):
                for number in (1, 2):
                    if low + number > terms:
                        continue

                    @pl.when(live == low + 1 if number == 1 else live >= low + 2)
                    def _(low=low, number=number):
                        if low == 0:
                            acc[...] = dot_of(low, number)
                        else:
                            acc[...] += dot_of(low, number)

            blocks = [acc[:, m * size : (m + 1) * size] for m in range(slots)]
            if extra is not None:
                scale = scales(got.at[g], slots, size)
                blocks = [b + decode(got.at[g], scale, m, size) for m, b in enumerate(blocks)]
            encode(coded.at[g], blocks)
            for t in range(parts):
                @pl.when(g == t * n + n - 1)
                def _(t=t):
                    out_copy(t).start()
            return carry

        lax.fori_loop(0, rows, one, 0)
        for t in range(parts):
            out_copy(t).wait()

    if joined:
        out_shape = [jax.ShapeDtypeStruct((rows, height, size), jnp.int16)]
    else:
        out_shape = [jax.ShapeDtypeStruct((n, height, size), jnp.int16)] * parts
    operands = [*tables, values, *lefts] + ([] if extra is None else [extra])
    dma = pltpu.SemaphoreType.DMA
    got_rows = rows if extra is not None else 1
    out = pl.pallas_call(
        kernel,
        out_shape=out_shape,
        in_specs=[SCALARS] * 4 + [HERE] * (len(operands) - 4),
        out_specs=[HERE] * len(out_shape),
        scratch_shapes=[
            pltpu.VMEM((rows, terms, size, size), values.dtype),
            pltpu.VMEM((ahead, terms, slots, size, size), values.dtype),
            pltpu.VMEM((size, slots * size), jnp.float32),
            pltpu.VMEM((rows, height, size), jnp.int16),
            pltpu.VMEM((got_rows, height, size), jnp.int16),
            dma((parts,)), dma((ahead, terms)), dma((parts,)), dma((parts,)),
        ],
        cost_estimate=pl.CostEstimate(
            flops=2 * rows * terms * slots * size**3,
            bytes_accessed=rows * terms * (slots + 1) * size * size * 2,
            transcendentals=0,
        ),
        name="product",
    )(*operands)
    return out[0] if joined else out


def finish(received, values, flags, first, stride, count, before=None):
    parts = len(received)
    n, height, size = received[0].shape
    slots = values.shape[1]

    def kernel(flag_ref, own_ref, *refs):
        got, out_ref = refs[:parts], refs[-1]
        flag = flag_ref[first + pl.program_id(0)]
        scale = [scales(g.at[0], slots, size) for g in got]
        for m in range(slots):
            total = decode(got[0].at[0], scale[0], m, size)
            for p in range(1, parts):
                total = total + decode(got[p].at[0], scale[p], m, size)
            own = own_ref[0, m].astype(jnp.float32)
            out_ref[0, m] = jnp.where(flag == 1, total, 2.0 * own - total).astype(out_ref.dtype)

    piece = pl.BlockSpec((1, height, size), lambda i, f: (i, 0, 0))
    in_specs = [pl.BlockSpec((1, slots, size, size), lambda i, f: ((first + i) * stride, 0, 0, 0))]
    in_specs += [piece] * parts
    operands = [flags, values, *received]
    if before is not None:
        in_specs.append(HERE)
        operands.append(before)
    return pl.pallas_call(
        kernel,
        out_shape=jax.ShapeDtypeStruct((count, slots, size, size), values.dtype),
        grid_spec=pltpu.PrefetchScalarGridSpec(
            num_scalar_prefetch=1,
            grid=(n,),
            in_specs=in_specs,
            out_specs=pl.BlockSpec((1, slots, size, size), lambda i, f: (first + i, 0, 0, 0)),
        ),
        input_output_aliases={} if before is None else {len(operands) - 1: 0},
        name="finish",
    )(*operands)


def inner(values, pattern, branch_flag):
    parts, depths, panels = lax.axis_size("row"), lax.axis_size("depth"), lax.axis_size("col")
    row, depth, z = lax.axis_index("row"), lax.axis_index("depth"), lax.axis_index("col")
    rows_here, slots, _, _ = values.shape
    count = branch_flag.shape[0] // (parts * depths)
    stride = rows_here // count
    panel_cols = rows_here * parts * depths // panels
    per_part = panels // parts
    chunks = chunks_of(count)
    across = [[(i, i ^ t) for i in range(parts)] for t in range(parts)]
    up = [(i, i + 1) for i in range(panels - 1)]
    down = [(i + 1, i) for i in range(panels - 1)]
    where = jnp.stack([row, depth, z]).astype(jnp.int32)

    own = [values[a * stride : (a + n - 1) * stride + 1 : stride] for a, n in chunks]
    ups, downs = [[] for _ in chunks], [[] for _ in chunks]
    u, d = list(own), list(own)
    every = lax.all_to_all(
        jnp.broadcast_to(pattern[None, ::stride], (parts * panels * depths, count, slots)),
        ("row", "col", "depth"), split_axis=0, concat_axis=0, tiled=True,
    )
    tables = make_tables(
        where, every.reshape(-1), pattern.reshape(-1),
        (parts, panels, depths, count, slots, rows_here, panel_cols), chunks,
    )
    flags = lax.dynamic_slice_in_dim(branch_flag, (row * depths + depth) * count, count)

    for _ in range(panels - 1):
        for c in range(len(chunks)):
            u[c] = lax.ppermute(u[c], "col", up)
            d[c] = lax.ppermute(d[c], "col", down)
            ups[c].append(u[c])
            downs[c].append(d[c])

    out = None
    lefts = []
    for c in range(len(chunks)):
        picked = gather_panels(own[c], ups[c], downs[c], where, parts, per_part)
        got = [picked[0]]
        for t in range(1, parts):
            got.append(lax.ppermute(picked[t], "row", across[t]))
        lefts.append(got)

    base = [sum(parts * m for _, m in chunks[:c]) for c in range(len(chunks))]
    per_depth = parts * count
    for c, (first, n) in enumerate(chunks):
        extra = None
        for s in range(1, depths):
            here = []
            for t in range(parts):
                here.append(
                    lax.ppermute(lefts[c][t], "depth", [((i + s) % depths, i) for i in range(depths)])
                )
            part = product(here, values, tables, s * per_depth + base[c], joined=True)
            back = lax.ppermute(part, "depth", [(i, (i + s) % depths) for i in range(depths)])
            assert extra is None
            extra = back
        mine = product(lefts[c], values, tables, base[c], extra=extra)
        summed = [mine[0]]
        for t in range(1, parts):
            summed.append(lax.ppermute(mine[t], "row", across[t]))
        out = finish(summed, values, flags, first, stride, count, before=out)
    return out


def solution(mesh):
    in_specs = (P(("row", "depth"), "col", None, None), P(("row", "depth"), "col"), P())
    out_specs = P(("row", "depth"), "col", None, None)
    return jax.shard_map(inner, mesh=mesh, in_specs=in_specs, out_specs=out_specs, check_vma=False)
```

time: 475 us -> 226 us (0.48)
  local copies, waits for them, and re-layouts: 185 us -> 13.6 us
  waiting for transfers between devices: 202 us -> 101 us
  Pallas kernels: 0 us -> 54.2 us
  starting transfers between devices: 8.27 us -> 55.4 us
  matrix products: 29.2 us -> 0 us
  blocking collectives: 23.4 us -> 0 us
  between operations: 13.5 us -> 0.44 us
  other arithmetic: 11.5 us -> 0.6 us
    gather x25 -> x0, local copies, waits for them, and re-layouts: 153 us -> none  [the longest x16 135 us: group_product(): picked = values[row_index[:, :, None], slot_index]]
    ppermute x0 -> x34, waiting for transfers between devices: none -> 93.5 us  [the longest x6 30.3 us: inner(): u[c] = lax.ppermute(u[c], 'col', up)]
    reduce_scatter x1 -> x0, waiting for transfers between devices: 91 us -> none  [body(): lax.psum_scatter(partial_terms, ('row', 'depth'), scatter_dimension=0, ti...]
    all_to_all x2 -> x1, waiting for transfers between devices: 72.3 us -> 7.28 us  [inner(): lax.all_to_all(jnp.broadcast_to(pattern[None, ::stride], (parts * panels...]
    pallas_call x0 -> x9, Pallas kernels: none -> 54.2 us  [the longest x4 33.7 us: product(): pl.pallas_call(kernel, out_shape=out_shape, in_specs=[SCALARS] * 4 + [HER...]
    ppermute x0 -> x34, starting transfers between devices: none -> 51 us  [the longest x6 24.4 us: inner(): u[c] = lax.ppermute(u[c], 'col', up)]
    all_gather x1 -> x0, waiting for transfers between devices: 38.4 us -> none  [body(): lax.all_gather(mine_vals, 'col', axis=1, tiled=True)]
    dot_general x8 -> x0, matrix products: 29.2 us -> none  [group_product(): jnp.einsum('ilab,ilmbc->imac', block_vals, picked, preferred_element_type...]
  transfers between devices with their start and end apart: 4 -> 35, of which waited for: 3 -> 16; matrix products, arithmetic and copies ran while one was open for 4% -> 2% of each run, Pallas kernels for 0% -> 21%
where the time goes in v1:
time: 226 us; the launch traced here: 225 us
  waiting for transfers between devices  101 us (45%)
  starting transfers between devices  55.4 us (25%)
  Pallas kernels  54.2 us (24%)
  local copies, waits for them, and re-layouts  13.6 us (6%)
    pallas_call x4, Pallas kernels, product(): pl.pallas_call(kernel, out_shape=out_shape, in_specs=[SCALARS] * 4 + [HER...  33.7 us
    ppermute x6, waiting for transfers between devices, inner(): u[c] = lax.ppermute(u[c], 'col', up)  30.3 us
    ppermute x6, waiting for transfers between devices, inner(): got.append(lax.ppermute(picked[t], 'row', across[t]))  24.9 us
    ppermute x6, starting transfers between devices, inner(): u[c] = lax.ppermute(u[c], 'col', up)  24.4 us
    ppermute x6, waiting for transfers between devices, inner(): d[c] = lax.ppermute(d[c], 'col', down)  18.6 us
    ppermute x6, waiting for transfers between devices, inner(): summed.append(lax.ppermute(mine[t], 'row', across[t]))  18.3 us
    unnamed x65, local copies, waits for them, and re-layouts  8.62 us
    ppermute x6, starting transfers between devices, inner(): summed.append(lax.ppermute(mine[t], 'row', across[t]))  8.44 us
  transfers between devices with their start and end apart: 35, of which 16 were waited for; matrix products, arithmetic and copies ran while one was open for 2% of the time, Pallas kernels for 21%

profile of v1, /device:TPU:0, one launch (start us, length us, event | category | flops | bytes accessed | tf_op | source)
XLA Modules:
  0.0 225.1 jit_solution(8108891482704009005)
XLA Ops:
  0.0 1.1 slice.11.refs_0_
  1.1 5.0 %collective-permute-start.17 = (bf16[3,5,128,128]{3,2,1,0:T(8,128)(2,1)S(1)}, bf16[3,5,128,128]{3,2,1,0:T(8,128)(2,1)S(1)}, u32[]{:S(2)}, u32[]{:S(2)}) collective-permute-start(bf16[3,5,128,128]{3,2,1,0:T(8,128)(2,1)S(1)} %slice.11.refs_0_), channel_id=1, source_target_pairs={{0,2},{2,4},{4,6},{1,3},{3,5},{5,7},{8,10},{10,12},{12,14},{9,11},... | collective-permute-start | bytes 1474568 | tf_op jit(solution)/shard_map/ppermute | solution.py:369
  6.1 1.3 collective-permute-start.20
  7.4 9.1 %collective-permute-done.17.refs_1_ = bf16[3,5,128,128]{3,2,1,0:T(8,128)(2,1)S(1)} collective-permute-done((bf16[3,5,128,128]{3,2,1,0:T(8,128)(2,1)S(1)}, bf16[3,5,128,128]{3,2,1,0:T(8,128)(2,1)S(1)}, u32[]{:S(2)}, u32[]{:S(2)}) %collective-permute-start.17) | collective-permute-done | bytes 491552 | tf_op jit(solution)/shard_map/ppermute | solution.py:369
  16.5 4.4 %collective-permute-start.18 = (bf16[3,5,128,128]{3,2,1,0:T(8,128)(2,1)S(1)}, bf16[3,5,128,128]{3,2,1,0:T(8,128)(2,1)S(1)}, u32[]{:S(2)}, u32[]{:S(2)}) collective-permute-start(bf16[3,5,128,128]{3,2,1,0:T(8,128)(2,1)S(1)} %collective-permute-done.17.refs_1_), channel_id=1, source_target_pairs={{0,2},{2,4},{4,6},{1,3},{3,5},{5,7},{8,10},{10,12},{12,14},{9,11},... | collective-permute-start | bytes 1474568 | tf_op jit(solution)/shard_map/ppermute | solution.py:369
  20.9 1.3 collective-permute-start.21
  22.2 8.3 %collective-permute-done.18.refs_2_ = bf16[3,5,128,128]{3,2,1,0:T(8,128)(2,1)S(1)} collective-permute-done((bf16[3,5,128,128]{3,2,1,0:T(8,128)(2,1)S(1)}, bf16[3,5,128,128]{3,2,1,0:T(8,128)(2,1)S(1)}, u32[]{:S(2)}, u32[]{:S(2)}) %collective-permute-start.18) | collective-permute-done | bytes 491552 | tf_op jit(solution)/shard_map/ppermute | solution.py:369
  30.5 4.4 %collective-permute-start.19 = (bf16[3,5,128,128]{3,2,1,0:T(8,128)(2,1)S(1)}, bf16[3,5,128,128]{3,2,1,0:T(8,128)(2,1)S(1)}, u32[]{:S(2)}, u32[]{:S(2)}) collective-permute-start(bf16[3,5,128,128]{3,2,1,0:T(8,128)(2,1)S(1)} %collective-permute-done.18.refs_2_), channel_id=1, source_target_pairs={{0,2},{2,4},{4,6},{1,3},{3,5},{5,7},{8,10},{10,12},{12,14},{9,11},... | collective-permute-start | bytes 1474568 | tf_op jit(solution)/shard_map/ppermute | solution.py:369
  34.9 1.3 collective-permute-start.22
  36.2 0.6 pad_add_fusion.where_ref
  36.8 6.8 %collective-permute-done.19.refs_3_ = bf16[3,5,128,128]{3,2,1,0:T(8,128)(2,1)S(1)} collective-permute-done((bf16[3,5,128,128]{3,2,1,0:T(8,128)(2,1)S(1)}, bf16[3,5,128,128]{3,2,1,0:T(8,128)(2,1)S(1)}, u32[]{:S(2)}, u32[]{:S(2)}) %collective-permute-start.19) | collective-permute-done | bytes 491552 | tf_op jit(solution)/shard_map/ppermute | solution.py:369
  43.6 4.2 %collective-permute-done.22.refs_6_ = bf16[3,5,128,128]{3,2,1,0:T(8,128)(2,1)S(1)} collective-permute-done((bf16[3,5,128,128]{3,2,1,0:T(8,128)(2,1)S(1)}, bf16[3,5,128,128]{3,2,1,0:T(8,128)(2,1)S(1)}, u32[]{:S(2)}, u32[]{:S(2)}) %collective-permute-start.22) | collective-permute-done | bytes 491552 | tf_op jit(solution)/shard_map/ppermute | solution.py:370
  47.8 0.8 copy-done.17
  48.6 3.1 %gather_panels.3 = (bf16[3,5,128,128]{3,2,1,0:T(8,128)(2,1)}, bf16[3,5,128,128]{3,2,1,0:T(8,128)(2,1)}, bf16[3,5,128,128]{3,2,1,0:T(8,128)(2,1)}, bf16[3,5,128,128]{3,2,1,0:T(8,128)(2,1)}) custom-call(s32[3]{0:T(128)} %pad_add_fusion.where_ref, bf16[3,5,128,128]{3,2,1,0:T(8,128)(2,1)} %copy-done.1, bf16[3,5,128,128]{3,2,1,0:T(8,128)(2,1)} %copy-done.12, ...), custom_call_target="tpu_custom_call" | custom-call | bytes 3932160 | tf_op jit(solution)/shard_map/gather_panels/pallas_call | solution.py:146
  51.7 1.6 collective-permute-start.23
  53.2 1.5 collective-permute-start.24
  55.2 1.0 slice.10.refs_0_
  56.3 4.2 %collective-permute-start = (bf16[2,5,128,128]{3,2,1,0:T(8,128)(2,1)S(1)}, bf16[2,5,128,128]{3,2,1,0:T(8,128)(2,1)}, u32[]{:S(2)}, u32[]{:S(2)}) collective-permute-start(bf16[2,5,128,128]{3,2,1,0:T(8,128)(2,1)S(1)} %slice.10.refs_0_), channel_id=1, source_target_pairs={{0,2},{2,4},{4,6},{1,3},{3,5},{5,7},{8,10},{10,12},{12,14},{9,11},... | collective-permute-start | bytes 983048 | tf_op jit(solution)/shard_map/ppermute | solution.py:369
  60.5 5.6 %collective-permute-done.23.refs_1_ = bf16[3,5,128,128]{3,2,1,0:T(8,128)(2,1)S(1)} collective-permute-done((bf16[3,5,128,128]{3,2,1,0:T(8,128)(2,1)}, bf16[3,5,128,128]{3,2,1,0:T(8,128)(2,1)S(1)}, u32[]{:S(2)}, u32[]{:S(2)}) %collective-permute-start.23) | collective-permute-done | bytes 491552 | tf_op jit(solution)/shard_map/ppermute | solution.py:380
  66.1 7.8 %collective-permute-done.24.refs_2_ = bf16[3,5,128,128]{3,2,1,0:T(8,128)(2,1)S(1)} collective-permute-done((bf16[3,5,128,128]{3,2,1,0:T(8,128)(2,1)}, bf16[3,5,128,128]{3,2,1,0:T(8,128)(2,1)S(1)}, u32[]{:S(2)}, u32[]{:S(2)}) %collective-permute-start.24) | collective-permute-done | bytes 491552 | tf_op jit(solution)/shard_map/ppermute | solution.py:380
  74.3 1.3 collective-permute-start.3
  75.6 10.4 %collective-permute-done.3.refs_4_ = bf16[2,5,128,128]{3,2,1,0:T(8,128)(2,1)} collective-permute-done((bf16[2,5,128,128]{3,2,1,0:T(8,128)(2,1)S(1)}, bf16[2,5,128,128]{3,2,1,0:T(8,128)(2,1)}, u32[]{:S(2)}, u32[]{:S(2)}) %collective-permute-start.3) | collective-permute-done | bytes 327712 | tf_op jit(solution)/shard_map/ppermute | solution.py:370
  86.0 4.2 %collective-permute-start.1 = (bf16[2,5,128,128]{3,2,1,0:T(8,128)(2,1)}, bf16[2,5,128,128]{3,2,1,0:T(8,128)(2,1)}, u32[]{:S(2)}, u32[]{:S(2)}) collective-permute-start(bf16[2,5,128,128]{3,2,1,0:T(8,128)(2,1)} %collective-permute-done.refs_1_), channel_id=1, source_target_pairs={{0,2},{2,4},{4,6},{1,3},{3,5},{5,7},{8,10},{10,12},{12,14},{9,11},... | collective-permute-start | bytes 983048 | tf_op jit(solution)/shard_map/ppermute | solution.py:369
  90.2 1.3 collective-permute-start.4
  91.7 0.7 broadcast_in_dim.2
  92.4 4.5 %all-to-all-start = ((s32[32,5,5]{2,1,0:T(8,128)}), s32[32,5,5]{2,1,0:T(8,128)S(1)}, u32[]{:S(2)}, u32[]{:S(2)}) async-start(s32[32,5,5]{2,1,0:T(8,128)} %broadcast_in_dim.2), calls=%async_computation | async-start | bytes 262144 | tf_op jit(solution)/shard_map/all_to_all | solution.py:357
  97.0 0.8 reshape.8.pattern_ref
  97.7 7.3 %all-to-all-done = s32[32,5,5]{2,1,0:T(8,128)S(1)} async-done(((s32[32,5,5]{2,1,0:T(8,128)}), s32[32,5,5]{2,1,0:T(8,128)S(1)}, u32[]{:S(2)}, u32[]{:S(2)}) %all-to-all-start) | async-done | bytes 3232 | tf_op jit(solution)/shard_map/all_to_all | solution.py:357
  105.0 0.8 reshape.7.every_ref
  105.8 7.2 %tables.1 = (s32[200]{0:T(256)}, s32[200]{0:T(256)}, s32[1000]{0:T(1024)}, s32[40]{0:T(128)}) custom-call(s32[3]{0:T(128)} %pad_add_fusion.where_ref, s32[800]{0:T(1024)} %reshape.7.every_ref, s32[500]{0:T(512)} %reshape.8.pattern_ref), custom_call_target="tpu_custom_call" | custom-call | tf_op jit(solution)/shard_map/tables/pallas_call | solution.py:103
  113.1 0.7 copy-done.11
  113.8 8.6 %product.6 = s16[12,656,128]{2,1,0:T(8,128)(2,1)} custom-call(s32[200]{0:T(256)} %get-tuple-element.25.krow_ref, s32[200]{0:T(256)} %get-tuple-element.26.term_ref, s32[1000]{0:T(1024)} %get-tuple-element.27.slot_ref, s32[40]{0:T(128)} %get-tuple-element.28.live_ref, bf16[100,5,128,128]{3,2,1,0:T(8,128)(2,1)} %own_ref.3, ...), custom_call_target="tpu_custom_call" | custom-call | flops 1258291200 | bytes 11796480 | tf_op jit(solution)/shard_map/product/pallas_call | solution.py:280
  122.5 2.2 collective-permute-start.30
  124.7 2.2 collective-permute-start.2
  126.9 1.3 collective-permute-start.5
  128.2 6.1 %collective-permute-done.2.refs_3_ = bf16[2,5,128,128]{3,2,1,0:T(8,128)(2,1)S(1)} collective-permute-done((bf16[2,5,128,128]{3,2,1,0:T(8,128)(2,1)}, bf16[2,5,128,128]{3,2,1,0:T(8,128)(2,1)S(1)}, u32[]{:S(2)}, u32[]{:S(2)}) %collective-permute-start.2) | collective-permute-done | bytes 327712 | tf_op jit(solution)/shard_map/ppermute | solution.py:369
  134.4 4.0 %collective-permute-done.5.refs_6_ = bf16[2,5,128,128]{3,2,1,0:T(8,128)(2,1)S(1)} collective-permute-done((bf16[2,5,128,128]{3,2,1,0:T(8,128)(2,1)}, bf16[2,5,128,128]{3,2,1,0:T(8,128)(2,1)S(1)}, u32[]{:S(2)}, u32[]{:S(2)}) %collective-permute-start.5) | collective-permute-done | bytes 327712 | tf_op jit(solution)/shard_map/ppermute | solution.py:370
  138.4 0.7 copy-done.22
  139.1 2.8 %gather_panels.2 = (bf16[2,5,128,128]{3,2,1,0:T(8,128)(2,1)}, bf16[2,5,128,128]{3,2,1,0:T(8,128)(2,1)}, bf16[2,5,128,128]{3,2,1,0:T(8,128)(2,1)}, bf16[2,5,128,128]{3,2,1,0:T(8,128)(2,1)}) custom-call(s32[3]{0:T(128)} %pad_add_fusion.where_ref, bf16[2,5,128,128]{3,2,1,0:T(8,128)(2,1)} %copy-done.3, bf16[2,5,128,128]{3,2,1,0:T(8,128)(2,1)} %collective-permute-done.refs_1_, ...), custom_call_target="tpu_custom_call" | custom-call | bytes 2621440 | tf_op jit(solution)/shard_map/gather_panels/pallas_call | solution.py:146
  142.0 0.5 collective-permute-start.7
  142.5 3.0 %collective-permute-start.8 = (bf16[2,5,128,128]{3,2,1,0:T(8,128)(2,1)}, bf16[2,5,128,128]{3,2,1,0:T(8,128)(2,1)S(1)}, u32[]{:S(2)}, u32[]{:S(2)}) collective-permute-start(bf16[2,5,128,128]{3,2,1,0:T(8,128)(2,1)} %get-tuple-element.32), channel_id=1, source_target_pairs={{0,24},{8,16},{16,8},{24,0},{1,25},{9,17},{17,9},{25,1},{2,26},{10... | collective-permute-start | bytes 983048 | tf_op jit(solution)/shard_map/ppermute | solution.py:380
  145.5 7.3 %collective-permute-done.6.refs_1_ = bf16[2,5,128,128]{3,2,1,0:T(8,128)(2,1)S(1)} collective-permute-done((bf16[2,5,128,128]{3,2,1,0:T(8,128)(2,1)}, bf16[2,5,128,128]{3,2,1,0:T(8,128)(2,1)S(1)}, u32[]{:S(2)}, u32[]{:S(2)}) %collective-permute-start.6) | collective-permute-done | bytes 327712 | tf_op jit(solution)/shard_map/ppermute | solution.py:380
  152.8 0.8 copy-done.23
  153.6 4.3 %collective-permute-done.7.refs_2_ = bf16[2,5,128,128]{3,2,1,0:T(8,128)(2,1)S(1)} collective-permute-done((bf16[2,5,128,128]{3,2,1,0:T(8,128)(2,1)}, bf16[2,5,128,128]{3,2,1,0:T(8,128)(2,1)S(1)}, u32[]{:S(2)}, u32[]{:S(2)}) %collective-permute-start.7) | collective-permute-done | bytes 327712 | tf_op jit(solution)/shard_map/ppermute | solution.py:380
  157.9 0.5 collective-permute-start.12
  158.6 0.9 collective-permute-done.11.refs_2_
  160.2 0.7 copy-done.29
  160.9 7.0 %product.4 = s16[8,656,128]{2,1,0:T(8,128)(2,1)} custom-call(s32[200]{0:T(256)} %get-tuple-element.25.krow_ref, s32[200]{0:T(256)} %get-tuple-element.26.term_ref, s32[1000]{0:T(1024)} %get-tuple-element.27.slot_ref, s32[40]{0:T(128)} %get-tuple-element.28.live_ref, bf16[100,5,128,128]{3,2,1,0:T(8,128)(2,1)} %own_ref.3, bf16[2,5,128,128]{3,2,1,0:T(8,128)(2,1)} %copy-done.26, ...), custom_call_target="tpu_custom_call" | custom-call | flops 838860800 | bytes 7864320 | tf_op jit(solution)/shard_map/product/pallas_call | solution.py:280
  168.1 1.3 copy-done
  169.4 9.7 %product.7 = (s16[3,656,128]{2,1,0:T(8,128)(2,1)}, s16[3,656,128]{2,1,0:T(8,128)(2,1)}, s16[3,656,128]{2,1,0:T(8,128)(2,1)}, s16[3,656,128]{2,1,0:T(8,128)(2,1)}) custom-call(s32[200]{0:T(256)} %get-tuple-element.25.krow_ref, s32[200]{0:T(256)} %get-tuple-element.26.term_ref, s32[1000]{0:T(1024)} %get-tuple-element.27.slot_ref, ...), custom_call_target="tpu_custom_call" | custom-call | flops 1258291200 | bytes 11796480 | tf_op jit(solution)/shard_map/product/pallas_call | solution.py:280
  179.1 2.7 %collective-permute-start.31 = (s16[3,656,128]{2,1,0:T(8,128)(2,1)}, s16[3,656,128]{2,1,0:T(8,128)(2,1)S(1)}, u32[]{:S(2)}, u32[]{:S(2)}) collective-permute-start(s16[3,656,128]{2,1,0:T(8,128)(2,1)} %get-tuple-element.42), channel_id=1, source_target_pairs={{0,8},{8,0},{16,24},{24,16},{1,9},{9,1},{17,25},{25,17},{2,10},{10... | collective-permute-start | bytes 1511432 | tf_op jit(solution)/shard_map/ppermute | solution.py:400
  181.8 1.1 collective-permute-start.32
  183.4 1.1 copy-done.2
  184.5 8.3 %product.5 = (s16[2,656,128]{2,1,0:T(8,128)(2,1)}, s16[2,656,128]{2,1,0:T(8,128)(2,1)}, s16[2,656,128]{2,1,0:T(8,128)(2,1)}, s16[2,656,128]{2,1,0:T(8,128)(2,1)}) custom-call(s32[200]{0:T(256)} %get-tuple-element.25.krow_ref, s32[200]{0:T(256)} %get-tuple-element.26.term_ref, s32[1000]{0:T(1024)} %get-tuple-element.27.slot_ref, ...), custom_call_target="tpu_custom_call" | custom-call | flops 838860800 | bytes 7864320 | tf_op jit(solution)/shard_map/product/pallas_call | solution.py:280
  192.8 1.8 collective-permute-start.14
  194.5 1.1 collective-permute-start.15
  195.6 1.4 collective-permute-start.16
  197.0 0.6 dynamic_slice.3.flag_ref
  197.5 9.7 %collective-permute-done.32.refs_2_ = s16[3,656,128]{2,1,0:T(8,128)(2,1)S(1)} collective-permute-done((s16[3,656,128]{2,1,0:T(8,128)(2,1)}, s16[3,656,128]{2,1,0:T(8,128)(2,1)S(1)}, u32[]{:S(2)}, u32[]{:S(2)}) %collective-permute-start.32) | collective-permute-done | bytes 503840 | tf_op jit(solution)/shard_map/ppermute | solution.py:400
  207.2 0.8 copy-done.5
  208.2 4.4 %finish.2.refs_4_ = bf16[5,5,128,128]{3,2,1,0:T(8,128)(2,1)} custom-call(s32[5]{0:T(128)} %dynamic_slice.3.flag_ref, bf16[100,5,128,128]{3,2,1,0:T(8,128)(2,1)} %own_ref.3, s16[3,656,128]{2,1,0:T(8,128)(2,1)} %get-tuple-element.41.refs_0_, s16[3,656,128]{2,1,0:T(8,128)(2,1)} %copy-done.4, s16[3,656,128]{2,1,0:T(8,128)(2,1)} %copy-done.5, ...), custom_call_target="tpu_custom_call" | custom-call | tf_op jit(solution)/shard_map/finish/pallas_call | solution.py:326
  212.5 8.6 %collective-permute-done.15.refs_2_ = s16[2,656,128]{2,1,0:T(8,128)(2,1)S(1)} collective-permute-done((s16[2,656,128]{2,1,0:T(8,128)(2,1)}, s16[2,656,128]{2,1,0:T(8,128)(2,1)S(1)}, u32[]{:S(2)}, u32[]{:S(2)}) %collective-permute-start.15) | collective-permute-done | bytes 335904 | tf_op jit(solution)/shard_map/ppermute | solution.py:400
  221.2 0.7 copy-done.19
  222.0 3.1 %finish.3 = bf16[5,5,128,128]{3,2,1,0:T(8,128)(2,1)} custom-call(s32[5]{0:T(128)} %dynamic_slice.3.flag_ref, bf16[100,5,128,128]{3,2,1,0:T(8,128)(2,1)} %own_ref.3, s16[2,656,128]{2,1,0:T(8,128)(2,1)} %get-tuple-element.33.refs_0_, s16[2,656,128]{2,1,0:T(8,128)(2,1)} %copy-done.18, s16[2,656,128]{2,1,0:T(8,128)(2,1)} %copy-done.19, ...), custom_call_target="tpu_custom_call", output_to_operand_aliasing={{}: (6, {})} | custom-call | tf_op jit(solution)/shard_map/finish/pallas_call | solution.py:326
  (89 shorter events, 3.3 us)
Async XLA Ops:
  1.1 46.7 %copy-start.1 = (bf16[3,5,128,128]{3,2,1,0:T(8,128)(2,1)}, bf16[3,5,128,128]{3,2,1,0:T(8,128)(2,1)S(1)}, u32[]{:S(2)}) copy-start(bf16[3,5,128,128]{3,2,1,0:T(8,128)(2,1)S(1)} %slice.11.refs_0_) | copy-start | bytes 1474564
  1.1 15.4 %collective-permute-start.17 = (bf16[3,5,128,128]{3,2,1,0:T(8,128)(2,1)S(1)}, bf16[3,5,128,128]{3,2,1,0:T(8,128)(2,1)S(1)}, u32[]{:S(2)}, u32[]{:S(2)}) collective-permute-start(bf16[3,5,128,128]{3,2,1,0:T(8,128)(2,1)S(1)} %slice.11.refs_0_), channel_id=1, source_target_pairs={{0,2},{2,4},{4,6},{1,3},{3,5},{5,7},{8,10},{10,12},{12,14},{9,11},... | collective-permute-start | bytes 1474568 | tf_op jit(solution)/shard_map/ppermute | solution.py:369
  6.1 14.8 %collective-permute-start.20 = (bf16[3,5,128,128]{3,2,1,0:T(8,128)(2,1)S(1)}, bf16[3,5,128,128]{3,2,1,0:T(8,128)(2,1)S(1)}, u32[]{:S(2)}, u32[]{:S(2)}) collective-permute-start(bf16[3,5,128,128]{3,2,1,0:T(8,128)(2,1)S(1)} %slice.11.refs_0_), channel_id=1, source_target_pairs={{2,0},{4,2},{6,4},{3,1},{5,3},{7,5},{10,8},{12,10},{14,12},{11,9},... | collective-permute-start | bytes 1474568 | tf_op jit(solution)/shard_map/ppermute | solution.py:370
  16.5 31.3 %copy-start.12 = (bf16[3,5,128,128]{3,2,1,0:T(8,128)(2,1)}, bf16[3,5,128,128]{3,2,1,0:T(8,128)(2,1)S(1)}, u32[]{:S(2)}) copy-start(bf16[3,5,128,128]{3,2,1,0:T(8,128)(2,1)S(1)} %collective-permute-done.17.refs_1_) | copy-start | bytes 1474564
  16.5 14.0 %collective-permute-start.18 = (bf16[3,5,128,128]{3,2,1,0:T(8,128)(2,1)S(1)}, bf16[3,5,128,128]{3,2,1,0:T(8,128)(2,1)S(1)}, u32[]{:S(2)}, u32[]{:S(2)}) collective-permute-start(bf16[3,5,128,128]{3,2,1,0:T(8,128)(2,1)S(1)} %collective-permute-done.17.refs_1_), channel_id=1, source_target_pairs={{0,2},{2,4},{4,6},{1,3},{3,5},{5,7},{8,10},{10,12},{12,14},{9,11},... | collective-permute-start | bytes 1474568 | tf_op jit(solution)/shard_map/ppermute | solution.py:369
  20.9 26.9 %copy-start.13 = (bf16[3,5,128,128]{3,2,1,0:T(8,128)(2,1)}, bf16[3,5,128,128]{3,2,1,0:T(8,128)(2,1)S(1)}, u32[]{:S(2)}) copy-start(bf16[3,5,128,128]{3,2,1,0:T(8,128)(2,1)S(1)} %collective-permute-done.20.refs_4_) | copy-start | bytes 1474564
  20.9 14.0 %collective-permute-start.21 = (bf16[3,5,128,128]{3,2,1,0:T(8,128)(2,1)S(1)}, bf16[3,5,128,128]{3,2,1,0:T(8,128)(2,1)S(1)}, u32[]{:S(2)}, u32[]{:S(2)}) collective-permute-start(bf16[3,5,128,128]{3,2,1,0:T(8,128)(2,1)S(1)} %collective-permute-done.20.refs_4_), channel_id=1, source_target_pairs={{2,0},{4,2},{6,4},{3,1},{5,3},{7,5},{10,8},{12,10},{14,12},{11,9},... | collective-permute-start | bytes 1474568 | tf_op jit(solution)/shard_map/ppermute | solution.py:370
  30.5 17.3 %copy-start.14 = (bf16[3,5,128,128]{3,2,1,0:T(8,128)(2,1)}, bf16[3,5,128,128]{3,2,1,0:T(8,128)(2,1)S(1)}, u32[]{:S(2)}) copy-start(bf16[3,5,128,128]{3,2,1,0:T(8,128)(2,1)S(1)} %collective-permute-done.18.refs_2_) | copy-start | bytes 1474564
  30.5 13.1 %collective-permute-start.19 = (bf16[3,5,128,128]{3,2,1,0:T(8,128)(2,1)S(1)}, bf16[3,5,128,128]{3,2,1,0:T(8,128)(2,1)S(1)}, u32[]{:S(2)}, u32[]{:S(2)}) collective-permute-start(bf16[3,5,128,128]{3,2,1,0:T(8,128)(2,1)S(1)} %collective-permute-done.18.refs_2_), channel_id=1, source_target_pairs={{0,2},{2,4},{4,6},{1,3},{3,5},{5,7},{8,10},{10,12},{12,14},{9,11},... | collective-permute-start | bytes 1474568 | tf_op jit(solution)/shard_map/ppermute | solution.py:369
  34.9 12.9 %copy-start.15 = (bf16[3,5,128,128]{3,2,1,0:T(8,128)(2,1)}, bf16[3,5,128,128]{3,2,1,0:T(8,128)(2,1)S(1)}, u32[]{:S(2)}) copy-start(bf16[3,5,128,128]{3,2,1,0:T(8,128)(2,1)S(1)} %collective-permute-done.21.refs_5_) | copy-start | bytes 1474564
  34.9 12.9 %collective-permute-start.22 = (bf16[3,5,128,128]{3,2,1,0:T(8,128)(2,1)S(1)}, bf16[3,5,128,128]{3,2,1,0:T(8,128)(2,1)S(1)}, u32[]{:S(2)}, u32[]{:S(2)}) collective-permute-start(bf16[3,5,128,128]{3,2,1,0:T(8,128)(2,1)S(1)} %collective-permute-done.21.refs_5_), channel_id=1, source_target_pairs={{2,0},{4,2},{6,4},{3,1},{5,3},{7,5},{10,8},{12,10},{14,12},{11,9},... | collective-permute-start | bytes 1474568 | tf_op jit(solution)/shard_map/ppermute | solution.py:370
  36.8 54.7 %copy-start.30 = (s32[100,5]{0,1:T(8,128)S(1)}, s32[100,5]{0,1:T(8,128)}, u32[]{:S(2)}) copy-start(s32[100,5]{0,1:T(8,128)} %param.4) | copy-start | bytes 6004
  43.6 4.2 %copy-start.16 = (bf16[3,5,128,128]{3,2,1,0:T(8,128)(2,1)}, bf16[3,5,128,128]{3,2,1,0:T(8,128)(2,1)S(1)}, u32[]{:S(2)}) copy-start(bf16[3,5,128,128]{3,2,1,0:T(8,128)(2,1)S(1)} %collective-permute-done.19.refs_3_) | copy-start | bytes 1474564
  47.8 0.8 copy-start.17
  51.7 14.4 %collective-permute-start.23 = (bf16[3,5,128,128]{3,2,1,0:T(8,128)(2,1)}, bf16[3,5,128,128]{3,2,1,0:T(8,128)(2,1)S(1)}, u32[]{:S(2)}, u32[]{:S(2)}) collective-permute-start(bf16[3,5,128,128]{3,2,1,0:T(8,128)(2,1)} %get-tuple-element.38), channel_id=1, source_target_pairs={{0,8},{8,0},{16,24},{24,16},{1,9},{9,1},{17,25},{25,17},{2,10},{10... | collective-permute-start | bytes 1474568 | tf_op jit(solution)/shard_map/ppermute | solution.py:380
  53.2 20.6 %collective-permute-start.24 = (bf16[3,5,128,128]{3,2,1,0:T(8,128)(2,1)}, bf16[3,5,128,128]{3,2,1,0:T(8,128)(2,1)S(1)}, u32[]{:S(2)}, u32[]{:S(2)}) collective-permute-start(bf16[3,5,128,128]{3,2,1,0:T(8,128)(2,1)} %get-tuple-element.39), channel_id=1, source_target_pairs={{0,16},{8,24},{16,0},{24,8},{1,17},{9,25},{17,1},{25,9},{2,18},{10... | collective-permute-start | bytes 1474568 | tf_op jit(solution)/shard_map/ppermute | solution.py:380
  54.8 19.1 %collective-permute-start.25 = (bf16[3,5,128,128]{3,2,1,0:T(8,128)(2,1)}, bf16[3,5,128,128]{3,2,1,0:T(8,128)(2,1)S(1)}, u32[]{:S(2)}, u32[]{:S(2)}) collective-permute-start(bf16[3,5,128,128]{3,2,1,0:T(8,128)(2,1)} %get-tuple-element.40), channel_id=1, source_target_pairs={{0,24},{8,16},{16,8},{24,0},{1,25},{9,17},{17,9},{25,1},{2,26},{10... | collective-permute-start | bytes 1474568 | tf_op jit(solution)/shard_map/ppermute | solution.py:380
  56.2 66.2 %copy-start.3 = (bf16[2,5,128,128]{3,2,1,0:T(8,128)(2,1)}, bf16[2,5,128,128]{3,2,1,0:T(8,128)(2,1)S(1)}, u32[]{:S(2)}) copy-start(bf16[2,5,128,128]{3,2,1,0:T(8,128)(2,1)S(1)} %slice.10.refs_0_) | copy-start | bytes 983044
  56.3 18.1 %collective-permute-start = (bf16[2,5,128,128]{3,2,1,0:T(8,128)(2,1)S(1)}, bf16[2,5,128,128]{3,2,1,0:T(8,128)(2,1)}, u32[]{:S(2)}, u32[]{:S(2)}) collective-permute-start(bf16[2,5,128,128]{3,2,1,0:T(8,128)(2,1)S(1)} %slice.10.refs_0_), channel_id=1, source_target_pairs={{0,2},{2,4},{4,6},{1,3},{3,5},{5,7},{8,10},{10,12},{12,14},{9,11},... | collective-permute-start | bytes 983048 | tf_op jit(solution)/shard_map/ppermute | solution.py:369
  60.5 29.8 %collective-permute-start.26 = (bf16[3,5,128,128]{3,2,1,0:T(8,128)(2,1)}, bf16[3,5,128,128]{3,2,1,0:T(8,128)(2,1)S(1)}, u32[]{:S(2)}, u32[]{:S(2)}) collective-permute-start(bf16[3,5,128,128]{3,2,1,0:T(8,128)(2,1)} %get-tuple-element.37.refs_0_), channel_id=1, source_target_pairs={{1,0},{0,1},{3,2},{2,3},{5,4},{4,5},{7,6},{6,7},{9,8},{8,9},{11,10... | collective-permute-start | bytes 1474568 | tf_op jit(solution)/shard_map/ppermute | solution.py:391
  66.1 47.0 %copy-start.7 = (bf16[3,5,128,128]{3,2,1,0:T(8,128)(2,1)}, bf16[3,5,128,128]{3,2,1,0:T(8,128)(2,1)S(1)}, u32[]{:S(2)}) copy-start(bf16[3,5,128,128]{3,2,1,0:T(8,128)(2,1)S(1)} %collective-permute-done.23.refs_1_) | copy-start | bytes 1474564
  66.1 47.0 %collective-permute-start.27 = (bf16[3,5,128,128]{3,2,1,0:T(8,128)(2,1)S(1)}, bf16[3,5,128,128]{3,2,1,0:T(8,128)(2,1)S(1)}, u32[]{:S(2)}, u32[]{:S(2)}) collective-permute-start(bf16[3,5,128,128]{3,2,1,0:T(8,128)(2,1)S(1)} %collective-permute-done.23.refs_1_), channel_id=1, source_target_pairs={{1,0},{0,1},{3,2},{2,3},{5,4},{4,5},{7,6},{6,7},{9,8},{8,9},{11,10... | collective-permute-start | bytes 1474568 | tf_op jit(solution)/shard_map/ppermute | solution.py:391
  73.8 39.2 %copy-start.8 = (bf16[3,5,128,128]{3,2,1,0:T(8,128)(2,1)}, bf16[3,5,128,128]{3,2,1,0:T(8,128)(2,1)S(1)}, u32[]{:S(2)}) copy-start(bf16[3,5,128,128]{3,2,1,0:T(8,128)(2,1)S(1)} %collective-permute-done.24.refs_2_) | copy-start | bytes 1474564
  73.8 39.2 %collective-permute-start.28 = (bf16[3,5,128,128]{3,2,1,0:T(8,128)(2,1)S(1)}, bf16[3,5,128,128]{3,2,1,0:T(8,128)(2,1)}, u32[]{:S(2)}, u32[]{:S(2)}) collective-permute-start(bf16[3,5,128,128]{3,2,1,0:T(8,128)(2,1)S(1)} %collective-permute-done.24.refs_2_), channel_id=1, source_target_pairs={{1,0},{0,1},{3,2},{2,3},{5,4},{4,5},{7,6},{6,7},{9,8},{8,9},{11,10... | collective-permute-start | bytes 1474568 | tf_op jit(solution)/shard_map/ppermute | solution.py:391
  73.8 39.2 %copy-start.9 = (bf16[3,5,128,128]{3,2,1,0:T(8,128)(2,1)}, bf16[3,5,128,128]{3,2,1,0:T(8,128)(2,1)S(1)}, u32[]{:S(2)}) copy-start(bf16[3,5,128,128]{3,2,1,0:T(8,128)(2,1)S(1)} %collective-permute-done.25.refs_3_) | copy-start | bytes 1474564
  73.8 39.2 %collective-permute-start.29 = (bf16[3,5,128,128]{3,2,1,0:T(8,128)(2,1)S(1)}, bf16[3,5,128,128]{3,2,1,0:T(8,128)(2,1)}, u32[]{:S(2)}, u32[]{:S(2)}) collective-permute-start(bf16[3,5,128,128]{3,2,1,0:T(8,128)(2,1)S(1)} %collective-permute-done.25.refs_3_), channel_id=1, source_target_pairs={{1,0},{0,1},{3,2},{2,3},{5,4},{4,5},{7,6},{6,7},{9,8},{8,9},{11,10... | collective-permute-start | bytes 1474568 | tf_op jit(solution)/shard_map/ppermute | solution.py:391
  74.3 11.7 %collective-permute-start.3 = (bf16[2,5,128,128]{3,2,1,0:T(8,128)(2,1)S(1)}, bf16[2,5,128,128]{3,2,1,0:T(8,128)(2,1)}, u32[]{:S(2)}, u32[]{:S(2)}) collective-permute-start(bf16[2,5,128,128]{3,2,1,0:T(8,128)(2,1)S(1)} %slice.10.refs_0_), channel_id=1, source_target_pairs={{2,0},{4,2},{6,4},{3,1},{5,3},{7,5},{10,8},{12,10},{14,12},{11,9},... | collective-permute-start | bytes 983048 | tf_op jit(solution)/shard_map/ppermute | solution.py:370
  86.0 38.7 %collective-permute-start.1 = (bf16[2,5,128,128]{3,2,1,0:T(8,128)(2,1)}, bf16[2,5,128,128]{3,2,1,0:T(8,128)(2,1)}, u32[]{:S(2)}, u32[]{:S(2)}) collective-permute-start(bf16[2,5,128,128]{3,2,1,0:T(8,128)(2,1)} %collective-permute-done.refs_1_), channel_id=1, source_target_pairs={{0,2},{2,4},{4,6},{1,3},{3,5},{5,7},{8,10},{10,12},{12,14},{9,11},... | collective-permute-start | bytes 983048 | tf_op jit(solution)/shard_map/ppermute | solution.py:369
  90.2 22.9 %copy-start.10 = (bf16[3,5,128,128]{3,2,1,0:T(8,128)(2,1)}, bf16[3,5,128,128]{3,2,1,0:T(8,128)(2,1)S(1)}, u32[]{:S(2)}) copy-start(bf16[3,5,128,128]{3,2,1,0:T(8,128)(2,1)S(1)} %collective-permute-done.26.refs_0_) | copy-start | bytes 1474564
  90.2 36.7 %collective-permute-start.4 = (bf16[2,5,128,128]{3,2,1,0:T(8,128)(2,1)}, bf16[2,5,128,128]{3,2,1,0:T(8,128)(2,1)}, u32[]{:S(2)}, u32[]{:S(2)}) collective-permute-start(bf16[2,5,128,128]{3,2,1,0:T(8,128)(2,1)} %collective-permute-done.3.refs_4_), channel_id=1, source_target_pairs={{2,0},{4,2},{6,4},{3,1},{5,3},{7,5},{10,8},{12,10},{14,12},{11,9},... | collective-permute-start | bytes 983048 | tf_op jit(solution)/shard_map/ppermute | solution.py:370
  92.4 12.6 %all-to-all-start = ((s32[32,5,5]{2,1,0:T(8,128)}), s32[32,5,5]{2,1,0:T(8,128)S(1)}, u32[]{:S(2)}, u32[]{:S(2)}) async-start(s32[32,5,5]{2,1,0:T(8,128)} %broadcast_in_dim.2), calls=%async_computation | async-start | bytes 262144 | tf_op jit(solution)/shard_map/all_to_all | solution.py:357
  113.0 0.8 copy-start.11
  122.5 45.6 %collective-permute-start.30 = (s16[12,656,128]{2,1,0:T(8,128)(2,1)}, s16[12,656,128]{2,1,0:T(8,128)(2,1)S(1)}, u32[]{:S(2)}, u32[]{:S(2)}) collective-permute-start(s16[12,656,128]{2,1,0:T(8,128)(2,1)} %product.6), channel_id=1, source_target_pairs={{0,1},{1,0},{2,3},{3,2},{4,5},{5,4},{6,7},{7,6},{8,9},{9,8},{10,11... | collective-permute-start | bytes 6045704 | tf_op jit(solution)/shard_map/ppermute | solution.py:394
  124.7 9.7 %collective-permute-start.2 = (bf16[2,5,128,128]{3,2,1,0:T(8,128)(2,1)}, bf16[2,5,128,128]{3,2,1,0:T(8,128)(2,1)S(1)}, u32[]{:S(2)}, u32[]{:S(2)}) collective-permute-start(bf16[2,5,128,128]{3,2,1,0:T(8,128)(2,1)} %collective-permute-done.1.refs_2_), channel_id=1, source_target_pairs={{0,2},{2,4},{4,6},{1,3},{3,5},{5,7},{8,10},{10,12},{12,14},{9,11},... | collective-permute-start | bytes 983048 | tf_op jit(solution)/shard_map/ppermute | solution.py:369
  126.9 11.5 %collective-permute-start.5 = (bf16[2,5,128,128]{3,2,1,0:T(8,128)(2,1)}, bf16[2,5,128,128]{3,2,1,0:T(8,128)(2,1)S(1)}, u32[]{:S(2)}, u32[]{:S(2)}) collective-permute-start(bf16[2,5,128,128]{3,2,1,0:T(8,128)(2,1)} %collective-permute-done.4.refs_5_), channel_id=1, source_target_pairs={{2,0},{4,2},{6,4},{3,1},{5,3},{7,5},{10,8},{12,10},{14,12},{11,9},... | collective-permute-start | bytes 983048 | tf_op jit(solution)/shard_map/ppermute | solution.py:370
  134.4 4.0 %copy-start.21 = (bf16[2,5,128,128]{3,2,1,0:T(8,128)(2,1)}, bf16[2,5,128,128]{3,2,1,0:T(8,128)(2,1)S(1)}, u32[]{:S(2)}) copy-start(bf16[2,5,128,128]{3,2,1,0:T(8,128)(2,1)S(1)} %collective-permute-done.2.refs_3_) | copy-start | bytes 983044
  138.4 0.7 copy-start.22
  141.9 10.9 %collective-permute-start.6 = (bf16[2,5,128,128]{3,2,1,0:T(8,128)(2,1)}, bf16[2,5,128,128]{3,2,1,0:T(8,128)(2,1)S(1)}, u32[]{:S(2)}, u32[]{:S(2)}) collective-permute-start(bf16[2,5,128,128]{3,2,1,0:T(8,128)(2,1)} %get-tuple-element.30), channel_id=1, source_target_pairs={{0,8},{8,0},{16,24},{24,16},{1,9},{9,1},{17,25},{25,17},{2,10},{10... | collective-permute-start | bytes 983048 | tf_op jit(solution)/shard_map/ppermute | solution.py:380
  142.0 15.8 %collective-permute-start.7 = (bf16[2,5,128,128]{3,2,1,0:T(8,128)(2,1)}, bf16[2,5,128,128]{3,2,1,0:T(8,128)(2,1)S(1)}, u32[]{:S(2)}, u32[]{:S(2)}) collective-permute-start(bf16[2,5,128,128]{3,2,1,0:T(8,128)(2,1)} %get-tuple-element.31), channel_id=1, source_target_pairs={{0,16},{8,24},{16,0},{24,8},{1,17},{9,25},{17,1},{25,9},{2,18},{10... | collective-permute-start | bytes 983048 | tf_op jit(solution)/shard_map/ppermute | solution.py:380
  142.5 15.3 %collective-permute-start.8 = (bf16[2,5,128,128]{3,2,1,0:T(8,128)(2,1)}, bf16[2,5,128,128]{3,2,1,0:T(8,128)(2,1)S(1)}, u32[]{:S(2)}, u32[]{:S(2)}) collective-permute-start(bf16[2,5,128,128]{3,2,1,0:T(8,128)(2,1)} %get-tuple-element.32), channel_id=1, source_target_pairs={{0,24},{8,16},{16,8},{24,0},{1,25},{9,17},{17,9},{25,1},{2,26},{10... | collective-permute-start | bytes 983048 | tf_op jit(solution)/shard_map/ppermute | solution.py:380
  145.5 12.9 %collective-permute-start.9 = (bf16[2,5,128,128]{3,2,1,0:T(8,128)(2,1)}, bf16[2,5,128,128]{3,2,1,0:T(8,128)(2,1)S(1)}, u32[]{:S(2)}, u32[]{:S(2)}) collective-permute-start(bf16[2,5,128,128]{3,2,1,0:T(8,128)(2,1)} %get-tuple-element.29.refs_0_), channel_id=1, source_target_pairs={{1,0},{0,1},{3,2},{2,3},{5,4},{4,5},{7,6},{6,7},{9,8},{8,9},{11,10... | collective-permute-start | bytes 983048 | tf_op jit(solution)/shard_map/ppermute | solution.py:391
  152.8 0.8 copy-start.23
  153.6 4.8 %collective-permute-start.10 = (bf16[2,5,128,128]{3,2,1,0:T(8,128)(2,1)S(1)}, bf16[2,5,128,128]{3,2,1,0:T(8,128)(2,1)S(1)}, u32[]{:S(2)}, u32[]{:S(2)}) collective-permute-start(bf16[2,5,128,128]{3,2,1,0:T(8,128)(2,1)S(1)} %collective-permute-done.6.refs_1_), channel_id=1, source_target_pairs={{1,0},{0,1},{3,2},{2,3},{5,4},{4,5},{7,6},{6,7},{9,8},{8,9},{11,10... | collective-permute-start | bytes 983048 | tf_op jit(solution)/shard_map/ppermute | solution.py:391
  157.8 0.7 copy-start.24
  157.8 1.6 collective-permute-start.11
  157.8 1.6 copy-start.25
  157.9 2.1 collective-permute-start.12
  158.4 1.6 copy-start.26
  158.6 1.4 copy-start.27
  168.0 15.4 %collective-permute-start.13 = (s16[8,656,128]{2,1,0:T(8,128)(2,1)}, s16[8,656,128]{2,1,0:T(8,128)(2,1)S(1)}, u32[]{:S(2)}, u32[]{:S(2)}) collective-permute-start(s16[8,656,128]{2,1,0:T(8,128)(2,1)} %product.4), channel_id=1, source_target_pairs={{0,1},{1,0},{2,3},{3,2},{4,5},{5,4},{6,7},{7,6},{8,9},{9,8},{10,11... | collective-permute-start | bytes 4030472 | tf_op jit(solution)/shard_map/ppermute | solution.py:394
  168.1 1.3 copy-start
  179.1 16.5 %collective-permute-start.31 = (s16[3,656,128]{2,1,0:T(8,128)(2,1)}, s16[3,656,128]{2,1,0:T(8,128)(2,1)S(1)}, u32[]{:S(2)}, u32[]{:S(2)}) collective-permute-start(s16[3,656,128]{2,1,0:T(8,128)(2,1)} %get-tuple-element.42), channel_id=1, source_target_pairs={{0,8},{8,0},{16,24},{24,16},{1,9},{9,1},{17,25},{25,17},{2,10},{10... | collective-permute-start | bytes 1511432 | tf_op jit(solution)/shard_map/ppermute | solution.py:400
  181.8 25.4 %collective-permute-start.32 = (s16[3,656,128]{2,1,0:T(8,128)(2,1)}, s16[3,656,128]{2,1,0:T(8,128)(2,1)S(1)}, u32[]{:S(2)}, u32[]{:S(2)}) collective-permute-start(s16[3,656,128]{2,1,0:T(8,128)(2,1)} %get-tuple-element.43), channel_id=1, source_target_pairs={{0,16},{8,24},{16,0},{24,8},{1,17},{9,25},{17,1},{25,9},{2,18},{10... | collective-permute-start | bytes 1511432 | tf_op jit(solution)/shard_map/ppermute | solution.py:400
  182.9 14.0 %copy-start.31 = (s32[40]{0:T(128)S(1)}, s32[40]{0:T(128)}, u32[]{:S(2)}) copy-start(s32[40]{0:T(128)} %param.5) | copy-start | bytes 484
  182.9 24.3 %collective-permute-start.33 = (s16[3,656,128]{2,1,0:T(8,128)(2,1)}, s16[3,656,128]{2,1,0:T(8,128)(2,1)S(1)}, u32[]{:S(2)}, u32[]{:S(2)}) collective-permute-start(s16[3,656,128]{2,1,0:T(8,128)(2,1)} %get-tuple-element.44), channel_id=1, source_target_pairs={{0,24},{8,16},{16,8},{24,0},{1,25},{9,17},{17,9},{25,1},{2,26},{10... | collective-permute-start | bytes 1511432 | tf_op jit(solution)/shard_map/ppermute | solution.py:400
  183.4 1.1 copy-start.2
  192.8 19.7 %collective-permute-start.14 = (s16[2,656,128]{2,1,0:T(8,128)(2,1)}, s16[2,656,128]{2,1,0:T(8,128)(2,1)S(1)}, u32[]{:S(2)}, u32[]{:S(2)}) collective-permute-start(s16[2,656,128]{2,1,0:T(8,128)(2,1)} %get-tuple-element.34), channel_id=1, source_target_pairs={{0,8},{8,0},{16,24},{24,16},{1,9},{9,1},{17,25},{25,17},{2,10},{10... | collective-permute-start | bytes 1007624 | tf_op jit(solution)/shard_map/ppermute | solution.py:400
  194.5 26.6 %collective-permute-start.15 = (s16[2,656,128]{2,1,0:T(8,128)(2,1)}, s16[2,656,128]{2,1,0:T(8,128)(2,1)S(1)}, u32[]{:S(2)}, u32[]{:S(2)}) collective-permute-start(s16[2,656,128]{2,1,0:T(8,128)(2,1)} %get-tuple-element.35), channel_id=1, source_target_pairs={{0,16},{8,24},{16,0},{24,8},{1,17},{9,25},{17,1},{25,9},{2,18},{10... | collective-permute-start | bytes 1007624 | tf_op jit(solution)/shard_map/ppermute | solution.py:400
  195.6 11.6 %copy-start.4 = (s16[3,656,128]{2,1,0:T(8,128)(2,1)}, s16[3,656,128]{2,1,0:T(8,128)(2,1)S(1)}, u32[]{:S(2)}) copy-start(s16[3,656,128]{2,1,0:T(8,128)(2,1)S(1)} %collective-permute-done.31.refs_1_) | copy-start | bytes 1511428
  195.6 25.6 %collective-permute-start.16 = (s16[2,656,128]{2,1,0:T(8,128)(2,1)}, s16[2,656,128]{2,1,0:T(8,128)(2,1)S(1)}, u32[]{:S(2)}, u32[]{:S(2)}) collective-permute-start(s16[2,656,128]{2,1,0:T(8,128)(2,1)} %get-tuple-element.36), channel_id=1, source_target_pairs={{0,24},{8,16},{16,8},{24,0},{1,25},{9,17},{17,9},{25,1},{2,26},{10... | collective-permute-start | bytes 1007624 | tf_op jit(solution)/shard_map/ppermute | solution.py:400
  207.2 0.8 copy-start.5
  207.2 1.0 copy-start.6
  212.5 8.6 %copy-start.18 = (s16[2,656,128]{2,1,0:T(8,128)(2,1)}, s16[2,656,128]{2,1,0:T(8,128)(2,1)S(1)}, u32[]{:S(2)}) copy-start(s16[2,656,128]{2,1,0:T(8,128)(2,1)S(1)} %collective-permute-done.14.refs_1_) | copy-start | bytes 1007620
  221.2 0.9 copy-start.20
  (3 other events, 2.2 us)

commit v2 on v1

v2 whole, which is shorter than its diff:
```python
import jax
import jax.numpy as jnp
from jax import lax
from jax.experimental import pallas as pl
from jax.experimental.pallas import tpu as pltpu
from jax.sharding import PartitionSpec as P


PARTS = (2, 2, 1)
TOP = 32767.0
MANT = 8192.0
HERE = pl.BlockSpec(memory_space=pltpu.HBM)
SCALARS = pl.BlockSpec(memory_space=pltpu.SMEM)
NEAR = pl.BlockSpec(memory_space=pltpu.VMEM)
VMEM_BYTES = 8 << 20


def chunks_of(count):
    total = sum(PARTS)
    edges = [round(count * sum(PARTS[:i]) / total) for i in range(len(PARTS) + 1)]
    return [(a, b - a) for a, b in zip(edges[:-1], edges[1:]) if b > a]


def code_rows(count, size):
    return count * size + -(-2 * count // 16) * 16


def encode(out_ref, blocks):
    size, count = blocks[0].shape[0], len(blocks)
    top = jnp.concatenate([jnp.max(jnp.abs(x), axis=0, keepdims=True) for x in blocks], axis=0)
    top = jnp.maximum(top, 1e-30)
    e = jnp.floor(jnp.log2(top))
    mant = jnp.ceil(top * jnp.exp2(-e) * MANT) + 1.0
    inv = (TOP * MANT) / (mant * jnp.exp2(e))
    for m, x in enumerate(blocks):
        q = jnp.round(x * inv[m : m + 1])
        out_ref[pl.ds(m * size, size), :] = q.astype(jnp.int32).astype(jnp.int16)
    pad = out_ref.shape[0] - count * size - 2 * count
    codes = jnp.concatenate([e, mant, jnp.zeros((pad, size), jnp.float32)], axis=0)
    out_ref[pl.ds(count * size, 2 * count + pad), :] = codes.astype(jnp.int32).astype(jnp.int16)


def scales(ref, count, size):
    codes = ref[count * size :, :].astype(jnp.int32).astype(jnp.float32)
    exps, mants = codes[:count], codes[count : 2 * count]
    return mants * jnp.exp2(exps) * (1.0 / (TOP * MANT))


def decode(ref, scale, m, size):
    q = ref[pl.ds(m * size, size), :].astype(jnp.int32).astype(jnp.float32)
    return q * scale[m : m + 1, :]


def record_size(terms, slots):
    return 1 + 2 * terms + terms * slots


def make_tables(where, every, pattern, sizes, chunks):
    parts, panels, depths, count, slots, rows_here, panel_cols = sizes
    per_part = panels // parts
    terms = per_part * slots
    total, record = parts * depths * count, record_size(terms, slots)

    def kernel(where_ref, every_ref, pattern_ref, out_ref):
        row, depth, z = where_ref[0], where_ref[1], where_ref[2]
        base = 0
        for s in range(depths):
            d = lax.rem(depth + s, depths)
            for first, n in chunks:
                def one(g, carry, base=base, d=d, first=first, n=n):
                    t, i = lax.div(g, n), lax.rem(g, n)
                    p0 = row ^ t

                    def columns_at(q):
                        return (((p0 * panels + q) * depths + d) * count + first + i) * slots

                    at = (base + g) * record
                    target = [every_ref[columns_at(z) + m] for m in range(slots)]
                    live = jnp.int32(0)
                    for l in range(terms):
                        j, m = divmod(l, slots)
                        column = every_ref[columns_at(row * per_part + j) + m]
                        k = column + j * panel_cols - depth * rows_here
                        inside = jnp.logical_and(k >= 0, k < rows_here)

                        @pl.when(inside)
                        def _(k=k, l=l, live=live):
                            out_ref[at + 1 + live] = l
                            out_ref[at + 1 + terms + live] = k
                            mine = [pattern_ref[k * slots + x] for x in range(slots)]
                            for m, want in enumerate(target):
                                found = jnp.int32(0)
                                for x in range(1, slots):
                                    found = jnp.where(mine[x] == want, x, found)
                                out_ref[at + 1 + 2 * terms + live * slots + m] = found

                        live = live + inside.astype(jnp.int32)
                    out_ref[at] = live
                    return carry

                lax.fori_loop(0, parts * n, one, 0)
                base += parts * n

    return pl.pallas_call(
        kernel,
        out_shape=jax.ShapeDtypeStruct((total * record,), jnp.int32),
        in_specs=[SCALARS] * 3,
        out_specs=SCALARS,
        compiler_params=pltpu.CompilerParams(vmem_limit_bytes=VMEM_BYTES),
        name="tables",
    )(where, every, pattern)


def bring(values):
    rows = values.shape[0]
    cuts = [rows * i // 4 for i in range(5)]

    def kernel(values_ref, out_ref, sem):
        copies = []
        for i, (a, b) in enumerate(zip(cuts[:-1], cuts[1:])):
            part = pl.ds(a, b - a)
            copies.append(pltpu.make_async_copy(values_ref.at[part], out_ref.at[part], sem.at[i]))
            copies[-1].start()
        for copy in copies:
            copy.wait()

    return pl.pallas_call(
        kernel,
        out_shape=jax.ShapeDtypeStruct(values.shape, values.dtype),
        in_specs=[HERE],
        out_specs=NEAR,
        scratch_shapes=[pltpu.SemaphoreType.DMA((4,))],
        compiler_params=pltpu.CompilerParams(vmem_limit_bytes=4 * VMEM_BYTES),
        name="bring",
    )(values)


def gather_panels(sources, where, parts, per_part):
    n, slots, size, _ = sources[0].shape
    ring = len(sources)

    def kernel(where_ref, *refs):
        outs, sem = refs[len(sources) : len(sources) + parts], refs[-1]
        row, z = where_ref[0], where_ref[2]
        places = [(t, j) for t in range(parts - 1, -1, -1) for j in range(per_part)]

        def copy(k, t, j):
            to = outs[t].at[:, pl.ds(j * slots, slots)]
            return pltpu.make_async_copy(refs[k], to, sem.at[t * per_part + j])

        for t, j in places:
            q = (row ^ t) * per_part + j
            for k in range(ring):
                @pl.when(q == lax.rem(z + ring - k, ring))
                def _(t=t, j=j, k=k):
                    copy(k, t, j).start()
        for t, j in places:
            copy(0, t, j).wait()

    panels = parts * per_part
    out = jax.ShapeDtypeStruct((n, per_part * slots, size, size), sources[0].dtype)
    return pl.pallas_call(
        kernel,
        out_shape=[out] * parts,
        in_specs=[SCALARS] + [NEAR] * len(sources),
        out_specs=[NEAR] * parts,
        scratch_shapes=[pltpu.SemaphoreType.DMA((panels,))],
        compiler_params=pltpu.CompilerParams(vmem_limit_bytes=VMEM_BYTES),
        cost_estimate=pl.CostEstimate(
            flops=0, bytes_accessed=4 * panels * n * slots * size * size, transcendentals=0
        ),
        name="gather_panels",
    )(where, *sources)


def product(lefts, values, table, base, extra=None, joined=False):
    parts = len(lefts)
    n, terms, size, _ = lefts[0].shape
    slots = values.shape[1]
    height = code_rows(slots, size)
    rows, record = parts * n, record_size(terms, slots)

    def kernel(table_ref, values_ref, *refs):
        left_refs, rest = refs[:parts], refs[parts:]
        if extra is not None:
            extra_ref, rest = rest[0], rest[1:]
        outs, acc = rest[:-1], rest[-1]

        for t in range(parts):
            def one(i, carry, t=t):
                g = t * n + i
                at = (base + g) * record
                live = table_ref[at]

                def dot_of(low, number):
                    left, right = [], []
                    for l in range(low, low + number):
                        k = table_ref[at + 1 + terms + l]
                        slot = at + 1 + 2 * terms + l * slots
                        left.append(left_refs[t][i, table_ref[at + 1 + l]])
                        right.append(
                            jnp.concatenate(
                                [values_ref[k, table_ref[slot + m]] for m in range(slots)], axis=1
                            )
                        )
                    return jnp.dot(
                        jnp.concatenate(left, axis=1),
                        jnp.concatenate(right, axis=0),
                        preferred_element_type=jnp.float32,
                    )

                @pl.when(live == 0)
                def _():
                    acc[...] = jnp.zeros_like(acc)

                for low in range(0, terms, 2):
                    for number in (1, 2):
                        if low + number > terms:
                            continue

                        @pl.when(live == low + 1 if number == 1 else live >= low + 2)
                        def _(low=low, number=number):
                            if low == 0:
                                acc[...] = dot_of(low, number)
                            else:
                                acc[...] += dot_of(low, number)

                blocks = [acc[:, m * size : (m + 1) * size] for m in range(slots)]
                if extra is not None:
                    scale = scales(extra_ref.at[g], slots, size)
                    blocks = [b + decode(extra_ref.at[g], scale, m, size) for m, b in enumerate(blocks)]
                encode(outs[0].at[g] if joined else outs[t].at[i], blocks)
                return carry

            lax.fori_loop(0, n, one, 0)

    if joined:
        out_shape = [jax.ShapeDtypeStruct((rows, height, size), jnp.int16)]
    else:
        out_shape = [jax.ShapeDtypeStruct((n, height, size), jnp.int16)] * parts
    operands = [table, values, *lefts] + ([] if extra is None else [extra])
    out = pl.pallas_call(
        kernel,
        out_shape=out_shape,
        in_specs=[SCALARS] + [NEAR] * (len(operands) - 1),
        out_specs=[NEAR] * len(out_shape),
        scratch_shapes=[pltpu.VMEM((size, slots * size), jnp.float32)],
        compiler_params=pltpu.CompilerParams(vmem_limit_bytes=VMEM_BYTES),
        cost_estimate=pl.CostEstimate(
            flops=2 * rows * terms * slots * size**3,
            bytes_accessed=rows * terms * (slots + 1) * size * size * 2,
            transcendentals=0,
        ),
        name="product",
    )(*operands)
    return out[0] if joined else out


def finish(received, own, flags, where, depths, first, count, before=None):
    parts = len(received)
    n, _, size = received[0].shape
    slots = own.shape[1]

    def kernel(flag_ref, where_ref, own_ref, *refs):
        got, out_ref = refs[:parts], refs[-1]
        i = pl.program_id(0)
        flag = flag_ref[(where_ref[0] * depths + where_ref[1]) * count + first + i]
        scale = [scales(g.at[i], slots, size) for g in got]
        for m in range(slots):
            total = decode(got[0].at[i], scale[0], m, size)
            for p in range(1, parts):
                total = total + decode(got[p].at[i], scale[p], m, size)
            mine = own_ref[i, m].astype(jnp.float32)
            out_ref[0, m] = jnp.where(flag == 1, total, 2.0 * mine - total).astype(out_ref.dtype)

    in_specs = [NEAR] * (parts + 1)
    operands = [flags, where, own, *received]
    if before is not None:
        in_specs.append(HERE)
        operands.append(before)
    return pl.pallas_call(
        kernel,
        out_shape=jax.ShapeDtypeStruct((count, slots, size, size), own.dtype),
        grid_spec=pltpu.PrefetchScalarGridSpec(
            num_scalar_prefetch=2,
            grid=(n,),
            in_specs=in_specs,
            out_specs=pl.BlockSpec((1, slots, size, size), lambda i, *_: (first + i, 0, 0, 0)),
        ),
        compiler_params=pltpu.CompilerParams(vmem_limit_bytes=VMEM_BYTES),
        input_output_aliases={} if before is None else {len(operands) - 1: 0},
        name="finish",
    )(*operands)


def inner(values, pattern, branch_flag):
    parts, depths, panels = lax.axis_size("row"), lax.axis_size("depth"), lax.axis_size("col")
    row, depth, z = lax.axis_index("row"), lax.axis_index("depth"), lax.axis_index("col")
    rows_here, slots, _, _ = values.shape
    count = branch_flag.shape[0] // (parts * depths)
    stride = rows_here // count
    panel_cols = rows_here * parts * depths // panels
    per_part = panels // parts
    chunks = chunks_of(count)
    across = [[(i, i ^ t) for i in range(parts)] for t in range(parts)]
    ring = [(i, (i + 1) % panels) for i in range(panels)]
    where = jnp.stack([row, depth, z]).astype(jnp.int32)

    own = [values[a * stride : (a + n - 1) * stride + 1 : stride] for a, n in chunks]
    every = lax.all_to_all(
        jnp.broadcast_to(pattern[None, ::stride], (parts * panels * depths, count, slots)),
        ("row", "col", "depth"), split_axis=0, concat_axis=0, tiled=True,
    )
    tables = make_tables(
        where, every.reshape(-1), pattern.reshape(-1),
        (parts, panels, depths, count, slots, rows_here, panel_cols), chunks,
    )
    near = bring(values)

    held = [[x] for x in own]
    for _ in range(panels - 1):
        for c in range(len(chunks)):
            held[c].append(lax.ppermute(held[c][-1], "col", ring))

    out = None
    lefts = []
    for c in range(len(chunks)):
        picked = gather_panels(held[c], where, parts, per_part)
        got = [picked[0]]
        for t in range(1, parts):
            got.append(lax.ppermute(picked[t], "row", across[t]))
        lefts.append(got)

    base = [sum(parts * m for _, m in chunks[:c]) for c in range(len(chunks))]
    per_depth = parts * count
    for c, (first, n) in enumerate(chunks):
        extra = None
        for s in range(1, depths):
            here = []
            for t in range(parts):
                here.append(
                    lax.ppermute(lefts[c][t], "depth", [((i + s) % depths, i) for i in range(depths)])
                )
            part = product(here, near, tables, s * per_depth + base[c], joined=True)
            back = lax.ppermute(part, "depth", [(i, (i + s) % depths) for i in range(depths)])
            assert extra is None
            extra = back
        mine = product(lefts[c], near, tables, base[c], extra=extra)
        summed = [mine[0]]
        for t in range(1, parts):
            summed.append(lax.ppermute(mine[t], "row", across[t]))
        out = finish(summed, own[c], branch_flag, where, depths, first, count, before=out)
    return out


def solution(mesh):
    in_specs = (P(("row", "depth"), "col", None, None), P(("row", "depth"), "col"), P())
    out_specs = P(("row", "depth"), "col", None, None)
    return jax.shard_map(inner, mesh=mesh, in_specs=in_specs, out_specs=out_specs, check_vma=False)
```

time: 226 us -> 197 us (0.87)
  starting transfers between devices: 55.4 us -> 37 us
  Pallas kernels: 54.2 us -> 43.1 us
  local copies, waits for them, and re-layouts: 13.6 us -> 19.8 us
  waiting for transfers between devices: 101 us -> 96.8 us
    ppermute x12 -> x9, starting transfers between devices: 32.1 us -> 6.44 us  [inner(): held[c].append(lax.ppermute(held[c][-1], 'col', ring))]
    pallas_call x7 -> x11, Pallas kernels: 46.7 us -> 38.3 us  [the longest x6 22 us: product(): pl.pallas_call(kernel, out_shape=out_shape, in_specs=[SCALARS] + [NEAR] *...]
    unnamed x65 -> x23, local copies, waits for them, and re-layouts: 8.62 us -> 16.5 us
    all_to_all x1, waiting for transfers between devices: 7.28 us -> 0.01 us  [inner(): lax.all_to_all(jnp.broadcast_to(pattern[None, ::stride], (parts * panels...]
    ppermute x12 -> x9, waiting for transfers between devices: 48.9 us -> 54.2 us  [inner(): held[c].append(lax.ppermute(held[c][-1], 'col', ring))]
    ppermute x6 -> x9, starting transfers between devices: 7.1 us -> 11.9 us  [inner(): got.append(lax.ppermute(picked[t], 'row', across[t]))]
    ppermute x6 -> x9, starting transfers between devices: 8.44 us -> 11.8 us  [inner(): summed.append(lax.ppermute(mine[t], 'row', across[t]))]
    pallas_call x2 -> x3, Pallas kernels: 7.44 us -> 4.8 us  [finish(): pl.pallas_call(kernel, out_shape=jax.ShapeDtypeStruct((count, slots, size...]
  transfers between devices with their start and end apart: 35 -> 43, of which waited for: 16 -> 27; matrix products, arithmetic and copies ran while one was open for 2% -> 1% of each run, Pallas kernels for 21% -> 21%
where the time goes in v2:
time: 197 us
  waiting for transfers between devices  96.8 us (49%)
  Pallas kernels  43.1 us (22%)
  starting transfers between devices  37 us (19%)
  local copies, waits for them, and re-layouts  19.8 us (10%)
    ppermute x9, waiting for transfers between devices, inner(): held[c].append(lax.ppermute(held[c][-1], 'col', ring))  54.2 us
    ppermute x9, waiting for transfers between devices, inner(): got.append(lax.ppermute(picked[t], 'row', across[t]))  23.4 us
    pallas_call x6, Pallas kernels, product(): pl.pallas_call(kernel, out_shape=out_shape, in_specs=[SCALARS] + [NEAR] *...  22 us
    ppermute x9, waiting for transfers between devices, inner(): summed.append(lax.ppermute(mine[t], 'row', across[t]))  18.1 us
    unnamed x23, local copies, waits for them, and re-layouts  16.5 us
    ppermute x9, starting transfers between devices, inner(): got.append(lax.ppermute(picked[t], 'row', across[t]))  11.9 us
    ppermute x9, starting transfers between devices, inner(): summed.append(lax.ppermute(mine[t], 'row', across[t]))  11.8 us
    pallas_call x1, Pallas kernels, make_tables(): pl.pallas_call(kernel, out_shape=jax.ShapeDtypeStruct((total * record,),...  6.85 us
  transfers between devices with their start and end apart: 43, of which 27 were waited for; matrix products, arithmetic and copies ran while one was open for 1% of the time, Pallas kernels for 21%

profile of v2, /device:TPU:0, one launch (start us, length us, event | category | flops | bytes accessed | tf_op | source)
XLA Modules:
  0.0 197.0 jit_solution(17477238953950007226)
XLA Ops:
  0.0 1.1 fusion
  1.1 3.1 %collective-permute-start.28 = (bf16[2,5,128,128]{3,2,1,0:T(8,128)(2,1)S(1)}, bf16[2,5,128,128]{3,2,1,0:T(8,128)(2,1)S(1)}, u32[]{:S(2)}, u32[]{:S(2)}) collective-permute-start(bf16[2,5,128,128]{3,2,1,0:T(8,128)(2,1)S(1)} %get-tuple-element.53.refs_0_.own_ref), channel_id=1, source_target_pairs={{0,2},{2,4},{4,6},{6,0},{1,3},{3,5},{5,7},{7,1},{8,10},{10,12},{12... | collective-permute-start | bytes 983048 | tf_op jit(solution)/shard_map/ppermute | solution.py:323
  4.2 1.6 collective-permute-start.14
  5.8 9.0 %collective-permute-done.28.refs_1_ = bf16[2,5,128,128]{3,2,1,0:T(8,128)(2,1)S(1)} collective-permute-done((bf16[2,5,128,128]{3,2,1,0:T(8,128)(2,1)S(1)}, bf16[2,5,128,128]{3,2,1,0:T(8,128)(2,1)S(1)}, u32[]{:S(2)}, u32[]{:S(2)}) %collective-permute-start.28) | collective-permute-done | bytes 327712 | tf_op jit(solution)/shard_map/ppermute | solution.py:323
  14.8 7.0 %collective-permute-done.14.refs_1_ = bf16[2,5,128,128]{3,2,1,0:T(8,128)(2,1)S(1)} collective-permute-done((bf16[2,5,128,128]{3,2,1,0:T(8,128)(2,1)S(1)}, bf16[2,5,128,128]{3,2,1,0:T(8,128)(2,1)S(1)}, u32[]{:S(2)}, u32[]{:S(2)}) %collective-permute-start.14) | collective-permute-done | bytes 327712 | tf_op jit(solution)/shard_map/ppermute | solution.py:323
  21.9 7.0 %collective-permute-done.29.refs_2_ = bf16[2,5,128,128]{3,2,1,0:T(8,128)(2,1)S(1)} collective-permute-done((bf16[2,5,128,128]{3,2,1,0:T(8,128)(2,1)S(1)}, bf16[2,5,128,128]{3,2,1,0:T(8,128)(2,1)S(1)}, u32[]{:S(2)}, u32[]{:S(2)}) %collective-permute-start.29) | collective-permute-done | bytes 327712 | tf_op jit(solution)/shard_map/ppermute | solution.py:323
  28.9 7.0 %collective-permute-done.15.refs_2_ = bf16[2,5,128,128]{3,2,1,0:T(8,128)(2,1)S(1)} collective-permute-done((bf16[2,5,128,128]{3,2,1,0:T(8,128)(2,1)S(1)}, bf16[2,5,128,128]{3,2,1,0:T(8,128)(2,1)S(1)}, u32[]{:S(2)}, u32[]{:S(2)}) %collective-permute-start.15) | collective-permute-done | bytes 327712 | tf_op jit(solution)/shard_map/ppermute | solution.py:323
  36.0 6.9 %collective-permute-done.30.refs_3_ = bf16[2,5,128,128]{3,2,1,0:T(8,128)(2,1)S(1)} collective-permute-done((bf16[2,5,128,128]{3,2,1,0:T(8,128)(2,1)S(1)}, bf16[2,5,128,128]{3,2,1,0:T(8,128)(2,1)S(1)}, u32[]{:S(2)}, u32[]{:S(2)}) %collective-permute-start.30) | collective-permute-done | bytes 327712 | tf_op jit(solution)/shard_map/ppermute | solution.py:323
  42.9 1.1 gather_panels.5
  44.0 1.8 collective-permute-start.31
  45.8 1.5 collective-permute-start.32
  47.6 1.5 collective-permute-done.16.refs_3_
  49.1 1.1 gather_panels.4
  50.2 1.6 collective-permute-start.17
  51.7 2.9 %collective-permute-done.31.refs_1_ = bf16[2,5,128,128]{3,2,1,0:T(8,128)(2,1)S(1)} collective-permute-done((bf16[2,5,128,128]{3,2,1,0:T(8,128)(2,1)S(1)}, bf16[2,5,128,128]{3,2,1,0:T(8,128)(2,1)S(1)}, u32[]{:S(2)}, u32[]{:S(2)}) %collective-permute-start.31) | collective-permute-done | bytes 327712 | tf_op jit(solution)/shard_map/ppermute | solution.py:331
  54.7 1.7 collective-permute-start.18
  56.4 4.1 %collective-permute-done.32.refs_2_ = bf16[2,5,128,128]{3,2,1,0:T(8,128)(2,1)S(1)} collective-permute-done((bf16[2,5,128,128]{3,2,1,0:T(8,128)(2,1)S(1)}, bf16[2,5,128,128]{3,2,1,0:T(8,128)(2,1)S(1)}, u32[]{:S(2)}, u32[]{:S(2)}) %collective-permute-start.32) | collective-permute-done | bytes 327712 | tf_op jit(solution)/shard_map/ppermute | solution.py:331
  60.5 1.5 collective-permute-start.19
  62.0 0.9 collective-permute-done.33.refs_3_
  64.1 4.6 %collective-permute-done.17.refs_1_ = bf16[2,5,128,128]{3,2,1,0:T(8,128)(2,1)S(1)} collective-permute-done((bf16[2,5,128,128]{3,2,1,0:T(8,128)(2,1)S(1)}, bf16[2,5,128,128]{3,2,1,0:T(8,128)(2,1)S(1)}, u32[]{:S(2)}, u32[]{:S(2)}) %collective-permute-start.17) | collective-permute-done | bytes 327712 | tf_op jit(solution)/shard_map/ppermute | solution.py:331
  68.8 5.4 %collective-permute-done.18.refs_2_ = bf16[2,5,128,128]{3,2,1,0:T(8,128)(2,1)S(1)} collective-permute-done((bf16[2,5,128,128]{3,2,1,0:T(8,128)(2,1)S(1)}, bf16[2,5,128,128]{3,2,1,0:T(8,128)(2,1)S(1)}, u32[]{:S(2)}, u32[]{:S(2)}) %collective-permute-start.18) | collective-permute-done | bytes 327712 | tf_op jit(solution)/shard_map/ppermute | solution.py:331
  77.5 3.0 %all-to-all-start = ((s32[32,5,5]{2,1,0:T(8,128)}), s32[32,5,5]{2,1,0:T(8,128)S(1)}, u32[]{:S(2)}, u32[]{:S(2)}) async-start(s32[32,5,5]{2,1,0:T(8,128)} %broadcast_in_dim.2), calls=%async_computation | async-start | bytes 262144 | tf_op jit(solution)/shard_map/all_to_all | solution.py:310
  80.6 5.8 %bring.1.values_ref = bf16[100,5,128,128]{3,2,1,0:T(8,128)(2,1)S(1)} custom-call(bf16[100,5,128,128]{3,2,1,0:T(8,128)(2,1)} %values_ref.1), custom_call_target="tpu_custom_call" | custom-call | tf_op jit(solution)/shard_map/bring/pallas_call | solution.py:127
  86.4 5.6 %copy-done = bf16[100,5,128,128]{3,2,1,0:T(8,128)(2,1)} copy-done((bf16[100,5,128,128]{3,2,1,0:T(8,128)(2,1)}, bf16[100,5,128,128]{3,2,1,0:T(8,128)(2,1)S(1)}, u32[]{:S(2)}) %copy-start) | copy-done | bytes 16384024
  92.4 6.8 %tables.1.table_ref = s32[1440]{0:T(1024)S(1)} custom-call(s32[3]{0:T(128)S(1)} %pad_add_fusion.where_ref, s32[800]{0:T(1024)S(1)} %reshape.7.every_ref, s32[500]{0:T(512)S(1)} %reshape.8.pattern_ref), custom_call_target="tpu_custom_call" | custom-call | tf_op jit(solution)/shard_map/tables/pallas_call | solution.py:104
  99.3 5.6 %copy-done.1 = bf16[100,5,128,128]{3,2,1,0:T(8,128)(2,1)S(1)} copy-done((bf16[100,5,128,128]{3,2,1,0:T(8,128)(2,1)S(1)}, bf16[100,5,128,128]{3,2,1,0:T(8,128)(2,1)}, u32[]{:S(2)}) %copy-start.1) | copy-done | bytes 16384024
  105.0 1.0 copy-done.4
  105.9 1.0 copy-done.6
  106.9 1.0 copy-done.8
  107.9 4.2 %product.10 = s16[8,656,128]{2,1,0:T(8,128)(2,1)S(1)} custom-call(s32[1440]{0:T(1024)S(1)} %tables.1.table_ref, bf16[100,5,128,128]{3,2,1,0:T(8,128)(2,1)S(1)} %copy-done.1, bf16[2,5,128,128]{3,2,1,0:T(8,128)(2,1)S(1)} %copy-done.4, bf16[2,5,128,128]{3,2,1,0:T(8,128)(2,1)S(1)} %copy-done.6, bf16[2,5,128,128]{3,2,1,0:T(8,128)(2,1)S(1)} %copy-done.8, ...), custom_call_target="tpu_custom_call" | custom-call | flops 838860800 | bytes 7864320 | tf_op jit(solution)/shard_map/product/pallas_call | solution.py:242
  112.1 1.3 collective-permute-start.38
  113.4 0.9 slice.13.refs_0_.own_ref
  114.4 1.7 collective-permute-start
  116.1 4.7 %product.8 = s16[8,656,128]{2,1,0:T(8,128)(2,1)S(1)} custom-call(s32[1440]{0:T(1024)S(1)} %tables.1.table_ref, bf16[100,5,128,128]{3,2,1,0:T(8,128)(2,1)S(1)} %copy-done.2, bf16[2,5,128,128]{3,2,1,0:T(8,128)(2,1)} %collective-permute-done.20.refs_0_, bf16[2,5,128,128]{3,2,1,0:T(8,128)(2,1)} %collective-permute-done.21.refs_1_, ...), custom_call_target="tpu_custom_call" | custom-call | flops 838860800 | bytes 7864320 | tf_op jit(solution)/shard_map/product/pallas_call | solution.py:242
  120.9 1.5 collective-permute-done.refs_1_
  122.4 7.1 %collective-permute-done.1.refs_2_ = bf16[1,5,128,128]{3,2,1,0:T(8,128)(2,1)S(1)} collective-permute-done((bf16[1,5,128,128]{3,2,1,0:T(8,128)(2,1)S(1)}, bf16[1,5,128,128]{3,2,1,0:T(8,128)(2,1)S(1)}, u32[]{:S(2)}, u32[]{:S(2)}) %collective-permute-start.1) | collective-permute-done | bytes 163872 | tf_op jit(solution)/shard_map/ppermute | solution.py:323
  129.5 7.1 %collective-permute-done.2.refs_3_ = bf16[1,5,128,128]{3,2,1,0:T(8,128)(2,1)S(1)} collective-permute-done((bf16[1,5,128,128]{3,2,1,0:T(8,128)(2,1)S(1)}, bf16[1,5,128,128]{3,2,1,0:T(8,128)(2,1)S(1)}, u32[]{:S(2)}, u32[]{:S(2)}) %collective-permute-start.2) | collective-permute-done | bytes 163872 | tf_op jit(solution)/shard_map/ppermute | solution.py:323
  136.6 1.5 gather_panels.3
  138.1 1.2 collective-permute-start.3
  139.3 1.5 collective-permute-start.4
  141.6 2.0 %collective-permute-done.3.refs_1_ = bf16[1,5,128,128]{3,2,1,0:T(8,128)(2,1)S(1)} collective-permute-done((bf16[1,5,128,128]{3,2,1,0:T(8,128)(2,1)S(1)}, bf16[1,5,128,128]{3,2,1,0:T(8,128)(2,1)S(1)}, u32[]{:S(2)}, u32[]{:S(2)}) %collective-permute-start.3) | collective-permute-done | bytes 163872 | tf_op jit(solution)/shard_map/ppermute | solution.py:331
  143.7 1.8 collective-permute-done.4.refs_2_
  145.5 1.6 collective-permute-done.5.refs_3_
  147.6 0.9 collective-permute-done.8.refs_2_
  148.7 2.4 %product.6 = s16[4,656,128]{2,1,0:T(8,128)(2,1)S(1)} custom-call(s32[1440]{0:T(1024)S(1)} %tables.1.table_ref, bf16[100,5,128,128]{3,2,1,0:T(8,128)(2,1)S(1)} %copy-done.2, bf16[1,5,128,128]{3,2,1,0:T(8,128)(2,1)S(1)} %collective-permute-done.6.refs_0_, bf16[1,5,128,128]{3,2,1,0:T(8,128)(2,1)S(1)} %collective-permute-done.7.refs_1_, ...), custom_call_target="tpu_custom_call" | custom-call | flops 419430400 | bytes 3932160 | tf_op jit(solution)/shard_map/product/pallas_call | solution.py:242
  151.6 3.8 %product.11 = (s16[2,656,128]{2,1,0:T(8,128)(2,1)S(1)}, s16[2,656,128]{2,1,0:T(8,128)(2,1)S(1)}, s16[2,656,128]{2,1,0:T(8,128)(2,1)S(1)}, s16[2,656,128]{2,1,0:T(8,128)(2,1)S(1)}) custom-call(s32[1440]{0:T(1024)S(1)} %tables.1.table_ref, bf16[100,5,128,128]{3,2,1,0:T(8,128)(2,1)S(1)} %copy-done.2, bf16[2,5,128,128]{3,2,1,0:T(8,128)(2,1)S(1)} %get-tuple-element.45.refs_0_, ...), custom_call_target="tpu_custom_call" | custom-call | flops 838860800 | bytes 7864320 | tf_op jit(solution)/shard_map/product/pallas_call | solution.py:242
  155.4 1.3 collective-permute-start.39
  157.5 1.5 collective-permute-start.41
  159.0 4.4 %product.9 = (s16[2,656,128]{2,1,0:T(8,128)(2,1)S(1)}, s16[2,656,128]{2,1,0:T(8,128)(2,1)S(1)}, s16[2,656,128]{2,1,0:T(8,128)(2,1)S(1)}, s16[2,656,128]{2,1,0:T(8,128)(2,1)S(1)}) custom-call(s32[1440]{0:T(1024)S(1)} %tables.1.table_ref, bf16[100,5,128,128]{3,2,1,0:T(8,128)(2,1)S(1)} %copy-done.2, bf16[2,5,128,128]{3,2,1,0:T(8,128)(2,1)S(1)} %get-tuple-element.37.refs_0_, ...), custom_call_target="tpu_custom_call" | custom-call | flops 838860800 | bytes 7864320 | tf_op jit(solution)/shard_map/product/pallas_call | solution.py:242
  163.4 1.8 collective-permute-start.25
  166.1 1.6 collective-permute-start.27
  167.7 2.5 %product.7 = (s16[1,656,128]{2,1,0:T(8,128)(2,1)S(1)}, s16[1,656,128]{2,1,0:T(8,128)(2,1)S(1)}, s16[1,656,128]{2,1,0:T(8,128)(2,1)S(1)}, s16[1,656,128]{2,1,0:T(8,128)(2,1)S(1)}) custom-call(s32[1440]{0:T(1024)S(1)} %tables.1.table_ref, bf16[100,5,128,128]{3,2,1,0:T(8,128)(2,1)S(1)} %copy-done.2, bf16[1,5,128,128]{3,2,1,0:T(8,128)(2,1)S(1)} %get-tuple-element.29.refs_0_, ...), custom_call_target="tpu_custom_call" | custom-call | flops 419430400 | bytes 3932160 | tf_op jit(solution)/shard_map/product/pallas_call | solution.py:242
  170.2 3.5 %collective-permute-done.40.refs_2_ = s16[2,656,128]{2,1,0:T(8,128)(2,1)S(1)} collective-permute-done((s16[2,656,128]{2,1,0:T(8,128)(2,1)S(1)}, s16[2,656,128]{2,1,0:T(8,128)(2,1)S(1)}, u32[]{:S(2)}, u32[]{:S(2)}) %collective-permute-start.40) | collective-permute-done | bytes 335904 | tf_op jit(solution)/shard_map/ppermute | solution.py:351
  173.7 1.7 collective-permute-start.11
  175.5 1.0 collective-permute-start.12
  176.5 4.1 %collective-permute-done.25.refs_1_ = s16[2,656,128]{2,1,0:T(8,128)(2,1)S(1)} collective-permute-done((s16[2,656,128]{2,1,0:T(8,128)(2,1)S(1)}, s16[2,656,128]{2,1,0:T(8,128)(2,1)S(1)}, u32[]{:S(2)}, u32[]{:S(2)}) %collective-permute-start.25) | collective-permute-done | bytes 335904 | tf_op jit(solution)/shard_map/ppermute | solution.py:351
  180.5 1.6 collective-permute-start.13
  182.1 1.7 finish.3.refs_4_
  183.8 4.3 %collective-permute-done.26.refs_2_ = s16[2,656,128]{2,1,0:T(8,128)(2,1)S(1)} collective-permute-done((s16[2,656,128]{2,1,0:T(8,128)(2,1)S(1)}, s16[2,656,128]{2,1,0:T(8,128)(2,1)S(1)}, u32[]{:S(2)}, u32[]{:S(2)}) %collective-permute-start.26) | collective-permute-done | bytes 335904 | tf_op jit(solution)/shard_map/ppermute | solution.py:351
  188.7 1.7 finish.4.refs_4_
  190.4 1.0 collective-permute-done.11.refs_1_
  191.4 1.0 collective-permute-done.12.refs_2_
  192.3 3.2 %collective-permute-done.13.refs_3_ = s16[1,656,128]{2,1,0:T(8,128)(2,1)S(1)} collective-permute-done((s16[1,656,128]{2,1,0:T(8,128)(2,1)S(1)}, s16[1,656,128]{2,1,0:T(8,128)(2,1)S(1)}, u32[]{:S(2)}, u32[]{:S(2)}) %collective-permute-start.13) | collective-permute-done | bytes 167968 | tf_op jit(solution)/shard_map/ppermute | solution.py:351
  195.5 1.4 finish.5
  (67 shorter events, 9.9 us)
Async XLA Ops:
  1.1 75.5 %copy-start.10 = (s32[100,5]{0,1:T(8,128)S(1)}, s32[100,5]{0,1:T(8,128)}, u32[]{:S(2)}) copy-start(s32[100,5]{0,1:T(8,128)} %param.4) | copy-start | bytes 6004
  1.1 13.7 %collective-permute-start.28 = (bf16[2,5,128,128]{3,2,1,0:T(8,128)(2,1)S(1)}, bf16[2,5,128,128]{3,2,1,0:T(8,128)(2,1)S(1)}, u32[]{:S(2)}, u32[]{:S(2)}) collective-permute-start(bf16[2,5,128,128]{3,2,1,0:T(8,128)(2,1)S(1)} %get-tuple-element.53.refs_0_.own_ref), channel_id=1, source_target_pairs={{0,2},{2,4},{4,6},{6,0},{1,3},{3,5},{5,7},{7,1},{8,10},{10,12},{12... | collective-permute-start | bytes 983048 | tf_op jit(solution)/shard_map/ppermute | solution.py:323
  4.2 17.6 %collective-permute-start.14 = (bf16[2,5,128,128]{3,2,1,0:T(8,128)(2,1)S(1)}, bf16[2,5,128,128]{3,2,1,0:T(8,128)(2,1)S(1)}, u32[]{:S(2)}, u32[]{:S(2)}) collective-permute-start(bf16[2,5,128,128]{3,2,1,0:T(8,128)(2,1)S(1)} %get-tuple-element.54.refs_0_.own_ref), channel_id=1, source_target_pairs={{0,2},{2,4},{4,6},{6,0},{1,3},{3,5},{5,7},{7,1},{8,10},{10,12},{12... | collective-permute-start | bytes 983048 | tf_op jit(solution)/shard_map/ppermute | solution.py:323
  14.8 14.0 %collective-permute-start.29 = (bf16[2,5,128,128]{3,2,1,0:T(8,128)(2,1)S(1)}, bf16[2,5,128,128]{3,2,1,0:T(8,128)(2,1)S(1)}, u32[]{:S(2)}, u32[]{:S(2)}) collective-permute-start(bf16[2,5,128,128]{3,2,1,0:T(8,128)(2,1)S(1)} %collective-permute-done.28.refs_1_), channel_id=1, source_target_pairs={{0,2},{2,4},{4,6},{6,0},{1,3},{3,5},{5,7},{7,1},{8,10},{10,12},{12... | collective-permute-start | bytes 983048 | tf_op jit(solution)/shard_map/ppermute | solution.py:323
  21.9 14.0 %collective-permute-start.15 = (bf16[2,5,128,128]{3,2,1,0:T(8,128)(2,1)S(1)}, bf16[2,5,128,128]{3,2,1,0:T(8,128)(2,1)S(1)}, u32[]{:S(2)}, u32[]{:S(2)}) collective-permute-start(bf16[2,5,128,128]{3,2,1,0:T(8,128)(2,1)S(1)} %collective-permute-done.14.refs_1_), channel_id=1, source_target_pairs={{0,2},{2,4},{4,6},{6,0},{1,3},{3,5},{5,7},{7,1},{8,10},{10,12},{12... | collective-permute-start | bytes 983048 | tf_op jit(solution)/shard_map/ppermute | solution.py:323
  28.9 14.0 %collective-permute-start.30 = (bf16[2,5,128,128]{3,2,1,0:T(8,128)(2,1)S(1)}, bf16[2,5,128,128]{3,2,1,0:T(8,128)(2,1)S(1)}, u32[]{:S(2)}, u32[]{:S(2)}) collective-permute-start(bf16[2,5,128,128]{3,2,1,0:T(8,128)(2,1)S(1)} %collective-permute-done.29.refs_2_), channel_id=1, source_target_pairs={{0,2},{2,4},{4,6},{6,0},{1,3},{3,5},{5,7},{7,1},{8,10},{10,12},{12... | collective-permute-start | bytes 983048 | tf_op jit(solution)/shard_map/ppermute | solution.py:323
  35.9 13.2 %collective-permute-start.16 = (bf16[2,5,128,128]{3,2,1,0:T(8,128)(2,1)S(1)}, bf16[2,5,128,128]{3,2,1,0:T(8,128)(2,1)S(1)}, u32[]{:S(2)}, u32[]{:S(2)}) collective-permute-start(bf16[2,5,128,128]{3,2,1,0:T(8,128)(2,1)S(1)} %collective-permute-done.15.refs_2_), channel_id=1, source_target_pairs={{0,2},{2,4},{4,6},{6,0},{1,3},{3,5},{5,7},{7,1},{8,10},{10,12},{12... | collective-permute-start | bytes 983048 | tf_op jit(solution)/shard_map/ppermute | solution.py:323
  44.0 10.6 %collective-permute-start.31 = (bf16[2,5,128,128]{3,2,1,0:T(8,128)(2,1)S(1)}, bf16[2,5,128,128]{3,2,1,0:T(8,128)(2,1)S(1)}, u32[]{:S(2)}, u32[]{:S(2)}) collective-permute-start(bf16[2,5,128,128]{3,2,1,0:T(8,128)(2,1)S(1)} %get-tuple-element.46), channel_id=1, source_target_pairs={{0,8},{8,0},{16,24},{24,16},{1,9},{9,1},{17,25},{25,17},{2,10},{10... | collective-permute-start | bytes 983048 | tf_op jit(solution)/shard_map/ppermute | solution.py:331
  45.8 14.7 %collective-permute-start.32 = (bf16[2,5,128,128]{3,2,1,0:T(8,128)(2,1)S(1)}, bf16[2,5,128,128]{3,2,1,0:T(8,128)(2,1)S(1)}, u32[]{:S(2)}, u32[]{:S(2)}) collective-permute-start(bf16[2,5,128,128]{3,2,1,0:T(8,128)(2,1)S(1)} %get-tuple-element.47), channel_id=1, source_target_pairs={{0,16},{8,24},{16,0},{24,8},{1,17},{9,25},{17,1},{25,9},{2,18},{10... | collective-permute-start | bytes 983048 | tf_op jit(solution)/shard_map/ppermute | solution.py:331
  47.3 15.6 %collective-permute-start.33 = (bf16[2,5,128,128]{3,2,1,0:T(8,128)(2,1)S(1)}, bf16[2,5,128,128]{3,2,1,0:T(8,128)(2,1)S(1)}, u32[]{:S(2)}, u32[]{:S(2)}) collective-permute-start(bf16[2,5,128,128]{3,2,1,0:T(8,128)(2,1)S(1)} %get-tuple-element.48), channel_id=1, source_target_pairs={{0,24},{8,16},{16,8},{24,0},{1,25},{9,17},{17,9},{25,1},{2,26},{10... | collective-permute-start | bytes 983048 | tf_op jit(solution)/shard_map/ppermute | solution.py:331
  47.6 15.3 %collective-permute-start.34 = (bf16[2,5,128,128]{3,2,1,0:T(8,128)(2,1)S(1)}, bf16[2,5,128,128]{3,2,1,0:T(8,128)(2,1)S(1)}, u32[]{:S(2)}, u32[]{:S(2)}) collective-permute-start(bf16[2,5,128,128]{3,2,1,0:T(8,128)(2,1)S(1)} %get-tuple-element.45.refs_0_), channel_id=1, source_target_pairs={{1,0},{0,1},{3,2},{2,3},{5,4},{4,5},{7,6},{6,7},{9,8},{8,9},{11,10... | collective-permute-start | bytes 983048 | tf_op jit(solution)/shard_map/ppermute | solution.py:342
  50.2 18.6 %collective-permute-start.17 = (bf16[2,5,128,128]{3,2,1,0:T(8,128)(2,1)S(1)}, bf16[2,5,128,128]{3,2,1,0:T(8,128)(2,1)S(1)}, u32[]{:S(2)}, u32[]{:S(2)}) collective-permute-start(bf16[2,5,128,128]{3,2,1,0:T(8,128)(2,1)S(1)} %get-tuple-element.38), channel_id=1, source_target_pairs={{0,8},{8,0},{16,24},{24,16},{1,9},{9,1},{17,25},{25,17},{2,10},{10... | collective-permute-start | bytes 983048 | tf_op jit(solution)/shard_map/ppermute | solution.py:331
  54.7 19.5 %collective-permute-start.18 = (bf16[2,5,128,128]{3,2,1,0:T(8,128)(2,1)S(1)}, bf16[2,5,128,128]{3,2,1,0:T(8,128)(2,1)S(1)}, u32[]{:S(2)}, u32[]{:S(2)}) collective-permute-start(bf16[2,5,128,128]{3,2,1,0:T(8,128)(2,1)S(1)} %get-tuple-element.39), channel_id=1, source_target_pairs={{0,16},{8,24},{16,0},{24,8},{1,17},{9,25},{17,1},{25,9},{2,18},{10... | collective-permute-start | bytes 983048 | tf_op jit(solution)/shard_map/ppermute | solution.py:331
  60.5 13.6 %collective-permute-start.19 = (bf16[2,5,128,128]{3,2,1,0:T(8,128)(2,1)S(1)}, bf16[2,5,128,128]{3,2,1,0:T(8,128)(2,1)S(1)}, u32[]{:S(2)}, u32[]{:S(2)}) collective-permute-start(bf16[2,5,128,128]{3,2,1,0:T(8,128)(2,1)S(1)} %get-tuple-element.40), channel_id=1, source_target_pairs={{0,24},{8,16},{16,8},{24,0},{1,25},{9,17},{17,9},{25,1},{2,26},{10... | collective-permute-start | bytes 983048 | tf_op jit(solution)/shard_map/ppermute | solution.py:331
  62.9 11.8 %collective-permute-start.35 = (bf16[2,5,128,128]{3,2,1,0:T(8,128)(2,1)S(1)}, bf16[2,5,128,128]{3,2,1,0:T(8,128)(2,1)S(1)}, u32[]{:S(2)}, u32[]{:S(2)}) collective-permute-start(bf16[2,5,128,128]{3,2,1,0:T(8,128)(2,1)S(1)} %collective-permute-done.31.refs_1_), channel_id=1, source_target_pairs={{1,0},{0,1},{3,2},{2,3},{5,4},{4,5},{7,6},{6,7},{9,8},{8,9},{11,10... | collective-permute-start | bytes 983048 | tf_op jit(solution)/shard_map/ppermute | solution.py:342
  62.9 0.7 copy-start.3
  63.6 11.8 %collective-permute-start.36 = (bf16[2,5,128,128]{3,2,1,0:T(8,128)(2,1)S(1)}, bf16[2,5,128,128]{3,2,1,0:T(8,128)(2,1)S(1)}, u32[]{:S(2)}, u32[]{:S(2)}) collective-permute-start(bf16[2,5,128,128]{3,2,1,0:T(8,128)(2,1)S(1)} %collective-permute-done.32.refs_2_), channel_id=1, source_target_pairs={{1,0},{0,1},{3,2},{2,3},{5,4},{4,5},{7,6},{6,7},{9,8},{8,9},{11,10... | collective-permute-start | bytes 983048 | tf_op jit(solution)/shard_map/ppermute | solution.py:342
  68.7 30.5 %collective-permute-start.37 = (bf16[2,5,128,128]{3,2,1,0:T(8,128)(2,1)S(1)}, bf16[2,5,128,128]{3,2,1,0:T(8,128)(2,1)}, u32[]{:S(2)}, u32[]{:S(2)}) collective-permute-start(bf16[2,5,128,128]{3,2,1,0:T(8,128)(2,1)S(1)} %collective-permute-done.33.refs_3_), channel_id=1, source_target_pairs={{1,0},{0,1},{3,2},{2,3},{5,4},{4,5},{7,6},{6,7},{9,8},{8,9},{11,10... | collective-permute-start | bytes 983048 | tf_op jit(solution)/shard_map/ppermute | solution.py:342
  74.2 40.2 %collective-permute-start.20 = (bf16[2,5,128,128]{3,2,1,0:T(8,128)(2,1)S(1)}, bf16[2,5,128,128]{3,2,1,0:T(8,128)(2,1)}, u32[]{:S(2)}, u32[]{:S(2)}) collective-permute-start(bf16[2,5,128,128]{3,2,1,0:T(8,128)(2,1)S(1)} %get-tuple-element.37.refs_0_), channel_id=1, source_target_pairs={{1,0},{0,1},{3,2},{2,3},{5,4},{4,5},{7,6},{6,7},{9,8},{8,9},{11,10... | collective-permute-start | bytes 983048 | tf_op jit(solution)/shard_map/ppermute | solution.py:342
  74.2 41.9 %collective-permute-start.21 = (bf16[2,5,128,128]{3,2,1,0:T(8,128)(2,1)S(1)}, bf16[2,5,128,128]{3,2,1,0:T(8,128)(2,1)}, u32[]{:S(2)}, u32[]{:S(2)}) collective-permute-start(bf16[2,5,128,128]{3,2,1,0:T(8,128)(2,1)S(1)} %collective-permute-done.17.refs_1_), channel_id=1, source_target_pairs={{1,0},{0,1},{3,2},{2,3},{5,4},{4,5},{7,6},{6,7},{9,8},{8,9},{11,10... | collective-permute-start | bytes 983048 | tf_op jit(solution)/shard_map/ppermute | solution.py:342
  74.7 0.7 copy-start.5
  75.4 40.7 %collective-permute-start.22 = (bf16[2,5,128,128]{3,2,1,0:T(8,128)(2,1)S(1)}, bf16[2,5,128,128]{3,2,1,0:T(8,128)(2,1)}, u32[]{:S(2)}, u32[]{:S(2)}) collective-permute-start(bf16[2,5,128,128]{3,2,1,0:T(8,128)(2,1)S(1)} %collective-permute-done.18.refs_2_), channel_id=1, source_target_pairs={{1,0},{0,1},{3,2},{2,3},{5,4},{4,5},{7,6},{6,7},{9,8},{8,9},{11,10... | collective-permute-start | bytes 983048 | tf_op jit(solution)/shard_map/ppermute | solution.py:342
  75.4 0.7 copy-start.7
  76.1 39.9 %collective-permute-start.23 = (bf16[2,5,128,128]{3,2,1,0:T(8,128)(2,1)S(1)}, bf16[2,5,128,128]{3,2,1,0:T(8,128)(2,1)}, u32[]{:S(2)}, u32[]{:S(2)}) collective-permute-start(bf16[2,5,128,128]{3,2,1,0:T(8,128)(2,1)S(1)} %collective-permute-done.19.refs_3_), channel_id=1, source_target_pairs={{1,0},{0,1},{3,2},{2,3},{5,4},{4,5},{7,6},{6,7},{9,8},{8,9},{11,10... | collective-permute-start | bytes 983048 | tf_op jit(solution)/shard_map/ppermute | solution.py:342
  77.5 14.7 %all-to-all-start = ((s32[32,5,5]{2,1,0:T(8,128)}), s32[32,5,5]{2,1,0:T(8,128)S(1)}, u32[]{:S(2)}, u32[]{:S(2)}) async-start(s32[32,5,5]{2,1,0:T(8,128)} %broadcast_in_dim.2), calls=%async_computation | async-start | bytes 262144 | tf_op jit(solution)/shard_map/all_to_all | solution.py:310
  86.4 5.6 %copy-start = (bf16[100,5,128,128]{3,2,1,0:T(8,128)(2,1)}, bf16[100,5,128,128]{3,2,1,0:T(8,128)(2,1)S(1)}, u32[]{:S(2)}) copy-start(bf16[100,5,128,128]{3,2,1,0:T(8,128)(2,1)S(1)} %bring.1.values_ref) | copy-start | bytes 49152004
  99.3 5.7 %copy-start.1 = (bf16[100,5,128,128]{3,2,1,0:T(8,128)(2,1)S(1)}, bf16[100,5,128,128]{3,2,1,0:T(8,128)(2,1)}, u32[]{:S(2)}) copy-start(bf16[100,5,128,128]{3,2,1,0:T(8,128)(2,1)} %copy-done) | copy-start | bytes 49152004
  105.0 1.0 copy-start.4
  105.9 1.0 copy-start.6
  106.9 1.0 copy-start.8
  107.9 8.2 %copy-start.2 = (bf16[100,5,128,128]{3,2,1,0:T(8,128)(2,1)S(1)}, bf16[100,5,128,128]{3,2,1,0:T(8,128)(2,1)}, u32[]{:S(2)}) copy-start(bf16[100,5,128,128]{3,2,1,0:T(8,128)(2,1)} %copy-done) | copy-start | bytes 49152004
  112.1 39.5 %collective-permute-start.38 = (s16[8,656,128]{2,1,0:T(8,128)(2,1)S(1)}, s16[8,656,128]{2,1,0:T(8,128)(2,1)S(1)}, u32[]{:S(2)}, u32[]{:S(2)}) collective-permute-start(s16[8,656,128]{2,1,0:T(8,128)(2,1)S(1)} %product.10), channel_id=1, source_target_pairs={{0,1},{1,0},{2,3},{3,2},{4,5},{5,4},{6,7},{7,6},{8,9},{9,8},{10,11... | collective-permute-start | bytes 4030472 | tf_op jit(solution)/shard_map/ppermute | solution.py:345
  114.4 8.0 %collective-permute-start = (bf16[1,5,128,128]{3,2,1,0:T(8,128)(2,1)S(1)}, bf16[1,5,128,128]{3,2,1,0:T(8,128)(2,1)S(1)}, u32[]{:S(2)}, u32[]{:S(2)}) collective-permute-start(bf16[1,5,128,128]{3,2,1,0:T(8,128)(2,1)S(1)} %slice.13.refs_0_.own_ref), channel_id=1, source_target_pairs={{0,2},{2,4},{4,6},{6,0},{1,3},{3,5},{5,7},{7,1},{8,10},{10,12},{12... | collective-permute-start | bytes 491528 | tf_op jit(solution)/shard_map/ppermute | solution.py:323
  120.8 38.2 %collective-permute-start.24 = (s16[8,656,128]{2,1,0:T(8,128)(2,1)S(1)}, s16[8,656,128]{2,1,0:T(8,128)(2,1)S(1)}, u32[]{:S(2)}, u32[]{:S(2)}) collective-permute-start(s16[8,656,128]{2,1,0:T(8,128)(2,1)S(1)} %product.8), channel_id=1, source_target_pairs={{0,1},{1,0},{2,3},{3,2},{4,5},{5,4},{6,7},{7,6},{8,9},{9,8},{10,11... | collective-permute-start | bytes 4030472 | tf_op jit(solution)/shard_map/ppermute | solution.py:345
  122.3 7.1 %collective-permute-start.1 = (bf16[1,5,128,128]{3,2,1,0:T(8,128)(2,1)S(1)}, bf16[1,5,128,128]{3,2,1,0:T(8,128)(2,1)S(1)}, u32[]{:S(2)}, u32[]{:S(2)}) collective-permute-start(bf16[1,5,128,128]{3,2,1,0:T(8,128)(2,1)S(1)} %collective-permute-done.refs_1_), channel_id=1, source_target_pairs={{0,2},{2,4},{4,6},{6,0},{1,3},{3,5},{5,7},{7,1},{8,10},{10,12},{12... | collective-permute-start | bytes 491528 | tf_op jit(solution)/shard_map/ppermute | solution.py:323
  129.5 7.1 %collective-permute-start.2 = (bf16[1,5,128,128]{3,2,1,0:T(8,128)(2,1)S(1)}, bf16[1,5,128,128]{3,2,1,0:T(8,128)(2,1)S(1)}, u32[]{:S(2)}, u32[]{:S(2)}) collective-permute-start(bf16[1,5,128,128]{3,2,1,0:T(8,128)(2,1)S(1)} %collective-permute-done.1.refs_2_), channel_id=1, source_target_pairs={{0,2},{2,4},{4,6},{6,0},{1,3},{3,5},{5,7},{7,1},{8,10},{10,12},{12... | collective-permute-start | bytes 491528 | tf_op jit(solution)/shard_map/ppermute | solution.py:323
  138.1 5.6 %collective-permute-start.3 = (bf16[1,5,128,128]{3,2,1,0:T(8,128)(2,1)S(1)}, bf16[1,5,128,128]{3,2,1,0:T(8,128)(2,1)S(1)}, u32[]{:S(2)}, u32[]{:S(2)}) collective-permute-start(bf16[1,5,128,128]{3,2,1,0:T(8,128)(2,1)S(1)} %get-tuple-element.30), channel_id=1, source_target_pairs={{0,8},{8,0},{16,24},{24,16},{1,9},{9,1},{17,25},{25,17},{2,10},{10... | collective-permute-start | bytes 491528 | tf_op jit(solution)/shard_map/ppermute | solution.py:331
  139.3 6.2 %collective-permute-start.4 = (bf16[1,5,128,128]{3,2,1,0:T(8,128)(2,1)S(1)}, bf16[1,5,128,128]{3,2,1,0:T(8,128)(2,1)S(1)}, u32[]{:S(2)}, u32[]{:S(2)}) collective-permute-start(bf16[1,5,128,128]{3,2,1,0:T(8,128)(2,1)S(1)} %get-tuple-element.31), channel_id=1, source_target_pairs={{0,16},{8,24},{16,0},{24,8},{1,17},{9,25},{17,1},{25,9},{2,18},{10... | collective-permute-start | bytes 491528 | tf_op jit(solution)/shard_map/ppermute | solution.py:331
  140.9 6.2 %collective-permute-start.5 = (bf16[1,5,128,128]{3,2,1,0:T(8,128)(2,1)S(1)}, bf16[1,5,128,128]{3,2,1,0:T(8,128)(2,1)S(1)}, u32[]{:S(2)}, u32[]{:S(2)}) collective-permute-start(bf16[1,5,128,128]{3,2,1,0:T(8,128)(2,1)S(1)} %get-tuple-element.32), channel_id=1, source_target_pairs={{0,24},{8,16},{16,8},{24,0},{1,25},{9,17},{17,9},{25,1},{2,26},{10... | collective-permute-start | bytes 491528 | tf_op jit(solution)/shard_map/ppermute | solution.py:331
  143.7 3.4 %collective-permute-start.6 = (bf16[1,5,128,128]{3,2,1,0:T(8,128)(2,1)S(1)}, bf16[1,5,128,128]{3,2,1,0:T(8,128)(2,1)S(1)}, u32[]{:S(2)}, u32[]{:S(2)}) collective-permute-start(bf16[1,5,128,128]{3,2,1,0:T(8,128)(2,1)S(1)} %get-tuple-element.29.refs_0_), channel_id=1, source_target_pairs={{1,0},{0,1},{3,2},{2,3},{5,4},{4,5},{7,6},{6,7},{9,8},{8,9},{11,10... | collective-permute-start | bytes 491528 | tf_op jit(solution)/shard_map/ppermute | solution.py:342
  145.5 2.1 %collective-permute-start.7 = (bf16[1,5,128,128]{3,2,1,0:T(8,128)(2,1)S(1)}, bf16[1,5,128,128]{3,2,1,0:T(8,128)(2,1)S(1)}, u32[]{:S(2)}, u32[]{:S(2)}) collective-permute-start(bf16[1,5,128,128]{3,2,1,0:T(8,128)(2,1)S(1)} %collective-permute-done.3.refs_1_), channel_id=1, source_target_pairs={{1,0},{0,1},{3,2},{2,3},{5,4},{4,5},{7,6},{6,7},{9,8},{8,9},{11,10... | collective-permute-start | bytes 491528 | tf_op jit(solution)/shard_map/ppermute | solution.py:342
  147.1 1.4 collective-permute-start.8
  147.1 1.6 collective-permute-start.9
  151.2 14.0 %collective-permute-start.10 = (s16[4,656,128]{2,1,0:T(8,128)(2,1)S(1)}, s16[4,656,128]{2,1,0:T(8,128)(2,1)S(1)}, u32[]{:S(2)}, u32[]{:S(2)}) collective-permute-start(s16[4,656,128]{2,1,0:T(8,128)(2,1)S(1)} %product.6), channel_id=1, source_target_pairs={{0,1},{1,0},{2,3},{3,2},{4,5},{5,4},{6,7},{7,6},{8,9},{9,8},{10,11... | collective-permute-start | bytes 2015240 | tf_op jit(solution)/shard_map/ppermute | solution.py:345
  155.4 10.7 %collective-permute-start.39 = (s16[2,656,128]{2,1,0:T(8,128)(2,1)S(1)}, s16[2,656,128]{2,1,0:T(8,128)(2,1)S(1)}, u32[]{:S(2)}, u32[]{:S(2)}) collective-permute-start(s16[2,656,128]{2,1,0:T(8,128)(2,1)S(1)} %get-tuple-element.50), channel_id=1, source_target_pairs={{0,8},{8,0},{16,24},{24,16},{1,9},{9,1},{17,25},{25,17},{2,10},{10... | collective-permute-start | bytes 1007624 | tf_op jit(solution)/shard_map/ppermute | solution.py:351
  156.7 17.1 %collective-permute-start.40 = (s16[2,656,128]{2,1,0:T(8,128)(2,1)S(1)}, s16[2,656,128]{2,1,0:T(8,128)(2,1)S(1)}, u32[]{:S(2)}, u32[]{:S(2)}) collective-permute-start(s16[2,656,128]{2,1,0:T(8,128)(2,1)S(1)} %get-tuple-element.51), channel_id=1, source_target_pairs={{0,16},{8,24},{16,0},{24,8},{1,17},{9,25},{17,1},{25,9},{2,18},{10... | collective-permute-start | bytes 1007624 | tf_op jit(solution)/shard_map/ppermute | solution.py:351
  157.5 18.0 %collective-permute-start.41 = (s16[2,656,128]{2,1,0:T(8,128)(2,1)S(1)}, s16[2,656,128]{2,1,0:T(8,128)(2,1)S(1)}, u32[]{:S(2)}, u32[]{:S(2)}) collective-permute-start(s16[2,656,128]{2,1,0:T(8,128)(2,1)S(1)} %get-tuple-element.52), channel_id=1, source_target_pairs={{0,24},{8,16},{16,8},{24,0},{1,25},{9,17},{17,9},{25,1},{2,26},{10... | collective-permute-start | bytes 1007624 | tf_op jit(solution)/shard_map/ppermute | solution.py:351
  163.4 17.2 %collective-permute-start.25 = (s16[2,656,128]{2,1,0:T(8,128)(2,1)S(1)}, s16[2,656,128]{2,1,0:T(8,128)(2,1)S(1)}, u32[]{:S(2)}, u32[]{:S(2)}) collective-permute-start(s16[2,656,128]{2,1,0:T(8,128)(2,1)S(1)} %get-tuple-element.42), channel_id=1, source_target_pairs={{0,8},{8,0},{16,24},{24,16},{1,9},{9,1},{17,25},{25,17},{2,10},{10... | collective-permute-start | bytes 1007624 | tf_op jit(solution)/shard_map/ppermute | solution.py:351
  165.1 23.0 %collective-permute-start.26 = (s16[2,656,128]{2,1,0:T(8,128)(2,1)S(1)}, s16[2,656,128]{2,1,0:T(8,128)(2,1)S(1)}, u32[]{:S(2)}, u32[]{:S(2)}) collective-permute-start(s16[2,656,128]{2,1,0:T(8,128)(2,1)S(1)} %get-tuple-element.43), channel_id=1, source_target_pairs={{0,16},{8,24},{16,0},{24,8},{1,17},{9,25},{17,1},{25,9},{2,18},{10... | collective-permute-start | bytes 1007624 | tf_op jit(solution)/shard_map/ppermute | solution.py:351
  166.1 16.0 %copy-start.9 = (s32[40]{0:T(128)S(1)}, s32[40]{0:T(128)}, u32[]{:S(2)}) copy-start(s32[40]{0:T(128)} %flag_ref.5) | copy-start | bytes 484
  166.1 22.6 %collective-permute-start.27 = (s16[2,656,128]{2,1,0:T(8,128)(2,1)S(1)}, s16[2,656,128]{2,1,0:T(8,128)(2,1)S(1)}, u32[]{:S(2)}, u32[]{:S(2)}) collective-permute-start(s16[2,656,128]{2,1,0:T(8,128)(2,1)S(1)} %get-tuple-element.44), channel_id=1, source_target_pairs={{0,24},{8,16},{16,8},{24,0},{1,25},{9,17},{17,9},{25,1},{2,26},{10... | collective-permute-start | bytes 1007624 | tf_op jit(solution)/shard_map/ppermute | solution.py:351
  173.7 17.6 %collective-permute-start.11 = (s16[1,656,128]{2,1,0:T(8,128)(2,1)S(1)}, s16[1,656,128]{2,1,0:T(8,128)(2,1)S(1)}, u32[]{:S(2)}, u32[]{:S(2)}) collective-permute-start(s16[1,656,128]{2,1,0:T(8,128)(2,1)S(1)} %get-tuple-element.34), channel_id=1, source_target_pairs={{0,8},{8,0},{16,24},{24,16},{1,9},{9,1},{17,25},{25,17},{2,10},{10... | collective-permute-start | bytes 503816 | tf_op jit(solution)/shard_map/ppermute | solution.py:351
  175.5 16.9 %collective-permute-start.12 = (s16[1,656,128]{2,1,0:T(8,128)(2,1)S(1)}, s16[1,656,128]{2,1,0:T(8,128)(2,1)S(1)}, u32[]{:S(2)}, u32[]{:S(2)}) collective-permute-start(s16[1,656,128]{2,1,0:T(8,128)(2,1)S(1)} %get-tuple-element.35), channel_id=1, source_target_pairs={{0,16},{8,24},{16,0},{24,8},{1,17},{9,25},{17,1},{25,9},{2,18},{10... | collective-permute-start | bytes 503816 | tf_op jit(solution)/shard_map/ppermute | solution.py:351
  180.5 15.0 %collective-permute-start.13 = (s16[1,656,128]{2,1,0:T(8,128)(2,1)S(1)}, s16[1,656,128]{2,1,0:T(8,128)(2,1)S(1)}, u32[]{:S(2)}, u32[]{:S(2)}) collective-permute-start(s16[1,656,128]{2,1,0:T(8,128)(2,1)S(1)} %get-tuple-element.36), channel_id=1, source_target_pairs={{0,24},{8,16},{16,8},{24,0},{1,25},{9,17},{17,9},{25,1},{2,26},{10... | collective-permute-start | bytes 503816 | tf_op jit(solution)/shard_map/ppermute | solution.py:351

commit v3 on v2

--- a/solution.py
+++ b/solution.py
@@ -55,13 +55,20 @@
     return 1 + 2 * terms + terms * slots
 
 
-def make_tables(where, every, pattern, sizes, chunks):
+def make_tables(where, every, pattern, values, sizes, chunks):
     parts, panels, depths, count, slots, rows_here, panel_cols = sizes
     per_part = panels // parts
     terms = per_part * slots
     total, record = parts * depths * count, record_size(terms, slots)
 
-    def kernel(where_ref, every_ref, pattern_ref, out_ref):
+    cuts = [rows_here * i // 4 for i in range(5)]
+
+    def kernel(where_ref, every_ref, pattern_ref, values_ref, out_ref, near_ref, sem):
+        copies = []
+        for i, (a, b) in enumerate(zip(cuts[:-1], cuts[1:])):
+            part = pl.ds(a, b - a)
+            copies.append(pltpu.make_async_copy(values_ref.at[part], near_ref.at[part], sem.at[i]))
+            copies[-1].start()
         row, depth, z = where_ref[0], where_ref[1], where_ref[2]
         base = 0
         for s in range(depths):
@@ -100,39 +107,26 @@
 
                 lax.fori_loop(0, parts * n, one, 0)
                 base += parts * n
+        for copy in copies:
+            copy.wait()
 
     return pl.pallas_call(
         kernel,
-        out_shape=jax.ShapeDtypeStruct((total * record,), jnp.int32),
-        in_specs=[SCALARS] * 3,
-        out_specs=SCALARS,
-        compiler_params=pltpu.CompilerParams(vmem_limit_bytes=VMEM_BYTES),
-        name="tables",
-    )(where, every, pattern)
-
-
-def bring(values):
-    rows = values.shape[0]
-    cuts = [rows * i // 4 for i in range(5)]
-
-    def kernel(values_ref, out_ref, sem):
-        copies = []
-        for i, (a, b) in enumerate(zip(cuts[:-1], cuts[1:])):
-            part = pl.ds(a, b - a)
-            copies.append(pltpu.make_async_copy(values_ref.at[part], out_ref.at[part], sem.at[i]))
-            copies[-1].start()
-        for copy in copies:
-            copy.wait()
-
-    return pl.pallas_call(
-        kernel,
-        out_shape=jax.ShapeDtypeStruct(values.shape, values.dtype),
-        in_specs=[HERE],
-        out_specs=NEAR,
+        out_shape=[
+            jax.ShapeDtypeStruct((total * record,), jnp.int32),
+            jax.ShapeDtypeStruct(values.shape, values.dtype),
+        ],
+        in_specs=[SCALARS] * 3 + [HERE],
+        out_specs=[SCALARS, NEAR],
         scratch_shapes=[pltpu.SemaphoreType.DMA((4,))],
         compiler_params=pltpu.CompilerParams(vmem_limit_bytes=4 * VMEM_BYTES),
-        name="bring",
-    )(values)
+        name="tables",
+    )(where, every, pattern, values)
+
+
+def stop_of(z, panels):
+    even = jnp.where(z == 0, 0, panels - lax.div(z, 2))
+    return jnp.where(lax.rem(z, 2) == 1, lax.div(z + 1, 2), even)
 
 
 def gather_panels(sources, where, parts, per_part):
@@ -142,6 +136,7 @@
     def kernel(where_ref, *refs):
         outs, sem = refs[len(sources) : len(sources) + parts], refs[-1]
         row, z = where_ref[0], where_ref[2]
+        here = stop_of(z, ring)
         places = [(t, j) for t in range(parts - 1, -1, -1) for j in range(per_part)]
 
         def copy(k, t, j):
@@ -150,8 +145,9 @@
 
         for t, j in places:
             q = (row ^ t) * per_part + j
+            behind = lax.rem(here - stop_of(q, ring) + ring, ring)
             for k in range(ring):
-                @pl.when(q == lax.rem(z + ring - k, ring))
+                @pl.when(behind == k)
                 def _(t=t, j=j, k=k):
                     copy(k, t, j).start()
         for t, j in places:
@@ -303,7 +299,8 @@
     per_part = panels // parts
     chunks = chunks_of(count)
     across = [[(i, i ^ t) for i in range(parts)] for t in range(parts)]
-    ring = [(i, (i + 1) % panels) for i in range(panels)]
+    stops = [*range(0, 1), *range(1, panels, 2), *range(panels - 2 + panels % 2, 0, -2)]
+    ring = list(zip(stops, stops[1:] + stops[:1]))
     where = jnp.stack([row, depth, z]).astype(jnp.int32)
 
     own = [values[a * stride : (a + n - 1) * stride + 1 : stride] for a, n in chunks]
@@ -311,11 +308,10 @@
         jnp.broadcast_to(pattern[None, ::stride], (parts * panels * depths, count, slots)),
         ("row", "col", "depth"), split_axis=0, concat_axis=0, tiled=True,
     )
-    tables = make_tables(
-        where, every.reshape(-1), pattern.reshape(-1),
+    tables, near = make_tables(
+        where, every.reshape(-1), pattern.reshape(-1), values,
         (parts, panels, depths, count, slots, rows_here, panel_cols), chunks,
     )
-    near = bring(values)
 
     held = [[x] for x in own]
     for _ in range(panels - 1):

time: 197 us -> 183 us (0.929)
  local copies, waits for them, and re-layouts: 19.8 us -> 5.58 us
  starting transfers between devices: 37 us -> 43 us
  Pallas kernels: 43.1 us -> 37.5 us
    unnamed x23 -> x17, local copies, waits for them, and re-layouts: 16.5 us -> 2.32 us
    all_to_all x1, waiting for transfers between devices: 0.01 us -> 7.86 us  [inner(): lax.all_to_all(jnp.broadcast_to(pattern[None, ::stride], (parts * panels...]
    ppermute x9, waiting for transfers between devices: 54.2 us -> 46.4 us  [inner(): held[c].append(lax.ppermute(held[c][-1], 'col', ring))]
    pallas_call x2 -> x1, Pallas kernels: 12.6 us -> 7.09 us  [make_tables(): pl.pallas_call(kernel, out_shape=[jax.ShapeDtypeStruct((total * record,),...]
    ppermute x9, starting transfers between devices: 6.44 us -> 10.5 us  [inner(): held[c].append(lax.ppermute(held[c][-1], 'col', ring))]
  transfers between devices with their start and end apart: 43 -> 43, of which waited for: 27 -> 24; matrix products, arithmetic and copies ran while one was open for 1% -> 1% of each run, Pallas kernels for 21% -> 20%
where the time goes in v3:
time: 183 us
  waiting for transfers between devices  96.8 us (53%)
  starting transfers between devices  43 us (23%)
  Pallas kernels  37.5 us (20%)
  local copies, waits for them, and re-layouts  5.58 us (3%)
    ppermute x9, waiting for transfers between devices, inner(): held[c].append(lax.ppermute(held[c][-1], 'col', ring))  46.4 us
    ppermute x9, waiting for transfers between devices, inner(): got.append(lax.ppermute(picked[t], 'row', across[t]))  21.8 us
    pallas_call x6, Pallas kernels, product(): pl.pallas_call(kernel, out_shape=out_shape, in_specs=[SCALARS] + [NEAR] *...  21.8 us
    ppermute x9, waiting for transfers between devices, inner(): summed.append(lax.ppermute(mine[t], 'row', across[t]))  19.4 us
    ppermute x9, starting transfers between devices, inner(): got.append(lax.ppermute(picked[t], 'row', across[t]))  12.1 us
    ppermute x9, starting transfers between devices, inner(): summed.append(lax.ppermute(mine[t], 'row', across[t]))  11.5 us
    ppermute x9, starting transfers between devices, inner(): held[c].append(lax.ppermute(held[c][-1], 'col', ring))  10.5 us
    all_to_all x1, waiting for transfers between devices, inner(): lax.all_to_all(jnp.broadcast_to(pattern[None, ::stride], (parts * panels...  7.86 us
  transfers between devices with their start and end apart: 43, of which 24 were waited for; matrix products, arithmetic and copies ran while one was open for 1% of the time, Pallas kernels for 20%

profile of v3, /device:TPU:0, one launch (start us, length us, event | category | flops | bytes accessed | tf_op | source)
XLA Modules:
  0.0 183.2 jit_solution(2826395174062491528)
XLA Ops:
  0.0 1.1 fusion
  1.1 3.1 %collective-permute-start.28 = (bf16[2,5,128,128]{3,2,1,0:T(8,128)(2,1)S(1)}, bf16[2,5,128,128]{3,2,1,0:T(8,128)(2,1)S(1)}, u32[]{:S(2)}, u32[]{:S(2)}) collective-permute-start(bf16[2,5,128,128]{3,2,1,0:T(8,128)(2,1)S(1)} %get-tuple-element.57.refs_0_.own_ref), channel_id=1, source_target_pairs={{0,2},{2,6},{6,4},{4,0},{1,3},{3,7},{7,5},{5,1},{8,10},{10,14},{14... | collective-permute-start | bytes 983048 | tf_op jit(solution)/shard_map/ppermute | solution.py:319
  4.2 2.6 %collective-permute-start.14 = (bf16[2,5,128,128]{3,2,1,0:T(8,128)(2,1)S(1)}, bf16[2,5,128,128]{3,2,1,0:T(8,128)(2,1)S(1)}, u32[]{:S(2)}, u32[]{:S(2)}) collective-permute-start(bf16[2,5,128,128]{3,2,1,0:T(8,128)(2,1)S(1)} %get-tuple-element.58.refs_0_.own_ref), channel_id=1, source_target_pairs={{0,2},{2,6},{6,4},{4,0},{1,3},{3,7},{7,5},{5,1},{8,10},{10,14},{14... | collective-permute-start | bytes 983048 | tf_op jit(solution)/shard_map/ppermute | solution.py:319
  6.8 7.0 %collective-permute-done.28.refs_1_ = bf16[2,5,128,128]{3,2,1,0:T(8,128)(2,1)S(1)} collective-permute-done((bf16[2,5,128,128]{3,2,1,0:T(8,128)(2,1)S(1)}, bf16[2,5,128,128]{3,2,1,0:T(8,128)(2,1)S(1)}, u32[]{:S(2)}, u32[]{:S(2)}) %collective-permute-start.28) | collective-permute-done | bytes 327712 | tf_op jit(solution)/shard_map/ppermute | solution.py:319
  13.8 1.1 collective-permute-start.29
  14.9 5.9 %collective-permute-done.14.refs_1_ = bf16[2,5,128,128]{3,2,1,0:T(8,128)(2,1)S(1)} collective-permute-done((bf16[2,5,128,128]{3,2,1,0:T(8,128)(2,1)S(1)}, bf16[2,5,128,128]{3,2,1,0:T(8,128)(2,1)S(1)}, u32[]{:S(2)}, u32[]{:S(2)}) %collective-permute-start.14) | collective-permute-done | bytes 327712 | tf_op jit(solution)/shard_map/ppermute | solution.py:319
  20.8 1.1 collective-permute-start.15
  22.0 5.9 %collective-permute-done.29.refs_2_ = bf16[2,5,128,128]{3,2,1,0:T(8,128)(2,1)S(1)} collective-permute-done((bf16[2,5,128,128]{3,2,1,0:T(8,128)(2,1)S(1)}, bf16[2,5,128,128]{3,2,1,0:T(8,128)(2,1)S(1)}, u32[]{:S(2)}, u32[]{:S(2)}) %collective-permute-start.29) | collective-permute-done | bytes 327712 | tf_op jit(solution)/shard_map/ppermute | solution.py:319
  27.9 1.1 collective-permute-start.30
  29.0 5.9 %collective-permute-done.15.refs_2_ = bf16[2,5,128,128]{3,2,1,0:T(8,128)(2,1)S(1)} collective-permute-done((bf16[2,5,128,128]{3,2,1,0:T(8,128)(2,1)S(1)}, bf16[2,5,128,128]{3,2,1,0:T(8,128)(2,1)S(1)}, u32[]{:S(2)}, u32[]{:S(2)}) %collective-permute-start.15) | collective-permute-done | bytes 327712 | tf_op jit(solution)/shard_map/ppermute | solution.py:319
  34.9 1.1 collective-permute-start.16
  36.1 5.8 %collective-permute-done.30.refs_3_ = bf16[2,5,128,128]{3,2,1,0:T(8,128)(2,1)S(1)} collective-permute-done((bf16[2,5,128,128]{3,2,1,0:T(8,128)(2,1)S(1)}, bf16[2,5,128,128]{3,2,1,0:T(8,128)(2,1)S(1)}, u32[]{:S(2)}, u32[]{:S(2)}) %collective-permute-start.30) | collective-permute-done | bytes 327712 | tf_op jit(solution)/shard_map/ppermute | solution.py:319
  41.9 1.1 gather_panels.5
  43.0 1.9 %collective-permute-start.31 = (bf16[2,5,128,128]{3,2,1,0:T(8,128)(2,1)S(1)}, bf16[2,5,128,128]{3,2,1,0:T(8,128)(2,1)S(1)}, u32[]{:S(2)}, u32[]{:S(2)}) collective-permute-start(bf16[2,5,128,128]{3,2,1,0:T(8,128)(2,1)S(1)} %get-tuple-element.50), channel_id=1, source_target_pairs={{0,8},{8,0},{16,24},{24,16},{1,9},{9,1},{17,25},{25,17},{2,10},{10... | collective-permute-start | bytes 983048 | tf_op jit(solution)/shard_map/ppermute | solution.py:327
  44.9 1.5 collective-permute-start.32
  46.6 1.5 collective-permute-done.16.refs_3_
  48.1 1.1 gather_panels.4
  49.2 1.6 collective-permute-start.17
  50.8 2.9 %collective-permute-done.31.refs_1_ = bf16[2,5,128,128]{3,2,1,0:T(8,128)(2,1)S(1)} collective-permute-done((bf16[2,5,128,128]{3,2,1,0:T(8,128)(2,1)S(1)}, bf16[2,5,128,128]{3,2,1,0:T(8,128)(2,1)S(1)}, u32[]{:S(2)}, u32[]{:S(2)}) %collective-permute-start.31) | collective-permute-done | bytes 327712 | tf_op jit(solution)/shard_map/ppermute | solution.py:327
  53.7 1.8 %collective-permute-start.18 = (bf16[2,5,128,128]{3,2,1,0:T(8,128)(2,1)S(1)}, bf16[2,5,128,128]{3,2,1,0:T(8,128)(2,1)S(1)}, u32[]{:S(2)}, u32[]{:S(2)}) collective-permute-start(bf16[2,5,128,128]{3,2,1,0:T(8,128)(2,1)S(1)} %get-tuple-element.43), channel_id=1, source_target_pairs={{0,16},{8,24},{16,0},{24,8},{1,17},{9,25},{17,1},{25,9},{2,18},{10... | collective-permute-start | bytes 983048 | tf_op jit(solution)/shard_map/ppermute | solution.py:327
  55.5 3.8 %collective-permute-done.32.refs_2_ = bf16[2,5,128,128]{3,2,1,0:T(8,128)(2,1)S(1)} collective-permute-done((bf16[2,5,128,128]{3,2,1,0:T(8,128)(2,1)S(1)}, bf16[2,5,128,128]{3,2,1,0:T(8,128)(2,1)S(1)}, u32[]{:S(2)}, u32[]{:S(2)}) %collective-permute-start.32) | collective-permute-done | bytes 327712 | tf_op jit(solution)/shard_map/ppermute | solution.py:327
  59.4 1.5 collective-permute-start.19
  60.9 1.1 collective-permute-done.33.refs_3_
  62.0 0.7 copy-done
  63.2 4.5 %collective-permute-done.17.refs_1_ = bf16[2,5,128,128]{3,2,1,0:T(8,128)(2,1)S(1)} collective-permute-done((bf16[2,5,128,128]{3,2,1,0:T(8,128)(2,1)S(1)}, bf16[2,5,128,128]{3,2,1,0:T(8,128)(2,1)S(1)}, u32[]{:S(2)}, u32[]{:S(2)}) %collective-permute-start.17) | collective-permute-done | bytes 327712 | tf_op jit(solution)/shard_map/ppermute | solution.py:327
  67.8 5.4 %collective-permute-done.18.refs_2_ = bf16[2,5,128,128]{3,2,1,0:T(8,128)(2,1)S(1)} collective-permute-done((bf16[2,5,128,128]{3,2,1,0:T(8,128)(2,1)S(1)}, bf16[2,5,128,128]{3,2,1,0:T(8,128)(2,1)S(1)}, u32[]{:S(2)}, u32[]{:S(2)}) %collective-permute-start.18) | collective-permute-done | bytes 327712 | tf_op jit(solution)/shard_map/ppermute | solution.py:327
  73.7 0.7 copy-done.2
  74.4 0.7 copy-done.4
  75.8 0.7 broadcast_in_dim.2
  76.5 4.9 %all-to-all-start = ((s32[32,5,5]{2,1,0:T(8,128)}), s32[32,5,5]{2,1,0:T(8,128)S(1)}, u32[]{:S(2)}, u32[]{:S(2)}) async-start(s32[32,5,5]{2,1,0:T(8,128)} %broadcast_in_dim.2), calls=%async_computation | async-start | bytes 262144 | tf_op jit(solution)/shard_map/all_to_all | solution.py:307
  81.7 7.9 %all-to-all-done = s32[32,5,5]{2,1,0:T(8,128)S(1)} async-done(((s32[32,5,5]{2,1,0:T(8,128)}), s32[32,5,5]{2,1,0:T(8,128)S(1)}, u32[]{:S(2)}, u32[]{:S(2)}) %all-to-all-start) | async-done | bytes 3232 | tf_op jit(solution)/shard_map/all_to_all | solution.py:307
  89.8 7.1 %tables.1 = (s32[1440]{0:T(1024)S(1)}, bf16[100,5,128,128]{3,2,1,0:T(8,128)(2,1)S(1)}) custom-call(s32[3]{0:T(128)S(1)} %pad_add_fusion.where_ref, s32[800]{0:T(1024)S(1)} %reshape.7.every_ref, s32[500]{0:T(512)S(1)} %reshape.8.pattern_ref, bf16[100,5,128,128]{3,2,1,0:T(8,128)(2,1)} %values_ref.1), custom_call_target="tpu_custom_call" | custom-call | tf_op jit(solution)/shard_map/tables/pallas_call | solution.py:113
  97.0 4.1 %product.10 = s16[8,656,128]{2,1,0:T(8,128)(2,1)S(1)} custom-call(s32[1440]{0:T(1024)S(1)} %get-tuple-element.31.table_ref, bf16[100,5,128,128]{3,2,1,0:T(8,128)(2,1)S(1)} %get-tuple-element.32.values_ref, bf16[2,5,128,128]{3,2,1,0:T(8,128)(2,1)S(1)} %copy-done.1, bf16[2,5,128,128]{3,2,1,0:T(8,128)(2,1)S(1)} %copy-done.3, ...), custom_call_target="tpu_custom_call" | custom-call | flops 838860800 | bytes 7864320 | tf_op jit(solution)/shard_map/product/pallas_call | solution.py:238
  101.0 1.4 collective-permute-start.38
  102.4 0.9 slice.13.refs_0_.own_ref
  103.7 4.7 %product.8 = s16[8,656,128]{2,1,0:T(8,128)(2,1)S(1)} custom-call(s32[1440]{0:T(1024)S(1)} %get-tuple-element.31.table_ref, bf16[100,5,128,128]{3,2,1,0:T(8,128)(2,1)S(1)} %get-tuple-element.32.values_ref, bf16[2,5,128,128]{3,2,1,0:T(8,128)(2,1)} %collective-permute-done.20.refs_0_, bf16[2,5,128,128]{3,2,1,0:T(8,128)(2,1)} %collective-permute-done.21.refs_1_, ...), custom_call_target="tpu_custom_call" | custom-call | flops 838860800 | bytes 7864320 | tf_op jit(solution)/shard_map/product/pallas_call | solution.py:238
  108.5 1.9 %collective-permute-done.refs_1_ = bf16[1,5,128,128]{3,2,1,0:T(8,128)(2,1)S(1)} collective-permute-done((bf16[1,5,128,128]{3,2,1,0:T(8,128)(2,1)S(1)}, bf16[1,5,128,128]{3,2,1,0:T(8,128)(2,1)S(1)}, u32[]{:S(2)}, u32[]{:S(2)}) %collective-permute-start) | collective-permute-done | bytes 163872 | tf_op jit(solution)/shard_map/ppermute | solution.py:319
  110.4 6.2 %collective-permute-done.1.refs_2_ = bf16[1,5,128,128]{3,2,1,0:T(8,128)(2,1)S(1)} collective-permute-done((bf16[1,5,128,128]{3,2,1,0:T(8,128)(2,1)S(1)}, bf16[1,5,128,128]{3,2,1,0:T(8,128)(2,1)S(1)}, u32[]{:S(2)}, u32[]{:S(2)}) %collective-permute-start.1) | collective-permute-done | bytes 163872 | tf_op jit(solution)/shard_map/ppermute | solution.py:319
  116.7 6.2 %collective-permute-done.2.refs_3_ = bf16[1,5,128,128]{3,2,1,0:T(8,128)(2,1)S(1)} collective-permute-done((bf16[1,5,128,128]{3,2,1,0:T(8,128)(2,1)S(1)}, bf16[1,5,128,128]{3,2,1,0:T(8,128)(2,1)S(1)}, u32[]{:S(2)}, u32[]{:S(2)}) %collective-permute-start.2) | collective-permute-done | bytes 163872 | tf_op jit(solution)/shard_map/ppermute | solution.py:319
  122.9 1.5 gather_panels.3
  124.4 0.6 collective-permute-start.3
  125.0 0.7 collective-permute-start.4
  125.7 2.3 %collective-permute-start.5 = (bf16[1,5,128,128]{3,2,1,0:T(8,128)(2,1)S(1)}, bf16[1,5,128,128]{3,2,1,0:T(8,128)(2,1)S(1)}, u32[]{:S(2)}, u32[]{:S(2)}) collective-permute-start(bf16[1,5,128,128]{3,2,1,0:T(8,128)(2,1)S(1)} %get-tuple-element.36), channel_id=1, source_target_pairs={{0,24},{8,16},{16,8},{24,0},{1,25},{9,17},{17,9},{25,1},{2,26},{10... | collective-permute-start | bytes 491528 | tf_op jit(solution)/shard_map/ppermute | solution.py:327
  128.0 1.8 collective-permute-done.3.refs_1_
  129.8 2.3 %collective-permute-done.4.refs_2_ = bf16[1,5,128,128]{3,2,1,0:T(8,128)(2,1)S(1)} collective-permute-done((bf16[1,5,128,128]{3,2,1,0:T(8,128)(2,1)S(1)}, bf16[1,5,128,128]{3,2,1,0:T(8,128)(2,1)S(1)}, u32[]{:S(2)}, u32[]{:S(2)}) %collective-permute-start.4) | collective-permute-done | bytes 163872 | tf_op jit(solution)/shard_map/ppermute | solution.py:327
  132.7 0.8 collective-permute-done.7.refs_1_
  134.0 2.4 %product.6 = s16[4,656,128]{2,1,0:T(8,128)(2,1)S(1)} custom-call(s32[1440]{0:T(1024)S(1)} %get-tuple-element.31.table_ref, bf16[100,5,128,128]{3,2,1,0:T(8,128)(2,1)S(1)} %get-tuple-element.32.values_ref, bf16[1,5,128,128]{3,2,1,0:T(8,128)(2,1)S(1)} %collective-permute-done.6.refs_0_, bf16[1,5,128,128]{3,2,1,0:T(8,128)(2,1)S(1)} %collective-permute-done.7.refs_1_, ...), custom_call_target="tpu_custom_call" | custom-call | flops 419430400 | bytes 3932160 | tf_op jit(solution)/shard_map/product/pallas_call | solution.py:238
  136.8 3.8 %product.11 = (s16[2,656,128]{2,1,0:T(8,128)(2,1)S(1)}, s16[2,656,128]{2,1,0:T(8,128)(2,1)S(1)}, s16[2,656,128]{2,1,0:T(8,128)(2,1)S(1)}, s16[2,656,128]{2,1,0:T(8,128)(2,1)S(1)}) custom-call(s32[1440]{0:T(1024)S(1)} %get-tuple-element.31.table_ref, bf16[100,5,128,128]{3,2,1,0:T(8,128)(2,1)S(1)} %get-tuple-element.32.values_ref, ...), custom_call_target="tpu_custom_call" | custom-call | flops 838860800 | bytes 7864320 | tf_op jit(solution)/shard_map/product/pallas_call | solution.py:238
  140.6 2.2 %collective-permute-start.39 = (s16[2,656,128]{2,1,0:T(8,128)(2,1)S(1)}, s16[2,656,128]{2,1,0:T(8,128)(2,1)S(1)}, u32[]{:S(2)}, u32[]{:S(2)}) collective-permute-start(s16[2,656,128]{2,1,0:T(8,128)(2,1)S(1)} %get-tuple-element.54), channel_id=1, source_target_pairs={{0,8},{8,0},{16,24},{24,16},{1,9},{9,1},{17,25},{25,17},{2,10},{10... | collective-permute-start | bytes 1007624 | tf_op jit(solution)/shard_map/ppermute | solution.py:347
  142.8 0.9 collective-permute-start.40
  143.7 0.6 collective-permute-start.41
  144.4 4.4 %product.9 = (s16[2,656,128]{2,1,0:T(8,128)(2,1)S(1)}, s16[2,656,128]{2,1,0:T(8,128)(2,1)S(1)}, s16[2,656,128]{2,1,0:T(8,128)(2,1)S(1)}, s16[2,656,128]{2,1,0:T(8,128)(2,1)S(1)}) custom-call(s32[1440]{0:T(1024)S(1)} %get-tuple-element.31.table_ref, bf16[100,5,128,128]{3,2,1,0:T(8,128)(2,1)S(1)} %get-tuple-element.32.values_ref, ...), custom_call_target="tpu_custom_call" | custom-call | flops 838860800 | bytes 7864320 | tf_op jit(solution)/shard_map/product/pallas_call | solution.py:238
  148.8 2.5 %collective-permute-start.25 = (s16[2,656,128]{2,1,0:T(8,128)(2,1)S(1)}, s16[2,656,128]{2,1,0:T(8,128)(2,1)S(1)}, u32[]{:S(2)}, u32[]{:S(2)}) collective-permute-start(s16[2,656,128]{2,1,0:T(8,128)(2,1)S(1)} %get-tuple-element.46), channel_id=1, source_target_pairs={{0,8},{8,0},{16,24},{24,16},{1,9},{9,1},{17,25},{25,17},{2,10},{10... | collective-permute-start | bytes 1007624 | tf_op jit(solution)/shard_map/ppermute | solution.py:347
  151.3 0.6 collective-permute-start.26
  151.9 2.0 %collective-permute-start.27 = (s16[2,656,128]{2,1,0:T(8,128)(2,1)S(1)}, s16[2,656,128]{2,1,0:T(8,128)(2,1)S(1)}, u32[]{:S(2)}, u32[]{:S(2)}) collective-permute-start(s16[2,656,128]{2,1,0:T(8,128)(2,1)S(1)} %get-tuple-element.48), channel_id=1, source_target_pairs={{0,24},{8,16},{16,8},{24,0},{1,25},{9,17},{17,9},{25,1},{2,26},{10... | collective-permute-start | bytes 1007624 | tf_op jit(solution)/shard_map/ppermute | solution.py:347
  153.9 2.5 %product.7 = (s16[1,656,128]{2,1,0:T(8,128)(2,1)S(1)}, s16[1,656,128]{2,1,0:T(8,128)(2,1)S(1)}, s16[1,656,128]{2,1,0:T(8,128)(2,1)S(1)}, s16[1,656,128]{2,1,0:T(8,128)(2,1)S(1)}) custom-call(s32[1440]{0:T(1024)S(1)} %get-tuple-element.31.table_ref, bf16[100,5,128,128]{3,2,1,0:T(8,128)(2,1)S(1)} %get-tuple-element.32.values_ref, ...), custom_call_target="tpu_custom_call" | custom-call | flops 419430400 | bytes 3932160 | tf_op jit(solution)/shard_map/product/pallas_call | solution.py:238
  156.4 4.4 %collective-permute-done.40.refs_2_ = s16[2,656,128]{2,1,0:T(8,128)(2,1)S(1)} collective-permute-done((s16[2,656,128]{2,1,0:T(8,128)(2,1)S(1)}, s16[2,656,128]{2,1,0:T(8,128)(2,1)S(1)}, u32[]{:S(2)}, u32[]{:S(2)}) %collective-permute-start.40) | collective-permute-done | bytes 335904 | tf_op jit(solution)/shard_map/ppermute | solution.py:347
  160.9 5.0 %collective-permute-done.25.refs_1_ = s16[2,656,128]{2,1,0:T(8,128)(2,1)S(1)} collective-permute-done((s16[2,656,128]{2,1,0:T(8,128)(2,1)S(1)}, s16[2,656,128]{2,1,0:T(8,128)(2,1)S(1)}, u32[]{:S(2)}, u32[]{:S(2)}) %collective-permute-start.25) | collective-permute-done | bytes 335904 | tf_op jit(solution)/shard_map/ppermute | solution.py:347
  165.9 2.4 %collective-permute-start.13 = (s16[1,656,128]{2,1,0:T(8,128)(2,1)S(1)}, s16[1,656,128]{2,1,0:T(8,128)(2,1)S(1)}, u32[]{:S(2)}, u32[]{:S(2)}) collective-permute-start(s16[1,656,128]{2,1,0:T(8,128)(2,1)S(1)} %get-tuple-element.40), channel_id=1, source_target_pairs={{0,24},{8,16},{16,8},{24,0},{1,25},{9,17},{17,9},{25,1},{2,26},{10... | collective-permute-start | bytes 503816 | tf_op jit(solution)/shard_map/ppermute | solution.py:347
  168.4 1.7 finish.3.refs_4_
  170.1 5.1 %collective-permute-done.26.refs_2_ = s16[2,656,128]{2,1,0:T(8,128)(2,1)S(1)} collective-permute-done((s16[2,656,128]{2,1,0:T(8,128)(2,1)S(1)}, s16[2,656,128]{2,1,0:T(8,128)(2,1)S(1)}, u32[]{:S(2)}, u32[]{:S(2)}) %collective-permute-start.26) | collective-permute-done | bytes 335904 | tf_op jit(solution)/shard_map/ppermute | solution.py:347
  175.2 1.7 finish.4.refs_4_
  176.9 4.9 %collective-permute-done.12.refs_2_ = s16[1,656,128]{2,1,0:T(8,128)(2,1)S(1)} collective-permute-done((s16[1,656,128]{2,1,0:T(8,128)(2,1)S(1)}, s16[1,656,128]{2,1,0:T(8,128)(2,1)S(1)}, u32[]{:S(2)}, u32[]{:S(2)}) %collective-permute-start.12) | collective-permute-done | bytes 167968 | tf_op jit(solution)/shard_map/ppermute | solution.py:347
  181.8 1.4 finish.5
  (60 shorter events, 4.6 us)
Async XLA Ops:
  1.1 74.5 %copy-start.7 = (s32[100,5]{0,1:T(8,128)S(1)}, s32[100,5]{0,1:T(8,128)}, u32[]{:S(2)}) copy-start(s32[100,5]{0,1:T(8,128)} %param.4) | copy-start | bytes 6004
  1.1 12.7 %collective-permute-start.28 = (bf16[2,5,128,128]{3,2,1,0:T(8,128)(2,1)S(1)}, bf16[2,5,128,128]{3,2,1,0:T(8,128)(2,1)S(1)}, u32[]{:S(2)}, u32[]{:S(2)}) collective-permute-start(bf16[2,5,128,128]{3,2,1,0:T(8,128)(2,1)S(1)} %get-tuple-element.57.refs_0_.own_ref), channel_id=1, source_target_pairs={{0,2},{2,6},{6,4},{4,0},{1,3},{3,7},{7,5},{5,1},{8,10},{10,14},{14... | collective-permute-start | bytes 983048 | tf_op jit(solution)/shard_map/ppermute | solution.py:319
  4.2 16.6 %collective-permute-start.14 = (bf16[2,5,128,128]{3,2,1,0:T(8,128)(2,1)S(1)}, bf16[2,5,128,128]{3,2,1,0:T(8,128)(2,1)S(1)}, u32[]{:S(2)}, u32[]{:S(2)}) collective-permute-start(bf16[2,5,128,128]{3,2,1,0:T(8,128)(2,1)S(1)} %get-tuple-element.58.refs_0_.own_ref), channel_id=1, source_target_pairs={{0,2},{2,6},{6,4},{4,0},{1,3},{3,7},{7,5},{5,1},{8,10},{10,14},{14... | collective-permute-start | bytes 983048 | tf_op jit(solution)/shard_map/ppermute | solution.py:319
  13.8 14.0 %collective-permute-start.29 = (bf16[2,5,128,128]{3,2,1,0:T(8,128)(2,1)S(1)}, bf16[2,5,128,128]{3,2,1,0:T(8,128)(2,1)S(1)}, u32[]{:S(2)}, u32[]{:S(2)}) collective-permute-start(bf16[2,5,128,128]{3,2,1,0:T(8,128)(2,1)S(1)} %collective-permute-done.28.refs_1_), channel_id=1, source_target_pairs={{0,2},{2,6},{6,4},{4,0},{1,3},{3,7},{7,5},{5,1},{8,10},{10,14},{14... | collective-permute-start | bytes 983048 | tf_op jit(solution)/shard_map/ppermute | solution.py:319
  20.8 14.0 %collective-permute-start.15 = (bf16[2,5,128,128]{3,2,1,0:T(8,128)(2,1)S(1)}, bf16[2,5,128,128]{3,2,1,0:T(8,128)(2,1)S(1)}, u32[]{:S(2)}, u32[]{:S(2)}) collective-permute-start(bf16[2,5,128,128]{3,2,1,0:T(8,128)(2,1)S(1)} %collective-permute-done.14.refs_1_), channel_id=1, source_target_pairs={{0,2},{2,6},{6,4},{4,0},{1,3},{3,7},{7,5},{5,1},{8,10},{10,14},{14... | collective-permute-start | bytes 983048 | tf_op jit(solution)/shard_map/ppermute | solution.py:319
  27.9 14.0 %collective-permute-start.30 = (bf16[2,5,128,128]{3,2,1,0:T(8,128)(2,1)S(1)}, bf16[2,5,128,128]{3,2,1,0:T(8,128)(2,1)S(1)}, u32[]{:S(2)}, u32[]{:S(2)}) collective-permute-start(bf16[2,5,128,128]{3,2,1,0:T(8,128)(2,1)S(1)} %collective-permute-done.29.refs_2_), channel_id=1, source_target_pairs={{0,2},{2,6},{6,4},{4,0},{1,3},{3,7},{7,5},{5,1},{8,10},{10,14},{14... | collective-permute-start | bytes 983048 | tf_op jit(solution)/shard_map/ppermute | solution.py:319
  34.9 13.2 %collective-permute-start.16 = (bf16[2,5,128,128]{3,2,1,0:T(8,128)(2,1)S(1)}, bf16[2,5,128,128]{3,2,1,0:T(8,128)(2,1)S(1)}, u32[]{:S(2)}, u32[]{:S(2)}) collective-permute-start(bf16[2,5,128,128]{3,2,1,0:T(8,128)(2,1)S(1)} %collective-permute-done.15.refs_2_), channel_id=1, source_target_pairs={{0,2},{2,6},{6,4},{4,0},{1,3},{3,7},{7,5},{5,1},{8,10},{10,14},{14... | collective-permute-start | bytes 983048 | tf_op jit(solution)/shard_map/ppermute | solution.py:319
  43.0 10.6 %collective-permute-start.31 = (bf16[2,5,128,128]{3,2,1,0:T(8,128)(2,1)S(1)}, bf16[2,5,128,128]{3,2,1,0:T(8,128)(2,1)S(1)}, u32[]{:S(2)}, u32[]{:S(2)}) collective-permute-start(bf16[2,5,128,128]{3,2,1,0:T(8,128)(2,1)S(1)} %get-tuple-element.50), channel_id=1, source_target_pairs={{0,8},{8,0},{16,24},{24,16},{1,9},{9,1},{17,25},{25,17},{2,10},{10... | collective-permute-start | bytes 983048 | tf_op jit(solution)/shard_map/ppermute | solution.py:327
  44.9 14.5 %collective-permute-start.32 = (bf16[2,5,128,128]{3,2,1,0:T(8,128)(2,1)S(1)}, bf16[2,5,128,128]{3,2,1,0:T(8,128)(2,1)S(1)}, u32[]{:S(2)}, u32[]{:S(2)}) collective-permute-start(bf16[2,5,128,128]{3,2,1,0:T(8,128)(2,1)S(1)} %get-tuple-element.51), channel_id=1, source_target_pairs={{0,16},{8,24},{16,0},{24,8},{1,17},{9,25},{17,1},{25,9},{2,18},{10... | collective-permute-start | bytes 983048 | tf_op jit(solution)/shard_map/ppermute | solution.py:327
  46.4 15.6 %collective-permute-start.33 = (bf16[2,5,128,128]{3,2,1,0:T(8,128)(2,1)S(1)}, bf16[2,5,128,128]{3,2,1,0:T(8,128)(2,1)S(1)}, u32[]{:S(2)}, u32[]{:S(2)}) collective-permute-start(bf16[2,5,128,128]{3,2,1,0:T(8,128)(2,1)S(1)} %get-tuple-element.52), channel_id=1, source_target_pairs={{0,24},{8,16},{16,8},{24,0},{1,25},{9,17},{17,9},{25,1},{2,26},{10... | collective-permute-start | bytes 983048 | tf_op jit(solution)/shard_map/ppermute | solution.py:327
  46.6 15.4 %collective-permute-start.34 = (bf16[2,5,128,128]{3,2,1,0:T(8,128)(2,1)S(1)}, bf16[2,5,128,128]{3,2,1,0:T(8,128)(2,1)S(1)}, u32[]{:S(2)}, u32[]{:S(2)}) collective-permute-start(bf16[2,5,128,128]{3,2,1,0:T(8,128)(2,1)S(1)} %get-tuple-element.49.refs_0_), channel_id=1, source_target_pairs={{1,0},{0,1},{3,2},{2,3},{5,4},{4,5},{7,6},{6,7},{9,8},{8,9},{11,10... | collective-permute-start | bytes 983048 | tf_op jit(solution)/shard_map/ppermute | solution.py:338
  49.2 18.6 %collective-permute-start.17 = (bf16[2,5,128,128]{3,2,1,0:T(8,128)(2,1)S(1)}, bf16[2,5,128,128]{3,2,1,0:T(8,128)(2,1)S(1)}, u32[]{:S(2)}, u32[]{:S(2)}) collective-permute-start(bf16[2,5,128,128]{3,2,1,0:T(8,128)(2,1)S(1)} %get-tuple-element.42), channel_id=1, source_target_pairs={{0,8},{8,0},{16,24},{24,16},{1,9},{9,1},{17,25},{25,17},{2,10},{10... | collective-permute-start | bytes 983048 | tf_op jit(solution)/shard_map/ppermute | solution.py:327
  53.7 19.5 %collective-permute-start.18 = (bf16[2,5,128,128]{3,2,1,0:T(8,128)(2,1)S(1)}, bf16[2,5,128,128]{3,2,1,0:T(8,128)(2,1)S(1)}, u32[]{:S(2)}, u32[]{:S(2)}) collective-permute-start(bf16[2,5,128,128]{3,2,1,0:T(8,128)(2,1)S(1)} %get-tuple-element.43), channel_id=1, source_target_pairs={{0,16},{8,24},{16,0},{24,8},{1,17},{9,25},{17,1},{25,9},{2,18},{10... | collective-permute-start | bytes 983048 | tf_op jit(solution)/shard_map/ppermute | solution.py:327
  59.4 13.8 %collective-permute-start.19 = (bf16[2,5,128,128]{3,2,1,0:T(8,128)(2,1)S(1)}, bf16[2,5,128,128]{3,2,1,0:T(8,128)(2,1)S(1)}, u32[]{:S(2)}, u32[]{:S(2)}) collective-permute-start(bf16[2,5,128,128]{3,2,1,0:T(8,128)(2,1)S(1)} %get-tuple-element.44), channel_id=1, source_target_pairs={{0,24},{8,16},{16,8},{24,0},{1,25},{9,17},{17,9},{25,1},{2,26},{10... | collective-permute-start | bytes 983048 | tf_op jit(solution)/shard_map/ppermute | solution.py:327
  62.0 11.7 %collective-permute-start.35 = (bf16[2,5,128,128]{3,2,1,0:T(8,128)(2,1)S(1)}, bf16[2,5,128,128]{3,2,1,0:T(8,128)(2,1)S(1)}, u32[]{:S(2)}, u32[]{:S(2)}) collective-permute-start(bf16[2,5,128,128]{3,2,1,0:T(8,128)(2,1)S(1)} %collective-permute-done.31.refs_1_), channel_id=1, source_target_pairs={{1,0},{0,1},{3,2},{2,3},{5,4},{4,5},{7,6},{6,7},{9,8},{8,9},{11,10... | collective-permute-start | bytes 983048 | tf_op jit(solution)/shard_map/ppermute | solution.py:338
  62.0 0.7 copy-start
  62.7 11.7 %collective-permute-start.36 = (bf16[2,5,128,128]{3,2,1,0:T(8,128)(2,1)S(1)}, bf16[2,5,128,128]{3,2,1,0:T(8,128)(2,1)S(1)}, u32[]{:S(2)}, u32[]{:S(2)}) collective-permute-start(bf16[2,5,128,128]{3,2,1,0:T(8,128)(2,1)S(1)} %collective-permute-done.32.refs_2_), channel_id=1, source_target_pairs={{1,0},{0,1},{3,2},{2,3},{5,4},{4,5},{7,6},{6,7},{9,8},{8,9},{11,10... | collective-permute-start | bytes 983048 | tf_op jit(solution)/shard_map/ppermute | solution.py:338
  67.8 29.2 %collective-permute-start.37 = (bf16[2,5,128,128]{3,2,1,0:T(8,128)(2,1)S(1)}, bf16[2,5,128,128]{3,2,1,0:T(8,128)(2,1)}, u32[]{:S(2)}, u32[]{:S(2)}) collective-permute-start(bf16[2,5,128,128]{3,2,1,0:T(8,128)(2,1)S(1)} %collective-permute-done.33.refs_3_), channel_id=1, source_target_pairs={{1,0},{0,1},{3,2},{2,3},{5,4},{4,5},{7,6},{6,7},{9,8},{8,9},{11,10... | collective-permute-start | bytes 983048 | tf_op jit(solution)/shard_map/ppermute | solution.py:338
  73.2 30.2 %collective-permute-start.20 = (bf16[2,5,128,128]{3,2,1,0:T(8,128)(2,1)S(1)}, bf16[2,5,128,128]{3,2,1,0:T(8,128)(2,1)}, u32[]{:S(2)}, u32[]{:S(2)}) collective-permute-start(bf16[2,5,128,128]{3,2,1,0:T(8,128)(2,1)S(1)} %get-tuple-element.41.refs_0_), channel_id=1, source_target_pairs={{1,0},{0,1},{3,2},{2,3},{5,4},{4,5},{7,6},{6,7},{9,8},{8,9},{11,10... | collective-permute-start | bytes 983048 | tf_op jit(solution)/shard_map/ppermute | solution.py:338
  73.2 30.5 %collective-permute-start.21 = (bf16[2,5,128,128]{3,2,1,0:T(8,128)(2,1)S(1)}, bf16[2,5,128,128]{3,2,1,0:T(8,128)(2,1)}, u32[]{:S(2)}, u32[]{:S(2)}) collective-permute-start(bf16[2,5,128,128]{3,2,1,0:T(8,128)(2,1)S(1)} %collective-permute-done.17.refs_1_), channel_id=1, source_target_pairs={{1,0},{0,1},{3,2},{2,3},{5,4},{4,5},{7,6},{6,7},{9,8},{8,9},{11,10... | collective-permute-start | bytes 983048 | tf_op jit(solution)/shard_map/ppermute | solution.py:338
  73.7 0.7 copy-start.2
  74.4 29.3 %collective-permute-start.22 = (bf16[2,5,128,128]{3,2,1,0:T(8,128)(2,1)S(1)}, bf16[2,5,128,128]{3,2,1,0:T(8,128)(2,1)}, u32[]{:S(2)}, u32[]{:S(2)}) collective-permute-start(bf16[2,5,128,128]{3,2,1,0:T(8,128)(2,1)S(1)} %collective-permute-done.18.refs_2_), channel_id=1, source_target_pairs={{1,0},{0,1},{3,2},{2,3},{5,4},{4,5},{7,6},{6,7},{9,8},{8,9},{11,10... | collective-permute-start | bytes 983048 | tf_op jit(solution)/shard_map/ppermute | solution.py:338
  74.4 0.7 copy-start.4
  75.2 28.6 %collective-permute-start.23 = (bf16[2,5,128,128]{3,2,1,0:T(8,128)(2,1)S(1)}, bf16[2,5,128,128]{3,2,1,0:T(8,128)(2,1)}, u32[]{:S(2)}, u32[]{:S(2)}) collective-permute-start(bf16[2,5,128,128]{3,2,1,0:T(8,128)(2,1)S(1)} %collective-permute-done.19.refs_3_), channel_id=1, source_target_pairs={{1,0},{0,1},{3,2},{2,3},{5,4},{4,5},{7,6},{6,7},{9,8},{8,9},{11,10... | collective-permute-start | bytes 983048 | tf_op jit(solution)/shard_map/ppermute | solution.py:338
  76.5 13.1 %all-to-all-start = ((s32[32,5,5]{2,1,0:T(8,128)}), s32[32,5,5]{2,1,0:T(8,128)S(1)}, u32[]{:S(2)}, u32[]{:S(2)}) async-start(s32[32,5,5]{2,1,0:T(8,128)} %broadcast_in_dim.2), calls=%async_computation | async-start | bytes 262144 | tf_op jit(solution)/shard_map/all_to_all | solution.py:307
  89.8 7.1 %copy-start.1 = (bf16[2,5,128,128]{3,2,1,0:T(8,128)(2,1)S(1)}, bf16[2,5,128,128]{3,2,1,0:T(8,128)(2,1)}, u32[]{:S(2)}) copy-start(bf16[2,5,128,128]{3,2,1,0:T(8,128)(2,1)} %copy-done) | copy-start | bytes 983044
  89.8 7.1 %copy-start.3 = (bf16[2,5,128,128]{3,2,1,0:T(8,128)(2,1)S(1)}, bf16[2,5,128,128]{3,2,1,0:T(8,128)(2,1)}, u32[]{:S(2)}) copy-start(bf16[2,5,128,128]{3,2,1,0:T(8,128)(2,1)} %copy-done.2) | copy-start | bytes 983044
  89.8 7.1 %copy-start.5 = (bf16[2,5,128,128]{3,2,1,0:T(8,128)(2,1)S(1)}, bf16[2,5,128,128]{3,2,1,0:T(8,128)(2,1)}, u32[]{:S(2)}) copy-start(bf16[2,5,128,128]{3,2,1,0:T(8,128)(2,1)} %copy-done.4) | copy-start | bytes 983044
  101.0 35.8 %collective-permute-start.38 = (s16[8,656,128]{2,1,0:T(8,128)(2,1)S(1)}, s16[8,656,128]{2,1,0:T(8,128)(2,1)S(1)}, u32[]{:S(2)}, u32[]{:S(2)}) collective-permute-start(s16[8,656,128]{2,1,0:T(8,128)(2,1)S(1)} %product.10), channel_id=1, source_target_pairs={{0,1},{1,0},{2,3},{3,2},{4,5},{5,4},{6,7},{7,6},{8,9},{9,8},{10,11... | collective-permute-start | bytes 4030472 | tf_op jit(solution)/shard_map/ppermute | solution.py:341
  103.4 7.1 %collective-permute-start = (bf16[1,5,128,128]{3,2,1,0:T(8,128)(2,1)S(1)}, bf16[1,5,128,128]{3,2,1,0:T(8,128)(2,1)S(1)}, u32[]{:S(2)}, u32[]{:S(2)}) collective-permute-start(bf16[1,5,128,128]{3,2,1,0:T(8,128)(2,1)S(1)} %slice.13.refs_0_.own_ref), channel_id=1, source_target_pairs={{0,2},{2,6},{6,4},{4,0},{1,3},{3,7},{7,5},{5,1},{8,10},{10,14},{14... | collective-permute-start | bytes 491528 | tf_op jit(solution)/shard_map/ppermute | solution.py:319
  108.4 36.0 %collective-permute-start.24 = (s16[8,656,128]{2,1,0:T(8,128)(2,1)S(1)}, s16[8,656,128]{2,1,0:T(8,128)(2,1)S(1)}, u32[]{:S(2)}, u32[]{:S(2)}) collective-permute-start(s16[8,656,128]{2,1,0:T(8,128)(2,1)S(1)} %product.8), channel_id=1, source_target_pairs={{0,1},{1,0},{2,3},{3,2},{4,5},{5,4},{6,7},{7,6},{8,9},{9,8},{10,11... | collective-permute-start | bytes 4030472 | tf_op jit(solution)/shard_map/ppermute | solution.py:341
  110.4 6.2 %collective-permute-start.1 = (bf16[1,5,128,128]{3,2,1,0:T(8,128)(2,1)S(1)}, bf16[1,5,128,128]{3,2,1,0:T(8,128)(2,1)S(1)}, u32[]{:S(2)}, u32[]{:S(2)}) collective-permute-start(bf16[1,5,128,128]{3,2,1,0:T(8,128)(2,1)S(1)} %collective-permute-done.refs_1_), channel_id=1, source_target_pairs={{0,2},{2,6},{6,4},{4,0},{1,3},{3,7},{7,5},{5,1},{8,10},{10,14},{14... | collective-permute-start | bytes 491528 | tf_op jit(solution)/shard_map/ppermute | solution.py:319
  116.7 6.2 %collective-permute-start.2 = (bf16[1,5,128,128]{3,2,1,0:T(8,128)(2,1)S(1)}, bf16[1,5,128,128]{3,2,1,0:T(8,128)(2,1)S(1)}, u32[]{:S(2)}, u32[]{:S(2)}) collective-permute-start(bf16[1,5,128,128]{3,2,1,0:T(8,128)(2,1)S(1)} %collective-permute-done.1.refs_2_), channel_id=1, source_target_pairs={{0,2},{2,6},{6,4},{4,0},{1,3},{3,7},{7,5},{5,1},{8,10},{10,14},{14... | collective-permute-start | bytes 491528 | tf_op jit(solution)/shard_map/ppermute | solution.py:319
  124.4 5.4 %collective-permute-start.3 = (bf16[1,5,128,128]{3,2,1,0:T(8,128)(2,1)S(1)}, bf16[1,5,128,128]{3,2,1,0:T(8,128)(2,1)S(1)}, u32[]{:S(2)}, u32[]{:S(2)}) collective-permute-start(bf16[1,5,128,128]{3,2,1,0:T(8,128)(2,1)S(1)} %get-tuple-element.34), channel_id=1, source_target_pairs={{0,8},{8,0},{16,24},{24,16},{1,9},{9,1},{17,25},{25,17},{2,10},{10... | collective-permute-start | bytes 491528 | tf_op jit(solution)/shard_map/ppermute | solution.py:327
  125.0 7.1 %collective-permute-start.4 = (bf16[1,5,128,128]{3,2,1,0:T(8,128)(2,1)S(1)}, bf16[1,5,128,128]{3,2,1,0:T(8,128)(2,1)S(1)}, u32[]{:S(2)}, u32[]{:S(2)}) collective-permute-start(bf16[1,5,128,128]{3,2,1,0:T(8,128)(2,1)S(1)} %get-tuple-element.35), channel_id=1, source_target_pairs={{0,16},{8,24},{16,0},{24,8},{1,17},{9,25},{17,1},{25,9},{2,18},{10... | collective-permute-start | bytes 491528 | tf_op jit(solution)/shard_map/ppermute | solution.py:327
  125.7 6.4 %collective-permute-start.5 = (bf16[1,5,128,128]{3,2,1,0:T(8,128)(2,1)S(1)}, bf16[1,5,128,128]{3,2,1,0:T(8,128)(2,1)S(1)}, u32[]{:S(2)}, u32[]{:S(2)}) collective-permute-start(bf16[1,5,128,128]{3,2,1,0:T(8,128)(2,1)S(1)} %get-tuple-element.36), channel_id=1, source_target_pairs={{0,24},{8,16},{16,8},{24,0},{1,25},{9,17},{17,9},{25,1},{2,26},{10... | collective-permute-start | bytes 491528 | tf_op jit(solution)/shard_map/ppermute | solution.py:327
  129.8 2.8 %collective-permute-start.6 = (bf16[1,5,128,128]{3,2,1,0:T(8,128)(2,1)S(1)}, bf16[1,5,128,128]{3,2,1,0:T(8,128)(2,1)S(1)}, u32[]{:S(2)}, u32[]{:S(2)}) collective-permute-start(bf16[1,5,128,128]{3,2,1,0:T(8,128)(2,1)S(1)} %get-tuple-element.33.refs_0_), channel_id=1, source_target_pairs={{1,0},{0,1},{3,2},{2,3},{5,4},{4,5},{7,6},{6,7},{9,8},{8,9},{11,10... | collective-permute-start | bytes 491528 | tf_op jit(solution)/shard_map/ppermute | solution.py:338
  132.1 1.4 collective-permute-start.7
  132.1 1.6 collective-permute-start.8
  132.6 1.4 collective-permute-start.9
  136.4 14.8 %collective-permute-start.10 = (s16[4,656,128]{2,1,0:T(8,128)(2,1)S(1)}, s16[4,656,128]{2,1,0:T(8,128)(2,1)S(1)}, u32[]{:S(2)}, u32[]{:S(2)}) collective-permute-start(s16[4,656,128]{2,1,0:T(8,128)(2,1)S(1)} %product.6), channel_id=1, source_target_pairs={{0,1},{1,0},{2,3},{3,2},{4,5},{5,4},{6,7},{7,6},{8,9},{9,8},{10,11... | collective-permute-start | bytes 2015240 | tf_op jit(solution)/shard_map/ppermute | solution.py:341
  140.6 11.3 %collective-permute-start.39 = (s16[2,656,128]{2,1,0:T(8,128)(2,1)S(1)}, s16[2,656,128]{2,1,0:T(8,128)(2,1)S(1)}, u32[]{:S(2)}, u32[]{:S(2)}) collective-permute-start(s16[2,656,128]{2,1,0:T(8,128)(2,1)S(1)} %get-tuple-element.54), channel_id=1, source_target_pairs={{0,8},{8,0},{16,24},{24,16},{1,9},{9,1},{17,25},{25,17},{2,10},{10... | collective-permute-start | bytes 1007624 | tf_op jit(solution)/shard_map/ppermute | solution.py:347
  142.8 18.0 %collective-permute-start.40 = (s16[2,656,128]{2,1,0:T(8,128)(2,1)S(1)}, s16[2,656,128]{2,1,0:T(8,128)(2,1)S(1)}, u32[]{:S(2)}, u32[]{:S(2)}) collective-permute-start(s16[2,656,128]{2,1,0:T(8,128)(2,1)S(1)} %get-tuple-element.55), channel_id=1, source_target_pairs={{0,16},{8,24},{16,0},{24,8},{1,17},{9,25},{17,1},{25,9},{2,18},{10... | collective-permute-start | bytes 1007624 | tf_op jit(solution)/shard_map/ppermute | solution.py:347
  143.7 17.1 %collective-permute-start.41 = (s16[2,656,128]{2,1,0:T(8,128)(2,1)S(1)}, s16[2,656,128]{2,1,0:T(8,128)(2,1)S(1)}, u32[]{:S(2)}, u32[]{:S(2)}) collective-permute-start(s16[2,656,128]{2,1,0:T(8,128)(2,1)S(1)} %get-tuple-element.56), channel_id=1, source_target_pairs={{0,24},{8,16},{16,8},{24,0},{1,25},{9,17},{17,9},{25,1},{2,26},{10... | collective-permute-start | bytes 1007624 | tf_op jit(solution)/shard_map/ppermute | solution.py:347
  148.8 17.2 %collective-permute-start.25 = (s16[2,656,128]{2,1,0:T(8,128)(2,1)S(1)}, s16[2,656,128]{2,1,0:T(8,128)(2,1)S(1)}, u32[]{:S(2)}, u32[]{:S(2)}) collective-permute-start(s16[2,656,128]{2,1,0:T(8,128)(2,1)S(1)} %get-tuple-element.46), channel_id=1, source_target_pairs={{0,8},{8,0},{16,24},{24,16},{1,9},{9,1},{17,25},{25,17},{2,10},{10... | collective-permute-start | bytes 1007624 | tf_op jit(solution)/shard_map/ppermute | solution.py:347
  151.3 23.9 %collective-permute-start.26 = (s16[2,656,128]{2,1,0:T(8,128)(2,1)S(1)}, s16[2,656,128]{2,1,0:T(8,128)(2,1)S(1)}, u32[]{:S(2)}, u32[]{:S(2)}) collective-permute-start(s16[2,656,128]{2,1,0:T(8,128)(2,1)S(1)} %get-tuple-element.47), channel_id=1, source_target_pairs={{0,16},{8,24},{16,0},{24,8},{1,17},{9,25},{17,1},{25,9},{2,18},{10... | collective-permute-start | bytes 1007624 | tf_op jit(solution)/shard_map/ppermute | solution.py:347
  151.9 16.5 %copy-start.6 = (s32[40]{0:T(128)S(1)}, s32[40]{0:T(128)}, u32[]{:S(2)}) copy-start(s32[40]{0:T(128)} %flag_ref.5) | copy-start | bytes 484
  151.9 23.3 %collective-permute-start.27 = (s16[2,656,128]{2,1,0:T(8,128)(2,1)S(1)}, s16[2,656,128]{2,1,0:T(8,128)(2,1)S(1)}, u32[]{:S(2)}, u32[]{:S(2)}) collective-permute-start(s16[2,656,128]{2,1,0:T(8,128)(2,1)S(1)} %get-tuple-element.48), channel_id=1, source_target_pairs={{0,24},{8,16},{16,8},{24,0},{1,25},{9,17},{17,9},{25,1},{2,26},{10... | collective-permute-start | bytes 1007624 | tf_op jit(solution)/shard_map/ppermute | solution.py:347
  160.8 16.1 %collective-permute-start.11 = (s16[1,656,128]{2,1,0:T(8,128)(2,1)S(1)}, s16[1,656,128]{2,1,0:T(8,128)(2,1)S(1)}, u32[]{:S(2)}, u32[]{:S(2)}) collective-permute-start(s16[1,656,128]{2,1,0:T(8,128)(2,1)S(1)} %get-tuple-element.38), channel_id=1, source_target_pairs={{0,8},{8,0},{16,24},{24,16},{1,9},{9,1},{17,25},{25,17},{2,10},{10... | collective-permute-start | bytes 503816 | tf_op jit(solution)/shard_map/ppermute | solution.py:347
  160.8 20.9 %collective-permute-start.12 = (s16[1,656,128]{2,1,0:T(8,128)(2,1)S(1)}, s16[1,656,128]{2,1,0:T(8,128)(2,1)S(1)}, u32[]{:S(2)}, u32[]{:S(2)}) collective-permute-start(s16[1,656,128]{2,1,0:T(8,128)(2,1)S(1)} %get-tuple-element.39), channel_id=1, source_target_pairs={{0,16},{8,24},{16,0},{24,8},{1,17},{9,25},{17,1},{25,9},{2,18},{10... | collective-permute-start | bytes 503816 | tf_op jit(solution)/shard_map/ppermute | solution.py:347
  165.9 15.8 %collective-permute-start.13 = (s16[1,656,128]{2,1,0:T(8,128)(2,1)S(1)}, s16[1,656,128]{2,1,0:T(8,128)(2,1)S(1)}, u32[]{:S(2)}, u32[]{:S(2)}) collective-permute-start(s16[1,656,128]{2,1,0:T(8,128)(2,1)S(1)} %get-tuple-element.40), channel_id=1, source_target_pairs={{0,24},{8,16},{16,8},{24,0},{1,25},{9,17},{17,9},{25,1},{2,26},{10... | collective-permute-start | bytes 503816 | tf_op jit(solution)/shard_map/ppermute | solution.py:347
